TPU v7x, 32 devices: a whole 2x2x4 slice. The times are simulated.
32 devices in a mesh: dp: 8 (over z, x), expert: 4 (over y, core).
Axes of the slice: x: 2, y: 2, z: 4, core: 2. Of those that a mesh axis runs over, the one named last changes fastest.
Arguments:
- layer_input: bfloat16 [2, 32, 96, 1152], P(None, ('dp', 'expert')), may hold values from -6 to 6
- segments: int32 [2, 32, 96], P(None, ('dp', 'expert')), may hold values from 0 to 1, never falling along the last dimension, each value on 1 to 72 neighbouring positions
- routes: int32 [2, 32, 96, 1], P(None, ('dp', 'expert')), may hold values from 0 to 3
- cotangent: bfloat16 [2, 32, 96, 1152], P(None, ('dp', 'expert')), may hold values from -6 to 6
- norm1_gain: bfloat16 [1152], replicated, may hold values from 0.5 to 1.5
- in_weight: bfloat16 [4608, 1152], P('dp'), may hold values from -0.1875 to 0.1875
- conv_weight: bfloat16 [4, 2304], P(None, ('dp', 'expert')), may hold values from -0.5 to 0.5
- conv_bias: bfloat16 [2304], P(('dp', 'expert')), may hold values from -0.5 to 0.5
- xproj_weight: bfloat16 [2304, 104], P(('dp', 'expert')), may hold values from -0.5 to 0.5
- dtproj_weight: bfloat16 [72, 2304], P(None, ('dp', 'expert')), may hold values from -0.75 to 0.75
- dt_bias: bfloat16 [2304], P(('dp', 'expert')), may hold values from -5 to -1.5
- a_log: bfloat16 [16, 2304], P(None, ('dp', 'expert')), may hold values from 0 to 2.765625
- skip_gain: bfloat16 [2304], P(('dp', 'expert')), may hold values from 0.5 to 1.5
- out_weight: bfloat16 [2304, 1152], P('dp'), may hold values from -0.375 to 0.375
- norm2_gain: bfloat16 [1152], replicated, may hold values from 0.5 to 1.5
- router_weight: bfloat16 [1152, 4], replicated, may hold values from -0.125 to 0.125
- up_weight: bfloat16 [4, 3072, 1152], P('expert', 'dp'), may hold values from -0.1875 to 0.1875
- down_weight: bfloat16 [4, 3072, 1152], P('expert', 'dp'), may hold values from -0.875 to 0.875
Outputs:
- layer_output: bfloat16 [2, 32, 96, 1152], P(None, ('dp', 'expert'))
- input_grad: float32 [2, 32, 96, 1152], P(None, ('dp', 'expert'))
- norm1_gain_grad: float32 [1152], replicated
- in_weight_grad: float32 [4608, 1152], P('dp')
- conv_weight_grad: float32 [4, 2304], P(None, ('dp', 'expert'))
- conv_bias_grad: float32 [2304], P(('dp', 'expert'))
- xproj_weight_grad: float32 [2304, 104], P(('dp', 'expert'))
- dtproj_weight_grad: float32 [72, 2304], P(None, ('dp', 'expert'))
- dt_bias_grad: float32 [2304], P(('dp', 'expert'))
- a_log_grad: float32 [16, 2304], P(None, ('dp', 'expert'))
- skip_gain_grad: float32 [2304], P(('dp', 'expert'))
- out_weight_grad: float32 [2304, 1152], P('dp')
- norm2_gain_grad: float32 [1152], replicated
- router_weight_grad: float32 [1152, 4], replicated
- up_weight_grad: float32 [4, 3072, 1152], P('expert', 'dp')
- down_weight_grad: float32 [4, 3072, 1152], P('expert', 'dp')
Inputs may be any that keep to these rules, and one draw needn't show every extreme that they name: `segments`: segment numbers of a sequence start at 0 and never fall; a document has at most 72 positions.
All inputs are finite; a program needn't handle non-finite values.
Results may differ from a plain program's by a relative error of at most 0.02.
Values may be sent and summed in bfloat16 or wider, within the bound.
No kernel may reach another device: no remote copies, remote signals or barrier semaphores. Data moves between devices by JAX's collectives and lax.ppermute only.
A program may use at most 192 MiB of HBM per device.

v0:
```python
import jax
import jax.numpy as jnp
from jax import lax
from jax.sharding import PartitionSpec as P

CH = 16


HIGHEST = lax.Precision.HIGHEST
EPSILON = 1e-05


def rms_scale(values, gain_row):
    return (
        values * lax.rsqrt(jnp.mean(values * values, axis=-1, keepdims=True) + EPSILON) * gain_row
    )


def gelu_tanh(values):
    return jax.nn.gelu(values, approximate=True)


def same_doc_shift(segment, offset):
    padded = jnp.concatenate([jnp.full((offset,), -1, segment.dtype), segment])[: segment.shape[0]]
    return (padded == segment).astype(jnp.float32)


def conv_silu(inner_part, conv_taps, bias_row, segment):
    length = inner_part.shape[0]
    tap_count = conv_taps.shape[0]
    summed = jnp.zeros_like(inner_part) + bias_row
    for offset in range(tap_count):
        shifted = jnp.pad(inner_part, ((offset, 0), (0, 0)))[:length]
        summed = (
            summed
            + conv_taps[tap_count - 1 - offset] * shifted * same_doc_shift(segment, offset)[:, None]
        )
    return jax.nn.silu(summed)


def pair_combine(earlier, latter):
    return (earlier[0] * latter[0], latter[0] * earlier[1] + latter[1])


def scan_mix(
    conv_out, dt_part, dt_shift, b_rows, c_rows, log_rates, skip_row, gate_in, keep_row, block_len
):
    delta = jax.nn.softplus(dt_part + dt_shift)
    decay_rate = -jnp.exp(log_rates)
    length = conv_out.shape[0]
    blocks = length // block_len

    def split_blocks(values):
        return values.reshape((blocks, block_len) + values.shape[1:])

    def block_step(state_now, pieces):
        delta_b, conv_b, b_blk, c_blk, keep_b = pieces
        factor = jnp.exp(delta_b[:, None, :] * decay_rate[None]) * keep_b[:, None, None]
        driven = (delta_b * conv_b)[:, None, :] * b_blk[:, :, None]
        cum_factor, local_state = lax.associative_scan(pair_combine, (factor, driven), axis=0)
        states = local_state + cum_factor * state_now[None]
        return (states[-1], jnp.sum(c_blk[:, :, None] * states, axis=1))

    initial = jnp.zeros(decay_rate.shape, jnp.float32)
    final_state, outputs = lax.scan(
        jax.checkpoint(block_step),
        initial,
        (
            split_blocks(delta),
            split_blocks(conv_out),
            split_blocks(b_rows),
            split_blocks(c_rows),
            split_blocks(keep_row),
        ),
    )
    mixed_out = outputs.reshape(length, -1) + skip_row * conv_out
    return mixed_out * jax.nn.silu(gate_in)


def norm_route(residual, gain_two, router_full, chosen_rows):
    normed_two = rms_scale(residual, gain_two)
    logits = jnp.dot(normed_two, router_full, precision=HIGHEST, preferred_element_type=jnp.float32)
    probabilities = jax.nn.softmax(logits, axis=-1)
    return (normed_two, jnp.sum(probabilities * chosen_rows, axis=1))


def dispatch_matrix(route_row, expert_count, capacity):
    chosen = (route_row[:, None] == jnp.arange(expert_count, dtype=jnp.int32)[None]).astype(
        jnp.int32
    )
    earlier = jnp.cumsum(chosen, axis=0) - chosen
    slot_index = jnp.sum(earlier * chosen, axis=1)
    places = (slot_index[:, None] == jnp.arange(capacity, dtype=jnp.int32)[None]).astype(
        jnp.float32
    )
    return (chosen.astype(jnp.float32)[:, :, None] * places[:, None, :]).reshape(
        route_row.shape[0], expert_count * capacity
    )


def add_terms(totals, terms):
    if totals is None:
        return terms
    return jax.tree.map(jnp.add, totals, terms)


def on_device(
    layer_input,
    segments,
    routes,
    cotangent,
    norm1_gain,
    in_weight,
    conv_weight,
    conv_bias,
    xproj_weight,
    dtproj_weight,
    dt_bias,
    a_log,
    skip_gain,
    out_weight,
    norm2_gain,
    router_weight,
    up_weight,
    down_weight,
):
    micro_count = layer_input.shape[0]
    seq_len = layer_input.shape[2]
    model_width = layer_input.shape[3]
    expert_devices = lax.axis_size("expert")
    local_experts = up_weight.shape[0]
    expert_count = expert_devices * local_experts
    capacity = seq_len * 5 // (4 * expert_count)
    gain_one = norm1_gain.astype(jnp.float32)
    gain_two = norm2_gain.astype(jnp.float32)
    router_full = router_weight.astype(jnp.float32)

    def fetch_mixer():
        dense = (
            lax.all_gather(in_weight, "dp", axis=0, tiled=True),
            lax.all_gather(out_weight, "dp", axis=0, tiled=True),
            lax.all_gather(up_weight, "dp", axis=1, tiled=True),
            lax.all_gather(down_weight, "dp", axis=1, tiled=True),
        )
        rest = (
            lax.all_gather(conv_weight, ("dp", "expert"), axis=1, tiled=True),
            lax.all_gather(conv_bias, ("dp", "expert"), axis=0, tiled=True),
            lax.all_gather(xproj_weight, ("dp", "expert"), axis=0, tiled=True),
            lax.all_gather(dtproj_weight, ("dp", "expert"), axis=1, tiled=True),
            lax.all_gather(dt_bias, ("dp", "expert"), axis=0, tiled=True),
            lax.all_gather(a_log, ("dp", "expert"), axis=1, tiled=True),
            lax.all_gather(skip_gain, ("dp", "expert"), axis=0, tiled=True),
        )
        return (dense, rest)

    fetched = None
    dense_totals = None
    mixer_totals = None
    small_totals = None
    output_list = []
    grad_list = []
    for micro_step in range(micro_count):
        fetched = fetch_mixer()
        (in_full, out_full, up_full, down_full), (
            conv_full,
            convb_full,
            xproj_full,
            dtproj_full,
            dtb_full,
            alog_full,
            skip_full,
        ) = fetched
        rank_width = dtproj_full.shape[0]
        nstate = alog_full.shape[0]
        inner_width = in_full.shape[0] // 2
        rows_in = layer_input[micro_step, 0].astype(jnp.float32)
        segment = segments[micro_step, 0]
        route_row = routes[micro_step, 0, :, 0]
        keep_row = same_doc_shift(segment, 1)
        normed_one, norm_pull = jax.vjp(rms_scale, rows_in, gain_one)
        normed_low = normed_one.astype(jnp.bfloat16)
        joined = jnp.einsum("td,kd->tk", normed_low, in_full, preferred_element_type=jnp.float32)

        def conv_piece(inner_part, conv_taps, bias_row):
            return conv_silu(inner_part, conv_taps, bias_row, segment)

        conv_out, conv_pull = jax.vjp(
            conv_piece,
            joined[:, :inner_width],
            conv_full.astype(jnp.float32),
            convb_full.astype(jnp.float32),
        )
        conv_low = conv_out.astype(jnp.bfloat16)
        projected = jnp.dot(conv_low, xproj_full, preferred_element_type=jnp.float32)
        dt_low = projected[:, :rank_width].astype(jnp.bfloat16)
        dt_part = jnp.dot(dt_low, dtproj_full, preferred_element_type=jnp.float32)

        def scan_piece(
            conv_value, dt_value, dt_shift, b_rows, c_rows, log_rates, skip_row, gate_in
        ):
            return scan_mix(
                conv_value,
                dt_value,
                dt_shift,
                b_rows,
                c_rows,
                log_rates,
                skip_row,
                gate_in,
                keep_row,
                CH,
            )

        mixed_out, scan_pull = jax.vjp(
            scan_piece,
            conv_out,
            dt_part,
            dtb_full.astype(jnp.float32),
            projected[:, rank_width : rank_width + nstate],
            projected[:, rank_width + nstate :],
            alog_full.astype(jnp.float32),
            skip_full.astype(jnp.float32),
            joined[:, inner_width:],
        )
        mixed_low = mixed_out.astype(jnp.bfloat16)
        branch = jnp.dot(mixed_low, out_full, preferred_element_type=jnp.float32)
        residual = rows_in + branch
        chosen_rows = (
            route_row[:, None] == jnp.arange(expert_count, dtype=jnp.int32)[None]
        ).astype(jnp.float32)

        def route_piece(resid_value, gain_value, router_value):
            return norm_route(resid_value, gain_value, router_value, chosen_rows)

        (normed_two, gate_row), route_pull = jax.vjp(route_piece, residual, gain_two, router_full)
        placed = dispatch_matrix(route_row, expert_count, capacity).astype(jnp.bfloat16)
        sent_low = normed_two.astype(jnp.bfloat16)
        slot_rows = jnp.einsum(
            "tk,td->kd", placed, sent_low, preferred_element_type=jnp.float32
        ).astype(jnp.bfloat16)
        outgoing = slot_rows.reshape(expert_devices, local_experts, capacity, model_width)
        received = lax.all_to_all(outgoing, "expert", split_axis=0, concat_axis=0, tiled=True)
        hidden = jnp.einsum("sjcd,jfd->sjcf", received, up_full, preferred_element_type=jnp.float32)
        active_value, gelu_pull = jax.vjp(gelu_tanh, hidden)
        active_low = active_value.astype(jnp.bfloat16)
        returned = jnp.einsum(
            "sjcf,jfd->sjcd", active_low, down_full, preferred_element_type=jnp.float32
        ).astype(jnp.bfloat16)
        arrived = lax.all_to_all(returned, "expert", split_axis=0, concat_axis=0, tiled=True)
        gathered = jnp.dot(
            placed,
            arrived.reshape(expert_count * capacity, model_width),
            preferred_element_type=jnp.float32,
        )
        output_list.append((residual + gate_row[:, None] * gathered).astype(jnp.bfloat16))
        fetched = fetch_mixer()
        (in_full, out_full, up_full, down_full), (
            conv_full,
            convb_full,
            xproj_full,
            dtproj_full,
            dtb_full,
            alog_full,
            skip_full,
        ) = fetched
        cot_rows = cotangent[micro_step, 0].astype(jnp.float32)
        d_token_low = (cot_rows * gate_row[:, None]).astype(jnp.bfloat16)
        d_slots = jnp.einsum(
            "tk,td->kd", placed, d_token_low, preferred_element_type=jnp.float32
        ).astype(jnp.bfloat16)
        d_received = lax.all_to_all(
            d_slots.reshape(expert_devices, local_experts, capacity, model_width),
            "expert",
            split_axis=0,
            concat_axis=0,
            tiled=True,
        )
        down_term = jnp.einsum(
            "sjcf,sjcd->jfd", active_low, d_received, preferred_element_type=jnp.float32
        )
        d_active = jnp.einsum(
            "sjcd,jfd->sjcf", d_received, down_full, preferred_element_type=jnp.float32
        )
        d_hidden_low = gelu_pull(d_active)[0].astype(jnp.bfloat16)
        up_term = jnp.einsum(
            "sjcf,sjcd->jfd", d_hidden_low, received, preferred_element_type=jnp.float32
        )
        d_sent_slots = jnp.einsum(
            "sjcf,jfd->sjcd", d_hidden_low, up_full, preferred_element_type=jnp.float32
        ).astype(jnp.bfloat16)
        d_back = lax.all_to_all(d_sent_slots, "expert", split_axis=0, concat_axis=0, tiled=True)
        d_sent = jnp.dot(
            placed,
            d_back.reshape(expert_count * capacity, model_width),
            preferred_element_type=jnp.float32,
        )
        d_gate = jnp.sum(cot_rows * gathered, axis=1)
        d_resid_norm, d_gain_two, d_router = route_pull((d_sent, d_gate))
        d_residual = cot_rows + d_resid_norm
        d_branch_low = d_residual.astype(jnp.bfloat16)
        out_term = jnp.einsum(
            "tk,td->kd", mixed_low, d_branch_low, preferred_element_type=jnp.float32
        )
        d_mixed = jnp.einsum(
            "td,kd->tk", d_branch_low, out_full, preferred_element_type=jnp.float32
        )
        d_conv_scan, d_dt_part, d_dtb, d_brows, d_crows, d_alog, d_skip, d_gate_in = scan_pull(
            d_mixed
        )
        d_dt_low = d_dt_part.astype(jnp.bfloat16)
        dtproj_term = jnp.einsum("tr,tk->rk", dt_low, d_dt_low, preferred_element_type=jnp.float32)
        d_dt_rows = jnp.einsum(
            "tk,rk->tr", d_dt_low, dtproj_full, preferred_element_type=jnp.float32
        )
        d_proj_low = jnp.concatenate([d_dt_rows, d_brows, d_crows], axis=1).astype(jnp.bfloat16)
        xproj_term = jnp.einsum(
            "tk,tp->kp", conv_low, d_proj_low, preferred_element_type=jnp.float32
        )
        d_conv = d_conv_scan + jnp.einsum(
            "tp,kp->tk", d_proj_low, xproj_full, preferred_element_type=jnp.float32
        )
        d_inner, d_conv_taps, d_conv_bias = conv_pull(d_conv)
        d_joined_low = jnp.concatenate([d_inner, d_gate_in], axis=1).astype(jnp.bfloat16)
        in_term = jnp.einsum(
            "tk,td->kd", d_joined_low, normed_low, preferred_element_type=jnp.float32
        )
        d_normed = jnp.einsum(
            "tk,kd->td", d_joined_low, in_full, preferred_element_type=jnp.float32
        )
        d_rows_norm, d_gain_one = norm_pull(d_normed)
        grad_list.append(d_residual + d_rows_norm)
        dense_totals = add_terms(dense_totals, (in_term, out_term, up_term, down_term))
        mixer_totals = add_terms(
            mixer_totals, (d_conv_taps, d_conv_bias, xproj_term, dtproj_term, d_dtb, d_alog, d_skip)
        )
        small_totals = add_terms(small_totals, (d_gain_one, d_gain_two, d_router))
    in_total, out_total, up_total, down_total = dense_totals
    in_part, out_part, up_grad, down_grad = (
        lax.psum_scatter(
            in_total.astype(jnp.bfloat16), "dp", scatter_dimension=0, tiled=True
        ).astype(jnp.float32),
        lax.psum_scatter(
            out_total.astype(jnp.bfloat16), "dp", scatter_dimension=0, tiled=True
        ).astype(jnp.float32),
        lax.psum_scatter(
            up_total.astype(jnp.bfloat16), "dp", scatter_dimension=1, tiled=True
        ).astype(jnp.float32),
        lax.psum_scatter(
            down_total.astype(jnp.bfloat16), "dp", scatter_dimension=1, tiled=True
        ).astype(jnp.float32),
    )
    in_grad, out_grad = (
        lax.psum(in_part.astype(jnp.bfloat16), "expert").astype(jnp.float32),
        lax.psum(out_part.astype(jnp.bfloat16), "expert").astype(jnp.float32),
    )
    conv_total, convb_total, xproj_total, dtproj_total, dtb_total, alog_total, skip_total = (
        mixer_totals
    )
    conv_grad, convb_grad, xproj_grad, dtproj_grad, dtb_grad, alog_grad, skip_grad = (
        lax.psum_scatter(conv_total, ("dp", "expert"), scatter_dimension=1, tiled=True),
        lax.psum_scatter(convb_total, ("dp", "expert"), scatter_dimension=0, tiled=True),
        lax.psum_scatter(xproj_total, ("dp", "expert"), scatter_dimension=0, tiled=True),
        lax.psum_scatter(dtproj_total, ("dp", "expert"), scatter_dimension=1, tiled=True),
        lax.psum_scatter(dtb_total, ("dp", "expert"), scatter_dimension=0, tiled=True),
        lax.psum_scatter(alog_total, ("dp", "expert"), scatter_dimension=1, tiled=True),
        lax.psum_scatter(skip_total, ("dp", "expert"), scatter_dimension=0, tiled=True),
    )
    gain_one_total, gain_two_total, router_total = small_totals
    gain_one_grad, gain_two_grad, router_grad = lax.psum(
        (gain_one_total, gain_two_total, router_total), ("dp", "expert")
    )
    layer_output = jnp.stack(output_list, axis=0)[:, None]
    input_grad = jnp.stack(grad_list, axis=0)[:, None]
    return (
        layer_output,
        input_grad,
        gain_one_grad,
        in_grad,
        conv_grad,
        convb_grad,
        xproj_grad,
        dtproj_grad,
        dtb_grad,
        alog_grad,
        skip_grad,
        out_grad,
        gain_two_grad,
        router_grad,
        up_grad,
        down_grad,
    )


def solution(mesh):
    placed = (
        P(None, ("dp", "expert"), None, None),
        P(None, ("dp", "expert"), None),
        P(None, ("dp", "expert"), None, None),
        P(None, ("dp", "expert"), None, None),
        P(),
        P("dp", None),
        P(None, ("dp", "expert")),
        P(("dp", "expert")),
        P(("dp", "expert"), None),
        P(None, ("dp", "expert")),
        P(("dp", "expert")),
        P(None, ("dp", "expert")),
        P(("dp", "expert")),
        P("dp", None),
        P(),
        P(),
        P("expert", "dp", None),
        P("expert", "dp", None),
    )
    return jax.shard_map(
        on_device,
        mesh=mesh,
        in_specs=placed,
        out_specs=(
            P(None, ("dp", "expert"), None, None),
            P(None, ("dp", "expert"), None, None),
            P(),
            P("dp", None),
            P(None, ("dp", "expert")),
            P(("dp", "expert")),
            P(("dp", "expert"), None),
            P(None, ("dp", "expert")),
            P(("dp", "expert")),
            P(None, ("dp", "expert")),
            P(("dp", "expert")),
            P("dp", None),
            P(),
            P(),
            P("expert", "dp", None),
            P("expert", "dp", None),
        ),
        check_vma=False,
    )
```

profile of v0, /device:TPU:0, one launch (start us, length us, event | category | flops | bytes accessed | tf_op | source)
XLA Modules:
  0.0 4784.7 jit_solution(3323057267800405556)
XLA Ops:
  11.5 44.9 all-reduce.170
  56.5 40.4 all-gather
  97.1 41.4 all_gather.25
  138.7 42.0 all_gather.26
  180.8 38.3 all-gather.1
  224.7 7.5 fusion.234
  247.6 523.1 %while.79 = (s32[]{:T(128)}, f32[16,2304]{1,0:T(8,128)}, f32[6,16,2304]{2,1,0:T(8,128)}, f32[6,16,2304]{2,1,0:T(8,128)}, f32[6,16,2304]{2,1,0:T(8,128)}, /*index...) while((s32[]{:T(128)}, f32[16,2304]{1,0:T(8,128)}, ...), condition=%wide.region_13.15_spmd, body=%wide.region_11.14_spmd.sunk | while | flops 11059202 | bytes 124607680 | solution.py:65
  373.1 6.6 pad.2249
  773.3 522.5 %while.78 = (s32[]{:T(128)}, f32[16,2304]{1,0:T(8,128)}, f32[6,16,2304]{2,1,0:T(8,128)}, f32[6,16,2304]{2,1,0:T(8,128)}, f32[6,16,2304]{2,1,0:T(8,128)}, /*index...) while((s32[]{:T(128)}, f32[16,2304]{1,0:T(8,128)}, ...), condition=%wide.region_3.5_spmd, body=%wide.region_1.4_spmd.sunk | while | flops 11059202 | bytes 124607680 | solution.py:65
  1424.0 1215.6 %while.80 = (s32[]{:T(128)}, f32[16,2304]{1,0:T(8,128)}, f32[16,2304]{1,0:T(8,128)}, f32[6,16,2304]{2,1,0:T(8,128)}, f32[6,16,2304]{2,1,0:T(8,128)}, /*index=5*/...) while((s32[]{:T(128)}, f32[16,2304]{1,0:T(8,128)}, ...), condition=%wide.region_30.32_spmd.clone, body=%wide.region_23.31_spmd.clone.sunk | while | flops 34651652 | bytes 387687296 | solution.py:65
  1518.5 6.7 pad.2319
  1571.8 6.7 pad.2312
  1721.1 6.7 pad.2319
  1774.3 6.7 pad.2312
  1923.6 6.7 pad.2319
  1976.8 6.7 pad.2312
  2126.1 6.7 pad.2319
  2179.4 6.7 pad.2312
  2328.6 6.7 pad.2319
  2381.9 6.7 pad.2312
  2531.2 6.7 pad.2319
  2584.4 6.7 pad.2312
  2639.6 8.2 fusion.35
  2649.6 7.4 multiply_reduce_fusion.14
  2660.9 1216.9 %while.81 = (s32[]{:T(128)}, f32[16,2304]{1,0:T(8,128)}, f32[16,2304]{1,0:T(8,128)}, f32[6,16,2304]{2,1,0:T(8,128)}, f32[6,16,2304]{2,1,0:T(8,128)}, /*index=5*/...) while((s32[]{:T(128)}, f32[16,2304]{1,0:T(8,128)}, ...), condition=%wide.region_42.44_spmd.clone, body=%wide.region_35.43_spmd.clone.sunk | while | flops 34651652 | bytes 388277152 | solution.py:65
  2755.4 6.6 pad.2391
  2808.8 6.6 pad.2384
  2958.1 6.6 pad.2391
  3011.5 6.6 pad.2384
  3160.9 6.6 pad.2391
  3214.3 6.6 pad.2384
  3363.6 6.6 pad.2391
  3417.0 6.6 pad.2384
  3566.3 6.6 pad.2391
  3619.7 6.6 pad.2384
  3769.1 6.6 pad.2391
  3822.4 6.6 pad.2384
  3893.6 8.8 fusion.148
  3902.4 12.0 fusion.32
  3917.3 9.8 fusion.144
  3940.5 10.8 fusion.37
  3959.6 131.1 %reduce-scatter.11.cloned.1.call-done = bf16[576,1152]{1,0:T(8,128)(2,1)} async-done(((bf16[4608,1152]{1,0:T(8,128)(2,1)}), bf16[576,1152]{1,0:T(8,128)(2,1)}) %reduce-scatter.11.cloned.1.call-update) | async-done | bytes 1327120 | tf_op jit(solution)/shard_map/reduce_scatter | solution.py:339
  4097.4 123.7 %all-reduce.176.cloned.1.call-done = (f32[1152]{0:T(1024)}, f32[4,2304]{1,0:T(4,128)}, f32[2304]{0:T(1024)}, f32[2304]{0:T(1024)}, f32[2304]{0:T(1024)}, /*index=5*/f32[1152]{0:T(1024)}, f32[1152,4]{0,1:T(4,128)}) async-done(((f32[1152]{0:T(1024)}, f32[4,2304]{1,0:T(4,128)}, f32[2304]{0:T(1024)}, f32[2304]{0:T(1024)}, f32[2304]{0:T(1024)}, /*index=5*/f32[1152]{0:T(1024)}, f32[1152,4]{0,1:T(4,128)}), ...) | async-done | bytes 92176 | tf_op jit(solution)/shard_map/psum | solution.py:369
  4226.3 131.0 %all-reduce.178.cloned.1.call-done = (f32[72,2304]{1,0:T(8,128)}, f32[16,2304]{1,0:T(8,128)}) async-done(((f32[72,2304]{1,0:T(8,128)}, f32[16,2304]{1,0:T(8,128)}), (f32[72,2304]{1,0:T(8,128)}, f32[16,2304]{1,0:T(8,128)})) %all-reduce.178.cloned.1.call-update) | async-done | bytes 811024
  4360.3 130.6 %reduce-scatter.17.cloned.1.call-done = bf16[1,384,1152]{2,1,0:T(8,128)(2,1)} async-done(((bf16[1,3072,1152]{2,1,0:T(8,128)(2,1)}), bf16[1,384,1152]{2,1,0:T(8,128)(2,1)}) %reduce-scatter.17.cloned.1.call-update) | async-done | bytes 884752 | tf_op jit(solution)/shard_map/reduce_scatter | solution.py:348
  4493.4 129.1 %reduce-scatter.15.cloned.1.call-done = bf16[1,384,1152]{2,1,0:T(8,128)(2,1)} async-done(((bf16[1,3072,1152]{2,1,0:T(8,128)(2,1)}), bf16[1,384,1152]{2,1,0:T(8,128)(2,1)}) %reduce-scatter.15.cloned.1.call-update) | async-done | bytes 884752 | tf_op jit(solution)/shard_map/reduce_scatter | solution.py:345
  4625.0 49.1 %all-reduce.180.cloned.1.call-done = (bf16[576,1152]{1,0:T(8,128)(2,1)}, bf16[288,1152]{1,0:T(8,128)(2,1)}) async-done(((bf16[576,1152]{1,0:T(8,128)(2,1)}, bf16[288,1152]{1,0:T(8,128)(2,1)}), (bf16[576,1152]{1,0:T(8,128)(2,1)}, bf16[288,1152]{1,0:T(8,128)(2,1)})) %all-reduce.180.cloned.1.call-update) | async-done | bytes 1990672 | tf_op jit(solution)/shard_map/psum | solution.py:353
  4678.4 97.5 %reduce-scatter.19.cloned.1.call-done = f32[72,104]{1,0:T(8,128)} async-done(((f32[2304,104]{1,0:T(8,128)}), f32[72,104]{1,0:T(8,128)}) %reduce-scatter.19.cloned.1.call-update) | async-done | bytes 29968
  (4103 shorter events, 3526.2 us)
Async XLA Ops:
  7.2 1305.7 %copy-start = (bf16[1152,4]{0,1:T(4,128)(2,1)S(1)}, bf16[1152,4]{0,1:T(4,128)(2,1)}, u32[]{:S(2)}) copy-start(bf16[1152,4]{0,1:T(4,128)(2,1)} %param.42) | copy-start | bytes 27652
  7.2 217.4 %all-gather.7.cloned.1.call-start = ((), (), s32[]{:S(2)}) async-start(), calls=%async_computation.13 | async-start | bytes 11943936 | tf_op jit(solution)/shard_map/all_gather | solution.py:140
  8.0 1291.5 %all-gather.9.cloned.1.call-start = ((), (), s32[]{:S(2)}) async-start(), calls=%async_computation.14 | async-start | bytes 5971968 | tf_op jit(solution)/shard_map/all_gather | solution.py:141
  8.8 129.8 %copy-start.249 = (bf16[72,72]{1,0:T(8,128)(2,1)S(1)}, bf16[72,72]{1,0:T(8,128)(2,1)}, u32[]{:S(2)}) copy-start(bf16[72,72]{1,0:T(8,128)(2,1)} %param.36) | copy-start | bytes 31108
  8.8 1313.9 %all-gather.11.cloned.1.call-start = ((), (), s32[]{:S(2)}) async-start(), calls=%async_computation.15 | async-start | bytes 7962624 | tf_op jit(solution)/shard_map/all_gather | solution.py:142
  9.5 171.3 %copy-start.297 = (bf16[16,72]{1,0:T(8,128)(2,1)S(1)}, bf16[16,72]{1,0:T(8,128)(2,1)}, u32[]{:S(2)}) copy-start(bf16[16,72]{1,0:T(8,128)(2,1)} %param.38) | copy-start | bytes 6916
  9.5 1318.6 %all-gather.13.cloned.1.call-start = ((), (), s32[]{:S(2)}) async-start(), calls=%async_computation.16 | async-start | bytes 7962624 | tf_op jit(solution)/shard_map/all_gather | solution.py:143
  10.2 225.5 %copy-start.322 = (f32[96]{0:T(128)}, f32[96]{0:T(128)S(1)}, u32[]{:S(2)}) copy-start(f32[96]{0:T(128)S(1)} %get-tuple-element.1341) | copy-start | bytes 1156
  10.2 225.6 %copy-start.324 = (f32[96]{0:T(128)}, f32[96]{0:T(128)S(1)}, u32[]{:S(2)}) copy-start(f32[96]{0:T(128)S(1)} %get-tuple-element.1342) | copy-start | bytes 1156
  10.4 225.3 %copy-start.326 = (f32[96]{0:T(128)}, f32[96]{0:T(128)S(1)}, u32[]{:S(2)}) copy-start(f32[96]{0:T(128)S(1)} %get-tuple-element.1347) | copy-start | bytes 1156
  10.4 225.3 %copy-start.328 = (f32[96]{0:T(128)}, f32[96]{0:T(128)S(1)}, u32[]{:S(2)}) copy-start(f32[96]{0:T(128)S(1)} %get-tuple-element.1348) | copy-start | bytes 1156
  10.5 221.8 %copy-start.221 = (f32[1152]{0:T(1024)}, f32[1152]{0:T(1024)S(1)}, u32[]{:S(2)}) copy-start(f32[1152]{0:T(1024)S(1)} %convert_element_type.348) | copy-start | bytes 13828
  10.7 214.0 %copy-start.287 = (f32[96]{0:T(128)}, f32[96]{0:T(128)S(1)}, u32[]{:S(2)}) copy-start(f32[96]{0:T(128)S(1)} %fusion.255) | copy-start | bytes 1156
  10.7 221.6 %copy-start.289 = (f32[96]{0:T(128)}, f32[96]{0:T(128)S(1)}, u32[]{:S(2)}) copy-start(f32[96]{0:T(128)S(1)} %fusion.257) | copy-start | bytes 1156
  97.1 138.7 %copy-start.225 = (f32[2304]{0:T(1024)}, f32[2304]{0:T(1024)S(1)}, u32[]{:S(2)}) copy-start(f32[2304]{0:T(1024)S(1)} %get-tuple-element.986) | copy-start | bytes 27652
  97.1 138.7 %copy-start.240 = (f32[2304]{0:T(1024)}, f32[2304]{0:T(1024)S(1)}, u32[]{:S(2)}) copy-start(f32[2304]{0:T(1024)S(1)} %get-tuple-element.987) | copy-start | bytes 27652
  97.1 138.7 %copy-start.242 = (f32[2304]{0:T(1024)}, f32[2304]{0:T(1024)S(1)}, u32[]{:S(2)}) copy-start(f32[2304]{0:T(1024)S(1)} %get-tuple-element.988) | copy-start | bytes 27652
  97.1 138.7 %copy-start.244 = (f32[2304]{0:T(1024)}, f32[2304]{0:T(1024)S(1)}, u32[]{:S(2)}) copy-start(f32[2304]{0:T(1024)S(1)} %get-tuple-element.989) | copy-start | bytes 27652
  97.1 123.7 %copy-start.317 = (s32[2,1,96,1]{2,3,1,0:T(1,128)S(1)}, s32[2,1,96,1]{2,3,1,0:T(1,128)}, u32[]{:S(2)}) copy-start(s32[2,1,96,1]{2,3,1,0:T(1,128)} %param.29) | copy-start | bytes 2308
  138.5 101.6 %copy-start.219 = (bf16[2304,104]{1,0:T(8,128)(2,1)}, bf16[2304,104]{1,0:T(8,128)(2,1)S(1)}, u32[]{:S(2)}) copy-start(bf16[2304,104]{1,0:T(8,128)(2,1)S(1)} %all_gather.25) | copy-start | bytes 1437700
  1303.5 106.2 %copy-start.267 = (f32[96]{0:T(128)}, f32[96]{0:T(128)S(1)}, u32[]{:S(2)}) copy-start(f32[96]{0:T(128)S(1)} %fusion.256) | copy-start | bytes 1156
  1308.3 101.4 %copy-start.131 = (f32[96,1152]{1,0:T(8,128)}, f32[96,1152]{1,0:T(8,128)S(1)}, u32[]{:S(2)}) copy-start(f32[96,1152]{1,0:T(8,128)S(1)} %get-tuple-element.1358) | copy-start | bytes 1327108
  1308.3 101.4 %copy-start.265 = (f32[96]{0:T(128)}, f32[96]{0:T(128)S(1)}, u32[]{:S(2)}) copy-start(f32[96]{0:T(128)S(1)} %fusion.258) | copy-start | bytes 1156
  1309.4 9.8 all-to-all-start.2
  1319.2 14.6 all-to-all-start
  1333.8 12.2 all-to-all-start.3
  1346.0 9.9 all-to-all-start.1
  1358.4 10.6 all-to-all-start.4
  1368.9 13.4 all-to-all-start.6
  1382.4 15.4 all-to-all-start.5
  1397.7 9.8 all-to-all-start.7
  1401.2 2558.5 %reduce-scatter.13.cloned.1.call-start = ((), (), s32[]{:S(2)}) async-start(), calls=%async_computation.18 | async-start | bytes 5971968 | tf_op jit(solution)/shard_map/reduce_scatter | solution.py:342
  2647.8 1443.0 %reduce-scatter.11.cloned.1.call-start = ((), (), s32[]{:S(2)}) async-start(), calls=%async_computation.17 | async-start | bytes 11943936 | tf_op jit(solution)/shard_map/reduce_scatter | solution.py:339
  3914.6 306.5 %all-reduce.176.cloned.1.call-start = ((), (), s32[]{:S(2)}) async-start(), calls=%async_computation.22 | async-start | bytes 217088 | tf_op jit(solution)/shard_map/psum | solution.py:369
  3938.1 419.2 %all-reduce.178.cloned.1.call-start = ((), (), s32[]{:S(2)}) async-start(), calls=%async_computation.23 | async-start | bytes 1622016
  3940.4 550.5 %reduce-scatter.17.cloned.1.call-start = ((), (), s32[]{:S(2)}) async-start(), calls=%async_computation.20 | async-start | bytes 7962624 | tf_op jit(solution)/shard_map/reduce_scatter | solution.py:348
  3951.4 671.2 %reduce-scatter.15.cloned.1.call-start = ((), (), s32[]{:S(2)}) async-start(), calls=%async_computation.19 | async-start | bytes 7962624 | tf_op jit(solution)/shard_map/reduce_scatter | solution.py:345
  3959.5 131.3 %copy-start.321 = (f32[96]{0:T(128)S(1)}, f32[96]{0:T(128)}, u32[]{:S(2)}) copy-start(f32[96]{0:T(128)} %copy-done.320) | copy-start | bytes 1156
  3959.5 131.3 %copy-start.331 = (f32[96]{0:T(128)S(1)}, f32[96]{0:T(128)}, u32[]{:S(2)}) copy-start(f32[96]{0:T(128)} %get-tuple-element.980) | copy-start | bytes 1156
  3959.5 131.8 %copy-start.184 = (f32[96,2304]{1,0:T(8,128)S(1)}, f32[96,2304]{1,0:T(8,128)}, u32[]{:S(2)}) copy-start(f32[96,2304]{1,0:T(8,128)} %copy-done.181) | copy-start | bytes 2654212
  3959.5 131.8 %copy-start.252 = (bf16[96,72]{0,1:T(8,128)(2,1)S(1)}, bf16[96,72]{0,1:T(8,128)(2,1)}, u32[]{:S(2)}) copy-start(bf16[96,72]{0,1:T(8,128)(2,1)} %copy-done.251) | copy-start | bytes 41476
  3959.5 131.8 %copy-start.302 = (bf16[96,16]{0,1:T(8,128)(2,1)S(1)}, bf16[96,16]{0,1:T(8,128)(2,1)}, u32[]{:S(2)}) copy-start(bf16[96,16]{0,1:T(8,128)(2,1)} %copy-done.301) | copy-start | bytes 9220
  3959.6 131.8 %copy-start.306 = (bf16[96,16]{0,1:T(8,128)(2,1)S(1)}, bf16[96,16]{0,1:T(8,128)(2,1)}, u32[]{:S(2)}) copy-start(bf16[96,16]{0,1:T(8,128)(2,1)} %copy-done.305) | copy-start | bytes 9220
  3959.6 714.6 %all-reduce.180.cloned.1.call-start = ((), (), s32[]{:S(2)}) async-start(), calls=%async_computation.24 | async-start | bytes 3981312 | tf_op jit(solution)/shard_map/psum | solution.py:353
  4090.8 685.1 %reduce-scatter.19.cloned.1.call-start = ((), (), s32[]{:S(2)}) async-start(), calls=%async_computation.21 | async-start | bytes 1216512
  4674.2 103.5 %copy-start.1 = (bf16[1152,4]{0,1:T(4,128)(2,1)S(1)}, bf16[1152,4]{0,1:T(4,128)(2,1)}, u32[]{:S(2)}) copy-start(bf16[1152,4]{0,1:T(4,128)(2,1)} %param.42) | copy-start | bytes 27652
  4677.2 99.2 %copy-start.281 = (f32[1152]{0:T(1024)S(1)}, f32[1152]{0:T(1024)}, u32[]{:S(2)}) copy-start(f32[1152]{0:T(1024)} %get-tuple-element.2310) | copy-start | bytes 13828
  4677.2 99.8 %copy-start.250 = (f32[1152,4]{0,1:T(4,128)S(1)}, f32[1152,4]{0,1:T(4,128)}, u32[]{:S(2)}) copy-start(f32[1152,4]{0,1:T(4,128)} %get-tuple-element.2311) | copy-start | bytes 55300
  (1077 other events, 5103.9 us)
Sparse Core Ops, SparseCore 0:
  10.2 160.9 all-gather.6
  173.4 86.5 all-gather.8
  262.2 106.9 all-gather.10
  371.3 106.9 all-gather.12
  2647.9 100.3 reduce-scatter.12
  3914.7 175.9 reduce-scatter.10
  4098.3 122.7 all-reduce.175
  4227.8 129.4 all-reduce.177
  4361.5 129.3 reduce-scatter.16
  4494.4 128.0 reduce-scatter.14
  4625.1 48.9 all-reduce.179
  4679.7 96.1 reduce-scatter.18
where the time goes:
time: 4830 us; the launch traced here: 4780 us
  local copies, waits for them, and re-layouts  2370 us (49%)
  other arithmetic  1170 us (24%)
  waiting for transfers between devices  816 us (17%)
  blocking collectives  207 us (4%)
  matrix products  157 us (3%)
    pad x552, local copies, waits for them, and re-layouts, block_step(): lax.associative_scan(pair_combine, (factor, driven), axis=0)  2000 us
    add x144, other arithmetic, block_step(): lax.associative_scan(pair_combine, (factor, driven), axis=0)  265 us
    unnamed x14, waiting for transfers between devices  231 us
    mul x96, other arithmetic, pair_combine(): return (earlier[0] * latter[0], latter[0] * earlier[1] + latter[1])  187 us
    concatenate x144, other arithmetic, block_step(): lax.associative_scan(pair_combine, (factor, driven), axis=0)  170 us
    while x1752, local copies, waits for them, and re-layouts  132 us
    reduce_scatter x1, waiting for transfers between devices, on_device(): lax.psum_scatter(in_total.astype(jnp.bfloat16), 'dp', scatter_dimension=0...  131 us
    reduce_scatter x1, waiting for transfers between devices, on_device(): lax.psum_scatter(down_total.astype(jnp.bfloat16), 'dp', scatter_dimension...  131 us

commit v1 on v0

v1 whole, which is shorter than its diff:
```python
import jax
import jax.numpy as jnp
from jax import lax
from jax.experimental import pallas as pl
from jax.experimental.pallas import tpu as pltpu
from jax.sharding import PartitionSpec as P

LANES = 128
ROWS = 8

def wide(tile, width):
    return jnp.concatenate([tile] * (width // LANES), axis=1)

def narrow(values):
    total = values[:, :LANES]
    for start in range(LANES, values.shape[1], LANES):
        total = total + values[:, start : start + LANES]
    return total

def fold_states(pieces, position):
    folded = []
    for piece in pieces:
        total = piece[:ROWS]
        for start in range(ROWS, piece.shape[0], ROWS):
            total = total + piece[start : start + ROWS]
        folded.append(total)
    low = (position & 4) == 0
    folded = [
        jnp.where(low, a, b) + pltpu.roll(jnp.where(low, b, a), 4, 0)
        for a, b in zip(folded[:4], folded[4:])
    ]
    for step in (2, 1):
        low = (position & step) == 0
        half = len(folded) // 2
        folded = [
            jnp.where(low, a + pltpu.roll(a, ROWS - step, 0), b + pltpu.roll(b, step, 0))
            for a, b in zip(folded[:half], folded[half:])
        ]
    return folded[0]

def scan_forward(decay_ref, drive_ref, b_ref, c_ref, rate_ref, out_ref):
    length, width = decay_ref.shape[1:]
    rate = rate_ref[...]
    position = lax.broadcasted_iota(jnp.int32, (ROWS, width), 0)

    def block(index, state):
        start = pl.multiple_of(index * ROWS, ROWS)
        pieces = []
        for offset in range(ROWS):
            t = start + offset
            factor = jnp.exp2(decay_ref[0, pl.ds(t, 1), :] * rate)
            state = factor * state + drive_ref[0, pl.ds(t, 1), :] * wide(b_ref[0, t], width)
            pieces.append(state * wide(c_ref[0, t], width))
        out_ref[0, pl.ds(start, ROWS), :] = fold_states(pieces, position)
        return state

    lax.fori_loop(0, length // ROWS, block, jnp.zeros_like(rate))

def scan_backward(
    decay_ref, drive_ref, b_ref, c_ref, rate_ref, dout_ref,
    ddrive_ref, ddecay_ref, drate_ref, db_ref, dc_ref, state_ref, factor_ref,
):
    length, width = decay_ref.shape[1:]
    rate = rate_ref[...]
    position = lax.broadcasted_iota(jnp.int32, (ROWS, width), 0)

    @pl.when(pl.program_id(1) == 0)
    def _():
        db_ref[...] = jnp.zeros_like(db_ref)
        dc_ref[...] = jnp.zeros_like(dc_ref)

    state_ref[0] = jnp.zeros_like(rate)

    def replay(index, state):
        start = pl.multiple_of(index * ROWS, ROWS)
        for offset in range(ROWS):
            t = start + offset
            factor = jnp.exp2(decay_ref[0, pl.ds(t, 1), :] * rate)
            state = factor * state + drive_ref[0, pl.ds(t, 1), :] * wide(b_ref[0, t], width)
            factor_ref[t] = factor
            state_ref[t + 1] = state
        return state

    lax.fori_loop(0, length // ROWS, replay, jnp.zeros_like(rate))

    def block(index, carried):
        later, drate = carried
        start = pl.multiple_of(length - ROWS - index * ROWS, ROWS)
        drive_pieces = [None] * ROWS
        decay_pieces = [None] * ROWS
        for offset in reversed(range(ROWS)):
            t = start + offset
            dout = dout_ref[0, pl.ds(t, 1), :]
            dstate = later + dout * wide(c_ref[0, t], width)
            dc_ref[0, t] += narrow(dout * state_ref[t + 1])
            db_ref[0, t] += narrow(dstate * drive_ref[0, pl.ds(t, 1), :])
            drive_pieces[offset] = dstate * wide(b_ref[0, t], width)
            later = dstate * factor_ref[t]
            power = later * state_ref[t]
            decay_pieces[offset] = power * rate
            drate = drate + power * decay_ref[0, pl.ds(t, 1), :]
        ddrive_ref[0, pl.ds(start, ROWS), :] = fold_states(drive_pieces, position)
        ddecay_ref[0, pl.ds(start, ROWS), :] = fold_states(decay_pieces, position)
        return later, drate

    zero = jnp.zeros_like(rate)
    drate_ref[0] = lax.fori_loop(0, length // ROWS, block, (zero, zero))[1]

def tile_width(width):
    for tiles in (3, 2, 1):
        if width % (tiles * LANES) == 0:
            return tiles * LANES
    return width

def scan_specs(length, states, width):
    tokens = pl.BlockSpec((1, length, width), lambda s, c: (s, 0, c))
    maps = pl.BlockSpec((1, length, states, LANES), lambda s, c: (s, 0, 0, 0))
    rates = pl.BlockSpec((states, width), lambda s, c: (0, c))
    return tokens, maps, rates

def run_forward(decay, drive, b_wide, c_wide, rate):
    count, length, channels = decay.shape
    states = rate.shape[0]
    width = tile_width(channels)
    tokens, maps, rates = scan_specs(length, states, width)
    return pl.pallas_call(
        scan_forward,
        grid=(count, channels // width),
        in_specs=[tokens, tokens, maps, maps, rates],
        out_specs=tokens,
        out_shape=jax.ShapeDtypeStruct(decay.shape, jnp.float32),
        cost_estimate=pl.CostEstimate(
            flops=8 * decay.size * states, transcendentals=decay.size * states,
            bytes_accessed=4 * (3 * decay.size + 2 * b_wide.size)),
        name="scan_forward",
    )(decay, drive, b_wide, c_wide, rate)

def run_backward(decay, drive, b_wide, c_wide, rate, dout):
    count, length, channels = decay.shape
    states = rate.shape[0]
    width = tile_width(channels)
    tokens, maps, rates = scan_specs(length, states, width)
    full = jax.ShapeDtypeStruct(decay.shape, jnp.float32)
    return pl.pallas_call(
        scan_backward,
        grid=(count, channels // width),
        in_specs=[tokens, tokens, maps, maps, rates, tokens],
        out_specs=[tokens, tokens, pl.BlockSpec((1, states, width), lambda s, c: (s, 0, c)), maps, maps],
        out_shape=[full, full, jax.ShapeDtypeStruct((count, states, channels), jnp.float32),
            jax.ShapeDtypeStruct(b_wide.shape, jnp.float32), jax.ShapeDtypeStruct(b_wide.shape, jnp.float32)],
        scratch_shapes=[pltpu.VMEM((length + 1, states, width), jnp.float32), pltpu.VMEM((length, states, width), jnp.float32)],
        cost_estimate=pl.CostEstimate(
            flops=30 * decay.size * states, transcendentals=decay.size * states,
            bytes_accessed=4 * (5 * decay.size + 4 * b_wide.size)),
        compiler_params=pltpu.CompilerParams(vmem_limit_bytes=32 << 20),
        name="scan_backward",
    )(decay, drive, b_wide, c_wide, rate, dout)

HIGHEST = lax.Precision.HIGHEST
EPSILON = 1e-05
LOG2E = 1.4426950408889634
FAR = 1e30
LOW = jnp.bfloat16
BOTH = ("dp", "expert")


def dot(left, right, contract):
    return lax.dot_general(left, right, (contract, ((), ())), preferred_element_type=jnp.float32)


def rms_scale(values, gain_row):
    return (
        values * lax.rsqrt(jnp.mean(values * values, axis=-1, keepdims=True) + EPSILON) * gain_row
    )


def gelu_tanh(values):
    return jax.nn.gelu(values, approximate=True)


def norm_route(residual, gain_two, router_full, chosen_rows):
    normed_two = rms_scale(residual, gain_two)
    logits = jnp.dot(normed_two, router_full, precision=HIGHEST, preferred_element_type=jnp.float32)
    probabilities = jax.nn.softmax(logits, axis=-1)
    return (normed_two, jnp.sum(probabilities * chosen_rows, axis=1))


def later_rows(values, offset):
    if offset == 0:
        return values
    return jnp.pad(values, ((0, 0), (offset, 0), (0, 0)))[:, : values.shape[1]]


def earlier_rows(values, offset):
    if offset == 0:
        return values
    return jnp.pad(values, ((0, 0), (0, offset), (0, 0)))[:, offset:]


def same_document(segments, offset):
    if offset == 0:
        return jnp.ones(segments.shape, jnp.float32)
    padded = jnp.pad(segments, ((0, 0), (offset, 0)), constant_values=-1)
    return (padded[:, : segments.shape[1]] == segments).astype(jnp.float32)


def conv_sum(inner, taps, bias_row, masks):
    count = taps.shape[0]
    total = bias_row
    for offset in range(count):
        total = total + taps[count - 1 - offset] * later_rows(inner, offset) * masks[offset]
    return total


def dispatch_matrix(route_rows, expert_count, capacity, padded_capacity):
    length = route_rows.shape[1]
    chosen = (
        route_rows[:, :, None] == jnp.arange(expert_count, dtype=jnp.int32)[None, None]
    ).astype(jnp.float32)
    before = jnp.tril(jnp.ones((length, length), jnp.float32), -1)
    earlier = jnp.einsum("tu,sue->ste", before, chosen, preferred_element_type=jnp.float32)
    slot = jnp.sum(earlier * chosen, axis=2).astype(jnp.int32)
    places = jnp.arange(padded_capacity, dtype=jnp.int32)
    taken = ((slot[:, :, None] == places) & (places < capacity)).astype(jnp.float32)
    return (chosen[:, :, :, None] * taken[:, :, None, :]).reshape(
        route_rows.shape[0], length, expert_count * padded_capacity
    )


def own_part(weight, axis_name):
    rows = weight.shape[0] // lax.axis_size(axis_name)
    return lax.dynamic_slice_in_dim(weight, lax.axis_index(axis_name) * rows, rows, axis=0)


def on_device(
    layer_input,
    segments,
    routes,
    cotangent,
    norm1_gain,
    in_weight,
    conv_weight,
    conv_bias,
    xproj_weight,
    dtproj_weight,
    dt_bias,
    a_log,
    skip_gain,
    out_weight,
    norm2_gain,
    router_weight,
    up_weight,
    down_weight,
):
    seq_len, model_width = layer_input.shape[2:]
    sequences = layer_input.shape[0] * layer_input.shape[1]
    tokens = sequences * seq_len
    expert_devices = lax.axis_size("expert")
    dp_devices = lax.axis_size("dp")
    local_experts = up_weight.shape[0]
    assert local_experts == 1
    expert_count = expert_devices
    capacity = seq_len * 5 // (4 * expert_count)
    padded_capacity = -(-capacity // 16) * 16
    slots = sequences * padded_capacity
    taps = conv_weight.shape[0]
    rank = dtproj_weight.shape[0]
    states = a_log.shape[0]
    pair = [(i, i ^ 1) for i in range(dp_devices)]
    ring = [(i, (i + 2) % dp_devices) for i in range(dp_devices)]
    steps = dp_devices // 2

    with jax.named_scope("fetch_in"):
        in_full = lax.all_gather(own_part(in_weight, "expert"), BOTH, axis=0, tiled=True)
    with jax.named_scope("fetch_small"):
        small = jnp.concatenate(
            [
                xproj_weight,
                dtproj_weight.T,
                a_log.T,
                conv_weight.T,
                conv_bias[:, None],
                dt_bias[:, None],
                skip_gain[:, None],
            ],
            axis=1,
        )
        small_full = lax.all_gather(small, BOTH, axis=0, tiled=True)
    with jax.named_scope("fetch_out"):
        out_full = lax.all_gather(own_part(out_weight, "expert"), BOTH, axis=0, tiled=True)
    with jax.named_scope("fetch_expert"):
        ups = [up_weight[0]]
        downs = [down_weight[0]]
        for _ in range(steps - 1):
            ups.append(lax.ppermute(ups[-1], "dp", ring))
            downs.append(lax.ppermute(downs[-1], "dp", ring))

    xproj_width = rank + 2 * states
    xproj_full = small_full[:, :xproj_width]
    across = small_full[:, xproj_width:].T
    dtproj_full = across[:rank]
    across = across[rank:].astype(jnp.float32)
    log_rates = across[:states]
    conv_full = across[states : states + taps]
    convb_full = across[states + taps]
    dtb_full = across[states + taps + 1]
    skip_full = across[states + taps + 2]
    inner_width = out_full.shape[0]
    gain_one = norm1_gain.astype(jnp.float32)
    gain_two = norm2_gain.astype(jnp.float32)
    router_full = router_weight.astype(jnp.float32)

    def split(values):
        return values.reshape(sequences, seq_len, values.shape[-1])

    def flat(values):
        return values.reshape(tokens, values.shape[-1])

    rows_in = layer_input.reshape(tokens, model_width).astype(jnp.float32)
    cot_rows = cotangent.reshape(tokens, model_width).astype(jnp.float32)
    segment_rows = segments.reshape(sequences, seq_len)
    route_rows = routes.reshape(sequences, seq_len)
    masks = [same_document(segment_rows, offset)[:, :, None] for offset in range(taps)]
    normed_one, norm_pull = jax.vjp(rms_scale, rows_in, gain_one)
    normed_low = normed_one.astype(LOW)
    joined = dot(normed_low, in_full, ((1,), (1,)))
    inner = split(joined[:, :inner_width])
    gate_in = split(joined[:, inner_width:])
    conv_out, silu_pull = jax.vjp(jax.nn.silu, conv_sum(inner, conv_full, convb_full, masks))
    conv_low = flat(conv_out).astype(LOW)
    projected = dot(conv_low, xproj_full, ((1,), (0,)))
    dt_low = projected[:, :rank].astype(LOW)
    b_wide = jnp.broadcast_to(
        split(projected[:, rank : rank + states])[..., None], (sequences, seq_len, states, LANES)
    )
    c_wide = jnp.broadcast_to(
        split(projected[:, rank + states :])[..., None], (sequences, seq_len, states, LANES)
    )
    dt_sum = split(dot(dt_low, dtproj_full, ((1,), (0,)))) + dtb_full
    delta = jax.nn.softplus(dt_sum)
    decay = jnp.where(masks[1] > 0, delta, FAR)
    drive = delta * conv_out
    rate = -jnp.exp(log_rates)
    rate_two = rate * LOG2E
    scanned = run_forward(decay, drive, b_wide, c_wide, rate_two)
    mixed = scanned + skip_full * conv_out
    gate_silu, gate_pull = jax.vjp(jax.nn.silu, gate_in)
    mixed_low = flat(mixed * gate_silu).astype(LOW)
    residual = rows_in + dot(mixed_low, out_full, ((1,), (0,)))

    chosen_rows = (
        route_rows.reshape(tokens, 1) == jnp.arange(expert_count, dtype=jnp.int32)[None]
    ).astype(jnp.float32)

    def route_piece(resid_value, gain_value, router_value):
        return norm_route(resid_value, gain_value, router_value, chosen_rows)

    (normed_two, gate_row), route_pull = jax.vjp(route_piece, residual, gain_two, router_full)
    placed = dispatch_matrix(route_rows, expert_count, capacity, padded_capacity).astype(LOW)
    sending = jnp.concatenate(
        [normed_two.astype(LOW), (cot_rows * gate_row[:, None]).astype(LOW)], axis=1
    )
    packed = jnp.einsum(
        "stk,std->skd", placed, split(sending), preferred_element_type=jnp.float32
    ).astype(LOW)
    packed = packed.reshape(sequences, expert_count, padded_capacity, 2 * model_width)
    packed = packed.transpose(1, 0, 2, 3).reshape(expert_count, slots, 2 * model_width)
    received = lax.all_to_all(packed, "expert", split_axis=0, concat_axis=0, tiled=True)
    received = received.reshape(expert_count * slots, 2 * model_width)
    own_count = received.shape[0]
    with jax.named_scope("pair_rows"):
        partner = lax.ppermute(received, "dp", pair)
    rows_all = jnp.concatenate([received, partner], axis=0)
    slot_rows = rows_all[:, :model_width]
    d_returned = rows_all[:, model_width:]

    returned = 0.0
    d_slots = 0.0
    up_terms = []
    down_terms = []
    for up, down in zip(ups, downs):
        hidden = dot(slot_rows, up, ((1,), (1,)))
        active, gelu_pull = jax.vjp(gelu_tanh, hidden)
        active_low = active.astype(LOW)
        returned = returned + dot(active_low, down, ((1,), (0,)))
        d_active = dot(d_returned, down, ((1,), (1,)))
        d_hidden_low = gelu_pull(d_active)[0].astype(LOW)
        d_slots = d_slots + dot(d_hidden_low, up, ((1,), (0,)))
        down_terms.append(dot(active_low, d_returned, ((0,), (0,))))
        up_terms.append(dot(d_hidden_low, slot_rows, ((0,), (0,))))
    results = jnp.concatenate([returned, d_slots], axis=1)
    with jax.named_scope("pair_results"):
        from_partner = lax.ppermute(results[own_count:].astype(LOW), "dp", pair)
    results = (results[:own_count] + from_partner.astype(jnp.float32)).astype(LOW)
    arrived = lax.all_to_all(
        results.reshape(expert_count, slots, 2 * model_width),
        "expert",
        split_axis=0,
        concat_axis=0,
        tiled=True,
    )
    arrived = arrived.reshape(expert_count, sequences, padded_capacity, 2 * model_width)
    arrived = arrived.transpose(1, 0, 2, 3).reshape(
        sequences, expert_count * padded_capacity, 2 * model_width
    )
    gathered_both = flat(
        jnp.einsum("stk,skd->std", placed, arrived, preferred_element_type=jnp.float32)
    )
    gathered = gathered_both[:, :model_width]
    d_sent = gathered_both[:, model_width:]
    layer_output = (residual + gate_row[:, None] * gathered).astype(LOW)

    with jax.named_scope("reduce_expert"):

        def ring_sum(terms):
            travelling = terms[1 % steps]
            for step in range(2, steps + 1):
                moved = lax.ppermute(travelling.astype(LOW), "dp", ring)
                travelling = terms[step % steps] + moved.astype(jnp.float32)
            return travelling

        up_grad = ring_sum(up_terms)
        down_grad = ring_sum(down_terms)

    d_gate = jnp.sum(cot_rows * gathered, axis=1)
    d_resid_norm, d_gain_two, d_router = route_pull((d_sent, d_gate))
    d_residual = cot_rows + d_resid_norm
    d_branch_low = d_residual.astype(LOW)

    out_term = dot(mixed_low, d_branch_low, ((0,), (0,))).astype(LOW)
    with jax.named_scope("reduce_out"):
        out_part = lax.psum_scatter(out_term, BOTH, scatter_dimension=0, tiled=True)
    d_mixed = split(dot(d_branch_low, out_full, ((1,), (1,))))
    d_gate_in = gate_pull(d_mixed * mixed)[0]
    d_scanned = d_mixed * gate_silu
    d_drive, d_decay, d_rate, d_b, d_c = run_backward(
        decay, drive, b_wide, c_wide, rate_two, d_scanned
    )
    d_skip = jnp.sum(d_scanned * conv_out, axis=(0, 1))
    d_alog = jnp.sum(d_rate, axis=0) * rate
    d_delta = d_decay * (1.0 / LOG2E) + d_drive * conv_out
    d_dt = d_delta * jax.nn.sigmoid(dt_sum)
    d_dtb = jnp.sum(d_dt, axis=(0, 1))
    d_dt_low = flat(d_dt).astype(LOW)
    dtproj_term = dot(d_dt_low, dt_low, ((0,), (0,)))
    d_dt_rows = dot(d_dt_low, dtproj_full, ((1,), (1,)))
    d_proj_low = jnp.concatenate(
        [
            d_dt_rows,
            jnp.sum(d_b, axis=3).reshape(tokens, states),
            jnp.sum(d_c, axis=3).reshape(tokens, states),
        ],
        axis=1,
    ).astype(LOW)
    xproj_term = dot(conv_low, d_proj_low, ((0,), (0,)))
    d_conv = (
        d_drive * delta
        + d_scanned * skip_full
        + split(dot(d_proj_low, xproj_full, ((1,), (1,))))
    )
    d_sum = silu_pull(d_conv)[0]
    d_convb = jnp.sum(d_sum, axis=(0, 1))
    d_inner = jnp.zeros_like(d_sum)
    tap_rows = [None] * taps
    for offset in range(taps):
        masked = d_sum * masks[offset]
        tap_rows[taps - 1 - offset] = jnp.sum(masked * later_rows(inner, offset), axis=(0, 1))
        d_inner = d_inner + conv_full[taps - 1 - offset] * earlier_rows(masked, offset)
    d_joined_low = jnp.concatenate([flat(d_inner), flat(d_gate_in)], axis=1).astype(LOW)
    in_term = dot(d_joined_low, normed_low, ((0,), (0,))).astype(LOW)
    with jax.named_scope("reduce_in"):
        in_part = lax.psum_scatter(in_term, BOTH, scatter_dimension=0, tiled=True)
    d_normed = dot(d_joined_low, in_full, ((1,), (0,)))
    d_rows_norm, d_gain_one = norm_pull(d_normed)
    input_grad = d_residual + d_rows_norm

    with jax.named_scope("reduce_small"):
        small_term = jnp.concatenate(
            [xproj_term, dtproj_term, d_alog.T]
            + [row[:, None] for row in tap_rows]
            + [d_convb[:, None], d_dtb[:, None], d_skip[:, None]],
            axis=1,
        ).astype(LOW)
        devices = dp_devices * expert_devices
        pieces = lax.all_to_all(
            small_term.reshape(devices, inner_width // devices, -1),
            BOTH,
            split_axis=0,
            concat_axis=0,
            tiled=True,
        )
        small_grad = jnp.sum(pieces.astype(jnp.float32), axis=0)
    xproj_grad = small_grad[:, :xproj_width]
    small_across = small_grad[:, xproj_width:].T
    dtproj_grad = small_across[:rank]
    alog_grad = small_across[rank : rank + states]
    conv_grad = small_across[rank + states : rank + states + taps]
    convb_grad, dtb_grad, skip_grad = small_across[rank + states + taps :]
    with jax.named_scope("reduce_gains"):
        gains = lax.psum(
            jnp.concatenate([d_gain_one[None], d_gain_two[None], d_router.T], axis=0), BOTH
        )
    with jax.named_scope("share_rows"):
        out_grad = lax.all_gather(out_part, "expert", axis=0, tiled=True).astype(jnp.float32)
        in_grad = lax.all_gather(in_part, "expert", axis=0, tiled=True).astype(jnp.float32)

    return (
        layer_output.reshape(layer_input.shape),
        input_grad.reshape(layer_input.shape),
        gains[0],
        in_grad,
        conv_grad,
        convb_grad,
        xproj_grad,
        dtproj_grad,
        dtb_grad,
        alog_grad,
        skip_grad,
        out_grad,
        gains[1],
        gains[2:].T,
        up_grad[None],
        down_grad[None],
    )


def solution(mesh):
    placed = (
        P(None, ("dp", "expert"), None, None),
        P(None, ("dp", "expert"), None),
        P(None, ("dp", "expert"), None, None),
        P(None, ("dp", "expert"), None, None),
        P(),
        P("dp", None),
        P(None, ("dp", "expert")),
        P(("dp", "expert")),
        P(("dp", "expert"), None),
        P(None, ("dp", "expert")),
        P(("dp", "expert")),
        P(None, ("dp", "expert")),
        P(("dp", "expert")),
        P("dp", None),
        P(),
        P(),
        P("expert", "dp", None),
        P("expert", "dp", None),
    )
    return jax.shard_map(
        on_device,
        mesh=mesh,
        in_specs=placed,
        out_specs=(
            P(None, ("dp", "expert"), None, None),
            P(None, ("dp", "expert"), None, None),
            P(),
            P("dp", None),
            P(None, ("dp", "expert")),
            P(("dp", "expert")),
            P(("dp", "expert"), None),
            P(None, ("dp", "expert")),
            P(("dp", "expert")),
            P(None, ("dp", "expert")),
            P(("dp", "expert")),
            P("dp", None),
            P(),
            P(),
            P("expert", "dp", None),
            P("expert", "dp", None),
        ),
        check_vma=False,
    )
```

time: 4830 us -> 783 us (0.16)
  local copies, waits for them, and re-layouts: 2370 us -> 62.8 us
  other arithmetic: 1170 us -> 42.2 us
  waiting for transfers between devices: 816 us -> 379 us
  blocking collectives: 207 us -> 115 us
  matrix products: 157 us -> 91.8 us
    pad x552 -> x0, local copies, waits for them, and re-layouts: 2000 us -> none  [block_step(): lax.associative_scan(pair_combine, (factor, driven), axis=0)]
    reduce_scatter x4 -> x1, waiting for transfers between devices: 391 us -> 0.02 us  [on_device(): in_part = lax.psum_scatter(in_term, BOTH, scatter_dimension=0, tiled=True)]
    add x247 -> x3, other arithmetic: 356 us -> 2.36 us  [the longest x1 2.35 us: on_device(): input_grad = d_residual + d_rows_norm]
    mul x181 -> x2, other arithmetic: 234 us -> 3.96 us  [the longest x1 3.2 us: on_device(): drive = delta * conv_out]
    reduce_sum x51 -> x9, other arithmetic: 247 us -> 20.2 us  [the longest x1 7.84 us: on_device(): d_convb = jnp.sum(d_sum, axis=(0, 1))]
    ppermute x0 -> x14, waiting for transfers between devices: none -> 207 us  [the longest x6 97.3 us: ring_sum(): moved = lax.ppermute(travelling.astype(LOW), 'dp', ring)]
    psum x2 -> x0, waiting for transfers between devices: 173 us -> none  [the longest x1 124 us: on_device(): lax.psum((gain_one_total, gain_two_total, router_total), ('dp', 'expert'))]
    concatenate x146 -> x3, other arithmetic: 170 us -> 1.54 us  [the longest x1 1.42 us: on_device(): rows_all = jnp.concatenate([received, partner], axis=0)]
where the time goes in v1:
time: 783 us; the launch traced here: 771 us
  waiting for transfers between devices  379 us (48%)
  blocking collectives  115 us (15%)
  matrix products  91.8 us (12%)
  local copies, waits for them, and re-layouts  62.8 us (8%)
  other arithmetic  42.2 us (5%)
  Pallas kernels  40.2 us (5%)
  starting transfers between devices  24.4 us (3%)
  between operations  15.8 us (2%)
    ppermute x6, waiting for transfers between devices, ring_sum(): moved = lax.ppermute(travelling.astype(LOW), 'dp', ring)  97.3 us
    dot_general x36, matrix products, dot(): lax.dot_general(left, right, (contract, ((), ())), preferred_element_type...  87.9 us
    unnamed x6, waiting for transfers between devices  67.4 us
    psum x1, blocking collectives, on_device(): lax.psum(jnp.concatenate([d_gain_one[None], d_gain_two[None], d_router.T]...  58.4 us
    ppermute x3, waiting for transfers between devices, on_device(): downs.append(lax.ppermute(downs[-1], 'dp', ring))  52.1 us
    all_gather x1, blocking collectives, on_device(): small_full = lax.all_gather(small, BOTH, axis=0, tiled=True)  48.5 us
    all_gather x1, waiting for transfers between devices, on_device(): lax.all_gather(own_part(in_weight, 'expert'), BOTH, axis=0, tiled=True)  36.3 us
    ppermute x3, waiting for transfers between devices, on_device(): ups.append(lax.ppermute(ups[-1], 'dp', ring))  31.7 us
  transfers between devices with their start and end apart: 22, of which 17 were waited for; matrix products, arithmetic and copies ran while one was open for 15% of the time, Pallas kernels for 2%

profile of v1, /device:TPU:0, one launch (start us, length us, event | category | flops | bytes accessed | tf_op | source)
XLA Modules:
  0.0 771.4 jit_solution(13354536941338224057)
XLA Ops:
  12.2 48.5 %all_gather.15 = bf16[2304,199]{1,0:T(8,128)(2,1)S(1)} all-gather(bf16[72,199]{1,0:T(8,128)(2,1)S(1)} %concatenate.44), channel_id=1, replica_groups=mesh['dp'=8,'expert'=4] {'dp','expert'}, dimensions={0}, use_global_device_ids=true | all-gather | bytes 945648 | tf_op jit(solution)/shard_map/fetch_small/all_gather | solution.py:288
  67.5 36.3 %all-gather.4.cloned.1.call-done = bf16[4608,1152]{1,0:T(8,128)(2,1)} async-done(((bf16[144,1152]{1,0:T(8,128)(2,1)}), bf16[4608,1152]{1,0:T(8,128)(2,1)}) %all-gather.4.cloned.1.call-update) | async-done | bytes 10616848 | tf_op jit(solution)/shard_map/fetch_in/all_gather | solution.py:274
  103.8 7.7 fusion.125
  116.7 3.2 fusion.116
  123.2 14.2 %scan_forward.1 = f32[2,96,2304]{2,1,0:T(8,128)} custom-call(f32[2,96,2304]{2,1,0:T(8,128)} %get-tuple-element.161.decay_ref, f32[2,96,2304]{2,1,0:T(8,128)} %get-tuple-element.160.drive_ref, f32[2,96,16,128]{3,2,1,0:T(8,128)} %broadcast_in_dim.52.b_ref, f32[2,96,16,128]{3,2,1,0:T(8,128)} %broadcast_in_dim.98.c_ref, f32[16,2304]{1,0:T(8,128)} %fusion.78.rate_ref), custom_call_target="tpu_custom_call" | custom-call | flops 56623104 | bytes 8454144 | tf_op jit(solution)/shard_map/scan_forward/pallas_call | solution.py:126
  137.4 3.4 multiply_convert_fusion
  140.8 29.9 %all-gather.6.cloned.1.call-done = bf16[2304,1152]{1,0:T(8,128)(2,1)} async-done(((bf16[72,1152]{1,0:T(8,128)(2,1)}), bf16[2304,1152]{1,0:T(8,128)(2,1)}) %all-gather.6.cloned.1.call-update) | async-done | bytes 5308432 | tf_op jit(solution)/shard_map/fetch_out/all_gather | solution.py:290
  170.8 4.3 multiply_reduce_fusion.9
  178.3 4.3 all-to-all-start
  185.4 13.1 %all-to-all-done = bf16[4,64,2304]{2,1,0:T(8,128)(2,1)} async-done(((bf16[4,64,2304]{2,1,0:T(8,128)(2,1)}), bf16[4,64,2304]{2,1,0:T(8,128)(2,1)}, u32[]{:S(2)}, u32[]{:S(2)}) %all-to-all-start) | async-done | bytes 1179680 | tf_op jit(solution)/shard_map/all_to_all | solution.py:368
  200.0 7.3 collective-permute-done.1
  207.4 18.8 %collective-permute-done.2 = bf16[384,1152]{1,0:T(8,128)(2,1)} collective-permute-done((bf16[384,1152]{1,0:T(8,128)(2,1)}, bf16[384,1152]{1,0:T(8,128)(2,1)}, u32[]{:S(2)}, u32[]{:S(2)}) %collective-permute-start.2) | collective-permute-done | bytes 884768 | tf_op jit(solution)/shard_map/fetch_expert/ppermute | solution.py:296
  226.3 18.7 %collective-permute-done.3 = bf16[384,1152]{1,0:T(8,128)(2,1)S(1)} collective-permute-done((bf16[384,1152]{1,0:T(8,128)(2,1)}, bf16[384,1152]{1,0:T(8,128)(2,1)S(1)}, u32[]{:S(2)}, u32[]{:S(2)}) %collective-permute-start.3) | collective-permute-done | bytes 884768 | tf_op jit(solution)/shard_map/fetch_expert/ppermute | solution.py:295
  245.2 18.8 %collective-permute-done.4 = bf16[384,1152]{1,0:T(8,128)(2,1)S(1)} collective-permute-done((bf16[384,1152]{1,0:T(8,128)(2,1)}, bf16[384,1152]{1,0:T(8,128)(2,1)S(1)}, u32[]{:S(2)}, u32[]{:S(2)}) %collective-permute-start.4) | collective-permute-done | bytes 884768 | tf_op jit(solution)/shard_map/fetch_expert/ppermute | solution.py:296
  273.4 2.6 fusion.44
  277.3 5.7 collective-permute-done.5
  283.8 2.3 convolution_add_fusion.5
  287.0 14.5 %collective-permute-done.6 = bf16[384,1152]{1,0:T(8,128)(2,1)S(1)} collective-permute-done((bf16[384,1152]{1,0:T(8,128)(2,1)S(1)}, bf16[384,1152]{1,0:T(8,128)(2,1)S(1)}, u32[]{:S(2)}, u32[]{:S(2)}) %collective-permute-start.6) | collective-permute-done | bytes 884768 | tf_op jit(solution)/shard_map/fetch_expert/ppermute | solution.py:296
  306.4 12.8 %convolution_add_fusion = f32[512,1152]{1,0:T(8,128)S(1)} fusion(f32[512,1152]{1,0:T(8,128)S(1)} %convolution_add_fusion.1, bf16[512,384]{1,0:T(8,128)(2,1)S(1)} %fusion.58, bf16[384,1152]{1,0:T(8,128)(2,1)S(1)} %collective-permute-done.5), kind=kOutput, calls=%fused_computation.6 | convolution fusion | flops 453574656 | bytes 5996544 | tf_op jit(solution)/shard_map/dot_general | solution.py:168
  320.8 26.1 %collective-permute-done.7 = bf16[256,2304]{1,0:T(8,128)(2,1)S(1)} collective-permute-done((bf16[256,2304]{1,0:T(8,128)(2,1)S(1)}, bf16[256,2304]{1,0:T(8,128)(2,1)S(1)}, u32[]{:S(2)}, u32[]{:S(2)}) %collective-permute-start.7) | collective-permute-done | bytes 1179680 | tf_op jit(solution)/shard_map/pair_results/ppermute | solution.py:393
  348.1 4.3 all-to-all-start.1
  352.5 15.9 %all-to-all-done.1 = bf16[4,64,2304]{2,1,0:T(8,128)(2,1)} async-done(((bf16[4,64,2304]{2,1,0:T(8,128)(2,1)}), bf16[4,64,2304]{2,1,0:T(8,128)(2,1)}, u32[]{:S(2)}, u32[]{:S(2)}) %all-to-all-start.1) | async-done | bytes 1179680 | tf_op jit(solution)/shard_map/all_to_all | solution.py:395
  375.6 3.1 multiply_reduce_fusion
  378.9 26.0 %scan_backward.1 = (f32[2,96,2304]{2,1,0:T(8,128)S(1)}, f32[2,96,2304]{2,1,0:T(8,128)S(1)}, f32[2,16,2304]{2,1,0:T(8,128)S(1)}, f32[2,96,16,128]{3,2,1,0:T(8,128)S(1)}, f32[2,96,16,128]{3,2,1,0:T(8,128)S(1)}) custom-call(f32[2,96,2304]{2,1,0:T(8,128)S(1)} %copy-done.3, f32[2,96,2304]{2,1,0:T(8,128)S(1)} %copy-done.2, f32[2,96,16,128]{3,2,1,0:T(8,128)S(1)} %copy-done.4, ...), custom_call_target="tpu_custom_call" | custom-call | flops 212336640 | bytes 15138816 | tf_op jit(solution)/shard_map/scan_backward/pallas_call | solution.py:144
  408.5 2.5 reduce_sum.226
  415.2 2.5 reduce_sum.227
  423.6 7.8 %fusion.118 = (bf16[2304]{0:T(1024)(128)(2,1)}, bf16[2304]{0:T(1024)(128)(2,1)}, bf16[2304]{0:T(1024)(128)(2,1)}, bf16[2304]{0:T(1024)(128)(2,1)}, bf16[2304]{0:...) fusion(f32[2,96,2304]{2,1,0:T(8,128)} %bitcast.157, ...), kind=kLoop, calls=%fused_computation.238 | loop fusion | flops 14144256 | bytes 17738496 | tf_op jit(solution)/shard_map/reduce_sum | solution.py:462
  433.2 6.0 convolution_convert_fusion
  440.6 4.1 convolution_convert_fusion.1
  448.8 22.6 %collective-permute-done.11 = bf16[384,1152]{1,0:T(8,128)(2,1)S(1)} collective-permute-done((bf16[384,1152]{1,0:T(8,128)(2,1)S(1)}, bf16[384,1152]{1,0:T(8,128)(2,1)S(1)}, u32[]{:S(2)}, u32[]{:S(2)}) %collective-permute-start.11) | collective-permute-done | bytes 884768 | tf_op jit(solution)/shard_map/reduce_expert/ppermute | solution.py:418
  473.4 17.1 %collective-permute-done.8 = bf16[384,1152]{1,0:T(8,128)(2,1)S(1)} collective-permute-done((bf16[384,1152]{1,0:T(8,128)(2,1)S(1)}, bf16[384,1152]{1,0:T(8,128)(2,1)S(1)}, u32[]{:S(2)}, u32[]{:S(2)}) %collective-permute-start.8) | collective-permute-done | bytes 884768 | tf_op jit(solution)/shard_map/reduce_expert/ppermute | solution.py:418
  493.5 32.3 %collective-permute-done.12 = bf16[384,1152]{1,0:T(8,128)(2,1)} collective-permute-done((bf16[384,1152]{1,0:T(8,128)(2,1)}, bf16[384,1152]{1,0:T(8,128)(2,1)}, u32[]{:S(2)}, u32[]{:S(2)}) %collective-permute-start.12) | collective-permute-done | bytes 884768 | tf_op jit(solution)/shard_map/reduce_expert/ppermute | solution.py:418
  525.8 3.1 fusion.4
  528.9 2.9 collective-permute-start.13
  531.8 25.2 %collective-permute-done.9 = bf16[384,1152]{1,0:T(8,128)(2,1)} collective-permute-done((bf16[384,1152]{1,0:T(8,128)(2,1)}, bf16[384,1152]{1,0:T(8,128)(2,1)}, u32[]{:S(2)}, u32[]{:S(2)}) %collective-permute-start.9) | collective-permute-done | bytes 884768 | tf_op jit(solution)/shard_map/reduce_expert/ppermute | solution.py:418
  557.0 2.8 fusion.2
  569.2 2.0 concatenate.64
  579.7 7.2 concatenate.59
  587.0 5.2 all-to-all-start.2
  592.6 8.0 %multiply_reduce_fusion.6 = (f32[1152]{0:T(1024)S(1)}, f32[192]{0:T(256)S(1)}, f32[192,1152]{1,0:T(8,128)}) fusion(f32[192]{0:T(256)S(1)} %copy-done.111, bf16[2,1,96,1152]{3,2,1,0:T(8,128)(2,1)S(1)} %copy-done.37, f32[1152]{0:T(1024)S(1)} %copy-done.83, bf16[4608,1152]{1,0:T(8,128)(2,1)} %all-gather.4.cloned.1.call-done, bf16[192,2304]{1,0:T(8,128)(2,1)} %bitcast.182, ...), kind=kOutput, calls=%fused_computation.97 | convolution fusion | flops 2043738880 | bytes 14166528 | tf_op jit(solution)/shard_map/dot_general | solution.py:168
  601.4 58.4 %psum.7 = f32[6,1152]{1,0:T(8,128)S(1)} all-reduce(f32[6,1152]{1,0:T(8,128)S(1)} %pad_maximum_fusion.7), channel_id=1, replica_groups=mesh['dp'=8,'expert'=4] {'dp','expert'}, use_global_device_ids=true, to_apply=%region_14.15 | all-reduce | flops 6912 | bytes 55296 | tf_op jit(solution)/shard_map/reduce_gains/psum | solution.py:500
  661.1 2.4 fusion.28
  663.4 3.6 fusion
  667.0 3.1 fusion.1
  675.3 67.3 %reduce-scatter.7.cloned.1.call-done = bf16[72,1152]{1,0:T(8,128)(2,1)} async-done(((bf16[2304,1152]{1,0:T(8,128)(2,1)}), bf16[72,1152]{1,0:T(8,128)(2,1)}) %reduce-scatter.7.cloned.1.call-update) | async-done | bytes 165904
  742.6 8.1 %all_gather.19 = bf16[288,1152]{1,0:T(8,128)(2,1)S(1)} all-gather(bf16[72,1152]{1,0:T(8,128)(2,1)} %reduce-scatter.7.cloned.1.call-done), channel_id=1, replica_groups=mesh['dp'=8,'expert'=4] {'expert'}, dimensions={0}, use_global_device_ids=true | all-gather | bytes 829440 | tf_op jit(solution)/shard_map/share_rows/all_gather | solution.py:504
  751.8 9.6 %all-gather.8.cloned.1.call-done = bf16[576,1152]{1,0:T(8,128)(2,1)} async-done(((bf16[144,1152]{1,0:T(8,128)(2,1)}), bf16[576,1152]{1,0:T(8,128)(2,1)}) %all-gather.8.cloned.1.call-update) | async-done | bytes 1327120 | tf_op jit(solution)/shard_map/share_rows/all_gather | solution.py:505
  761.5 3.0 convert_element_type.239
  (400 shorter events, 107.0 us)
Async XLA Ops:
  7.3 96.5 %all-gather.4.cloned.1.call-start = ((), (), s32[]{:S(2)}) async-start(), calls=%async_computation.5 | async-start | bytes 10948608 | tf_op jit(solution)/shard_map/fetch_in/all_gather | solution.py:274
  9.3 161.5 %all-gather.6.cloned.1.call-start = ((), (), s32[]{:S(2)}) async-start(), calls=%async_computation.6 | async-start | bytes 5474304 | tf_op jit(solution)/shard_map/fetch_out/all_gather | solution.py:290
  11.3 55.3 %copy-start.110 = (f32[192]{0:T(256)}, f32[192]{0:T(256)S(1)}, u32[]{:S(2)}) copy-start(f32[192]{0:T(256)S(1)} %rsqrt.20) | copy-start | bytes 2308
  11.3 55.3 %copy-start.82 = (f32[1152]{0:T(1024)}, f32[1152]{0:T(1024)S(1)}, u32[]{:S(2)}) copy-start(f32[1152]{0:T(1024)S(1)} %convert_element_type.205) | copy-start | bytes 13828
  12.0 50.3 %copy-start.116 = (bf16[1152]{0:T(1024)(128)(2,1)S(1)}, bf16[1152]{0:T(1024)(128)(2,1)}, u32[]{:S(2)}) copy-start(bf16[1152]{0:T(1024)(128)(2,1)} %param.32) | copy-start | bytes 6916
  12.0 50.8 %copy-start.117 = (s32[2,1,96,1]{2,3,1,0:T(1,128)S(1)}, s32[2,1,96,1]{2,3,1,0:T(1,128)}, u32[]{:S(2)}) copy-start(s32[2,1,96,1]{2,3,1,0:T(1,128)} %param.20) | copy-start | bytes 2308
  12.2 53.1 %copy-start.121 = (s32[2,1,96]{2,1,0:T(1,128)S(1)}, s32[2,1,96]{2,1,0:T(1,128)}, u32[]{:S(2)}) copy-start(s32[2,1,96]{2,1,0:T(1,128)} %param.19) | copy-start | bytes 2308
  64.4 47.0 %copy-start.52 = (f32[23,2304]{1,0:T(8,128)}, f32[23,2304]{1,0:T(8,128)S(1)}, u32[]{:S(2)}) copy-start(f32[23,2304]{1,0:T(8,128)S(1)} %slice_convert_fusion) | copy-start | bytes 635908
  65.9 46.0 %copy-start.112 = (f32[2,96]{1,0:T(2,128)}, f32[2,96]{1,0:T(2,128)S(1)}, u32[]{:S(2)}) copy-start(f32[2,96]{1,0:T(2,128)S(1)} %get-tuple-element.166) | copy-start | bytes 2308
  65.9 46.0 %copy-start.113 = (f32[2,96]{1,0:T(2,128)}, f32[2,96]{1,0:T(2,128)S(1)}, u32[]{:S(2)}) copy-start(f32[2,96]{1,0:T(2,128)S(1)} %get-tuple-element.167) | copy-start | bytes 2308
  66.8 44.7 %copy-start.34 = (bf16[192,1152]{1,0:T(8,128)(2,1)}, bf16[192,1152]{1,0:T(8,128)(2,1)S(1)}, u32[]{:S(2)}) copy-start(bf16[192,1152]{1,0:T(8,128)(2,1)S(1)} %multiply_convert_fusion.1) | copy-start | bytes 1327108
  111.8 25.6 %copy-start.19 = (f32[192,2304]{1,0:T(8,128)}, f32[192,2304]{1,0:T(8,128)S(1)}, u32[]{:S(2)}) copy-start(f32[192,2304]{1,0:T(8,128)S(1)} %get-tuple-element.156) | copy-start | bytes 5308420
  113.7 261.3 %copy-start.11 = (f32[2,96,2304]{2,1,0:T(8,128)}, f32[2,96,2304]{2,1,0:T(8,128)S(1)}, u32[]{:S(2)}) copy-start(f32[2,96,2304]{2,1,0:T(8,128)S(1)} %get-tuple-element.152) | copy-start | bytes 5308420
  175.1 197.8 %copy-start.14 = (f32[192,1152]{1,0:T(8,128)}, f32[192,1152]{1,0:T(8,128)S(1)}, u32[]{:S(2)}) copy-start(f32[192,1152]{1,0:T(8,128)S(1)} %get-tuple-element.171) | copy-start | bytes 2654212
  175.8 195.5 %copy-start.88 = (f32[192]{0:T(256)}, f32[192]{0:T(256)S(1)}, u32[]{:S(2)}) copy-start(f32[192]{0:T(256)S(1)} %get-tuple-element.172) | copy-start | bytes 2308
  175.9 195.5 %copy-start.93 = (f32[192]{0:T(256)}, f32[192]{0:T(256)S(1)}, u32[]{:S(2)}) copy-start(f32[192]{0:T(256)S(1)} %fusion.113) | copy-start | bytes 2308
  178.3 20.2 %all-to-all-start = ((bf16[4,64,2304]{2,1,0:T(8,128)(2,1)}), bf16[4,64,2304]{2,1,0:T(8,128)(2,1)}, u32[]{:S(2)}, u32[]{:S(2)}) async-start(bf16[4,64,2304]{2,1,0:T(8,128)(2,1)} %bitcast.172), calls=%async_computation | async-start | bytes 2359296 | tf_op jit(solution)/shard_map/all_to_all | solution.py:368
  182.6 24.6 %collective-permute-start.1 = (bf16[384,1152]{1,0:T(8,128)(2,1)}, bf16[384,1152]{1,0:T(8,128)(2,1)}, u32[]{:S(2)}, u32[]{:S(2)}) collective-permute-start(bf16[384,1152]{1,0:T(8,128)(2,1)} %bitcast.191), channel_id=1, source_target_pairs={{0,8},{4,12},{8,16},{12,20},{16,24},{20,28},{24,0},{28,4},{1,9},{5... | collective-permute-start | bytes 2654216 | tf_op jit(solution)/shard_map/fetch_expert/ppermute | solution.py:295
  184.6 41.6 %collective-permute-start.2 = (bf16[384,1152]{1,0:T(8,128)(2,1)}, bf16[384,1152]{1,0:T(8,128)(2,1)}, u32[]{:S(2)}, u32[]{:S(2)}) collective-permute-start(bf16[384,1152]{1,0:T(8,128)(2,1)} %bitcast.192), channel_id=1, source_target_pairs={{0,8},{4,12},{8,16},{12,20},{16,24},{20,28},{24,0},{28,4},{1,9},{5... | collective-permute-start | bytes 2654216 | tf_op jit(solution)/shard_map/fetch_expert/ppermute | solution.py:296
  198.5 67.3 %copy-start.54 = (bf16[1,384,1152]{2,1,0:T(8,128)(2,1)S(1)}, bf16[1,384,1152]{2,1,0:T(8,128)(2,1)}, u32[]{:S(2)}) copy-start(bf16[1,384,1152]{2,1,0:T(8,128)(2,1)} %param.34) | copy-start | bytes 2654212
  198.6 65.8 %collective-permute-start = (bf16[256,2304]{1,0:T(8,128)(2,1)}, bf16[256,2304]{1,0:T(8,128)(2,1)S(1)}, u32[]{:S(2)}, u32[]{:S(2)}) collective-permute-start(bf16[256,2304]{1,0:T(8,128)(2,1)} %bitcast.25), channel_id=1, source_target_pairs={{0,4},{4,0},{8,12},{12,8},{16,20},{20,16},{24,28},{28,24},{1,5},{5... | collective-permute-start | bytes 3538952 | tf_op jit(solution)/shard_map/pair_rows/ppermute | solution.py:372
  207.2 37.8 %collective-permute-start.3 = (bf16[384,1152]{1,0:T(8,128)(2,1)}, bf16[384,1152]{1,0:T(8,128)(2,1)S(1)}, u32[]{:S(2)}, u32[]{:S(2)}) collective-permute-start(bf16[384,1152]{1,0:T(8,128)(2,1)} %collective-permute-done.1), channel_id=1, source_target_pairs={{0,8},{4,12},{8,16},{12,20},{16,24},{20,28},{24,0},{28,4},{1,9},{5... | collective-permute-start | bytes 2654216 | tf_op jit(solution)/shard_map/fetch_expert/ppermute | solution.py:295
  226.2 37.8 %collective-permute-start.4 = (bf16[384,1152]{1,0:T(8,128)(2,1)}, bf16[384,1152]{1,0:T(8,128)(2,1)S(1)}, u32[]{:S(2)}, u32[]{:S(2)}) collective-permute-start(bf16[384,1152]{1,0:T(8,128)(2,1)} %collective-permute-done.2), channel_id=1, source_target_pairs={{0,8},{4,12},{8,16},{12,20},{16,24},{20,28},{24,0},{28,4},{1,9},{5... | collective-permute-start | bytes 2654216 | tf_op jit(solution)/shard_map/fetch_expert/ppermute | solution.py:296
  245.1 37.9 %collective-permute-start.5 = (bf16[384,1152]{1,0:T(8,128)(2,1)S(1)}, bf16[384,1152]{1,0:T(8,128)(2,1)S(1)}, u32[]{:S(2)}, u32[]{:S(2)}) collective-permute-start(bf16[384,1152]{1,0:T(8,128)(2,1)S(1)} %collective-permute-done.3), channel_id=1, source_target_pairs={{0,8},{4,12},{8,16},{12,20},{16,24},{20,28},{24,0},{28,4},{1,9},{5... | collective-permute-start | bytes 2654216 | tf_op jit(solution)/shard_map/fetch_expert/ppermute | solution.py:295
  264.0 37.4 %collective-permute-start.6 = (bf16[384,1152]{1,0:T(8,128)(2,1)S(1)}, bf16[384,1152]{1,0:T(8,128)(2,1)S(1)}, u32[]{:S(2)}, u32[]{:S(2)}) collective-permute-start(bf16[384,1152]{1,0:T(8,128)(2,1)S(1)} %collective-permute-done.4), channel_id=1, source_target_pairs={{0,8},{4,12},{8,16},{12,20},{16,24},{20,28},{24,0},{28,4},{1,9},{5... | collective-permute-start | bytes 2654216 | tf_op jit(solution)/shard_map/fetch_expert/ppermute | solution.py:296
  265.8 35.6 %copy-start.27 = (bf16[512,1152]{1,0:T(8,128)(2,1)}, bf16[512,1152]{1,0:T(8,128)(2,1)S(1)}, u32[]{:S(2)}) copy-start(bf16[512,1152]{1,0:T(8,128)(2,1)S(1)} %get-tuple-element.158) | copy-start | bytes 3538948
  276.0 27.5 %copy-start.66 = (bf16[512,384]{1,0:T(8,128)(2,1)}, bf16[512,384]{1,0:T(8,128)(2,1)S(1)}, u32[]{:S(2)}) copy-start(bf16[512,384]{1,0:T(8,128)(2,1)S(1)} %fusion.44) | copy-start | bytes 1179652
  277.2 28.3 %copy-start.64 = (bf16[512,384]{1,0:T(8,128)(2,1)}, bf16[512,384]{1,0:T(8,128)(2,1)S(1)}, u32[]{:S(2)}) copy-start(bf16[512,384]{1,0:T(8,128)(2,1)S(1)} %fusion.51) | copy-start | bytes 1179652
  319.3 27.6 %collective-permute-start.7 = (bf16[256,2304]{1,0:T(8,128)(2,1)S(1)}, bf16[256,2304]{1,0:T(8,128)(2,1)S(1)}, u32[]{:S(2)}, u32[]{:S(2)}) collective-permute-start(bf16[256,2304]{1,0:T(8,128)(2,1)S(1)} %fusion.9), channel_id=1, source_target_pairs={{0,4},{4,0},{8,12},{12,8},{16,20},{20,16},{24,28},{28,24},{1,5},{5... | collective-permute-start | bytes 3538952 | tf_op jit(solution)/shard_map/pair_results/ppermute | solution.py:393
  348.1 20.2 %all-to-all-start.1 = ((bf16[4,64,2304]{2,1,0:T(8,128)(2,1)}), bf16[4,64,2304]{2,1,0:T(8,128)(2,1)}, u32[]{:S(2)}, u32[]{:S(2)}) async-start(bf16[4,64,2304]{2,1,0:T(8,128)(2,1)} %bitcast.170), calls=%async_computation.1 | async-start | bytes 2359296 | tf_op jit(solution)/shard_map/all_to_all | solution.py:395
  352.4 308.0 %reduce-scatter.5.cloned.1.call-start = ((), (), s32[]{:S(2)}) async-start(), calls=%async_computation.7 | async-start | bytes 10948608 | tf_op jit(solution)/shard_map/reduce_in/reduce_scatter | solution.py:472
  378.8 26.0 %copy-start.12 = (f32[2,96,2304]{2,1,0:T(8,128)S(1)}, f32[2,96,2304]{2,1,0:T(8,128)}, u32[]{:S(2)}) copy-start(f32[2,96,2304]{2,1,0:T(8,128)} %copy-done.11) | copy-start | bytes 5308420
  378.8 26.0 %copy-start.17 = (f32[192,2304]{1,0:T(8,128)S(1)}, f32[192,2304]{1,0:T(8,128)}, u32[]{:S(2)}) copy-start(f32[192,2304]{1,0:T(8,128)} %copy-done.16) | copy-start | bytes 5308420
  378.9 26.0 %copy-start.70 = (f32[2304]{0:T(1024)S(1)}, f32[2304]{0:T(1024)}, u32[]{:S(2)}) copy-start(f32[2304]{0:T(1024)} %get-tuple-element.132) | copy-start | bytes 27652
  439.2 303.4 %reduce-scatter.7.cloned.1.call-start = ((), (), s32[]{:S(2)}) async-start(), calls=%async_computation.9 | async-start | bytes 5474304
  447.1 24.4 %collective-permute-start.11 = (bf16[384,1152]{1,0:T(8,128)(2,1)S(1)}, bf16[384,1152]{1,0:T(8,128)(2,1)S(1)}, u32[]{:S(2)}, u32[]{:S(2)}) collective-permute-start(bf16[384,1152]{1,0:T(8,128)(2,1)S(1)} %convolution_convert_fusion.3), channel_id=1, source_target_pairs={{0,8},{4,12},{8,16},{12,20},{16,24},{20,28},{24,0},{28,4},{1,9},{5... | collective-permute-start | bytes 2654216 | tf_op jit(solution)/shard_map/reduce_expert/ppermute | solution.py:418
  448.4 42.0 %copy-start.65 = (bf16[512,384]{1,0:T(8,128)(2,1)S(1)}, bf16[512,384]{1,0:T(8,128)(2,1)}, u32[]{:S(2)}) copy-start(bf16[512,384]{1,0:T(8,128)(2,1)} %copy-done.64) | copy-start | bytes 1179652
  448.4 42.0 %collective-permute-start.8 = (bf16[384,1152]{1,0:T(8,128)(2,1)S(1)}, bf16[384,1152]{1,0:T(8,128)(2,1)S(1)}, u32[]{:S(2)}, u32[]{:S(2)}) collective-permute-start(bf16[384,1152]{1,0:T(8,128)(2,1)S(1)} %convolution_convert_fusion.4), channel_id=1, source_target_pairs={{0,8},{4,12},{8,16},{12,20},{16,24},{20,28},{24,0},{28,4},{1,9},{5... | collective-permute-start | bytes 2654216 | tf_op jit(solution)/shard_map/reduce_expert/ppermute | solution.py:418
  473.1 52.6 %collective-permute-start.12 = (bf16[384,1152]{1,0:T(8,128)(2,1)}, bf16[384,1152]{1,0:T(8,128)(2,1)}, u32[]{:S(2)}, u32[]{:S(2)}) collective-permute-start(bf16[384,1152]{1,0:T(8,128)(2,1)} %fusion.5), channel_id=1, source_target_pairs={{0,8},{4,12},{8,16},{12,20},{16,24},{20,28},{24,0},{28,4},{1,9},{5... | collective-permute-start | bytes 2654216 | tf_op jit(solution)/shard_map/reduce_expert/ppermute | solution.py:418
  492.1 64.9 %collective-permute-start.9 = (bf16[384,1152]{1,0:T(8,128)(2,1)}, bf16[384,1152]{1,0:T(8,128)(2,1)}, u32[]{:S(2)}, u32[]{:S(2)}) collective-permute-start(bf16[384,1152]{1,0:T(8,128)(2,1)} %fusion.3), channel_id=1, source_target_pairs={{0,8},{4,12},{8,16},{12,20},{16,24},{20,28},{24,0},{28,4},{1,9},{5... | collective-permute-start | bytes 2654216 | tf_op jit(solution)/shard_map/reduce_expert/ppermute | solution.py:418
  493.5 63.5 %copy-start.33 = (bf16[512,1152]{1,0:T(8,128)(2,1)S(1)}, bf16[512,1152]{1,0:T(8,128)(2,1)}, u32[]{:S(2)}) copy-start(bf16[512,1152]{1,0:T(8,128)(2,1)} %copy-done.31) | copy-start | bytes 3538948
  493.5 63.5 %copy-start.63 = (bf16[512,384]{1,0:T(8,128)(2,1)S(1)}, bf16[512,384]{1,0:T(8,128)(2,1)}, u32[]{:S(2)}) copy-start(bf16[512,384]{1,0:T(8,128)(2,1)} %copy-done.62) | copy-start | bytes 1179652
  528.9 30.9 %copy-start.24 = (bf16[2,96,2304]{2,1,0:T(8,128)(2,1)S(1)}, bf16[2,96,2304]{2,1,0:T(8,128)(2,1)}, u32[]{:S(2)}) copy-start(bf16[2,96,2304]{2,1,0:T(8,128)(2,1)} %copy-done.23) | copy-start | bytes 2654212
  528.9 138.1 %collective-permute-start.13 = (bf16[384,1152]{1,0:T(8,128)(2,1)}, bf16[384,1152]{1,0:T(8,128)(2,1)}, u32[]{:S(2)}, u32[]{:S(2)}) collective-permute-start(bf16[384,1152]{1,0:T(8,128)(2,1)} %fusion.4), channel_id=1, source_target_pairs={{0,8},{4,12},{8,16},{12,20},{16,24},{20,28},{24,0},{28,4},{1,9},{5... | collective-permute-start | bytes 2654216 | tf_op jit(solution)/shard_map/reduce_expert/ppermute | solution.py:418
  559.8 103.6 %collective-permute-start.10 = (bf16[384,1152]{1,0:T(8,128)(2,1)}, bf16[384,1152]{1,0:T(8,128)(2,1)}, u32[]{:S(2)}, u32[]{:S(2)}) collective-permute-start(bf16[384,1152]{1,0:T(8,128)(2,1)} %fusion.2), channel_id=1, source_target_pairs={{0,8},{4,12},{8,16},{12,20},{16,24},{20,28},{24,0},{28,4},{1,9},{5... | collective-permute-start | bytes 2654216 | tf_op jit(solution)/shard_map/reduce_expert/ppermute | solution.py:418
  587.0 83.2 %all-to-all-start.2 = ((bf16[32,72,199]{2,1,0:T(8,128)(2,1)}), bf16[32,72,199]{2,1,0:T(8,128)(2,1)}, u32[]{:S(2)}, u32[]{:S(2)}) async-start(bf16[32,72,199]{2,1,0:T(8,128)(2,1)} %concatenate.59), calls=%async_computation.3 | async-start | bytes 2359296 | tf_op jit(solution)/shard_map/reduce_small/all_to_all | solution.py:485
  592.3 68.1 %copy-start.109 = (f32[192]{0:T(256)S(1)}, f32[192]{0:T(256)}, u32[]{:S(2)}) copy-start(f32[192]{0:T(256)} %copy-done.108) | copy-start | bytes 2308
  592.3 169.2 %all-gather.8.cloned.1.call-start = ((), (), s32[]{:S(2)}) async-start(), calls=%async_computation.8 | async-start | bytes 1658880 | tf_op jit(solution)/shard_map/share_rows/all_gather | solution.py:505
  (101 other events, 469.8 us)
Sparse Core Ops, SparseCore 0:
  11.6 92.1 all-gather.3
  106.7 64.0 all-gather.5
  439.3 196.3 reduce-scatter.4
  641.3 101.2 reduce-scatter.6
  744.0 17.4 all-gather.7

commit v2 on v1

v2 whole, which is shorter than its diff:
```python
import jax
import jax.numpy as jnp
from jax import lax
from jax.experimental import pallas as pl
from jax.experimental.pallas import tpu as pltpu
from jax.sharding import PartitionSpec as P

LANES = 128
VMEM_GRANT = 60 << 20
ROWS = 8

def wide(tile, width):
    return jnp.concatenate([tile] * (width // LANES), axis=1)

def narrow(values):
    total = values[:, :LANES]
    for start in range(LANES, values.shape[1], LANES):
        total = total + values[:, start : start + LANES]
    return total

def fold_states(pieces, position):
    folded = []
    for piece in pieces:
        total = piece[:ROWS]
        for start in range(ROWS, piece.shape[0], ROWS):
            total = total + piece[start : start + ROWS]
        folded.append(total)
    low = (position & 4) == 0
    folded = [
        jnp.where(low, a, b) + pltpu.roll(jnp.where(low, b, a), 4, 0)
        for a, b in zip(folded[:4], folded[4:])
    ]
    for step in (2, 1):
        low = (position & step) == 0
        half = len(folded) // 2
        folded = [
            jnp.where(low, a + pltpu.roll(a, ROWS - step, 0), b + pltpu.roll(b, step, 0))
            for a, b in zip(folded[:half], folded[half:])
        ]
    return folded[0]

def scan_forward(decay_ref, drive_ref, b_ref, c_ref, rate_ref, out_ref):
    length, width = decay_ref.shape[1:]
    rate = rate_ref[...]
    position = lax.broadcasted_iota(jnp.int32, (ROWS, width), 0)

    def block(index, state):
        start = pl.multiple_of(index * ROWS, ROWS)
        pieces = []
        for offset in range(ROWS):
            t = start + offset
            factor = jnp.exp2(decay_ref[0, pl.ds(t, 1), :] * rate)
            state = factor * state + drive_ref[0, pl.ds(t, 1), :] * wide(b_ref[0, t], width)
            pieces.append(state * wide(c_ref[0, t], width))
        out_ref[0, pl.ds(start, ROWS), :] = fold_states(pieces, position)
        return state

    lax.fori_loop(0, length // ROWS, block, jnp.zeros_like(rate))

def scan_backward(
    decay_ref, drive_ref, b_ref, c_ref, rate_ref, dout_ref,
    ddrive_ref, ddecay_ref, drate_ref, db_sum_ref, dc_sum_ref,
    db_ref, dc_ref, state_ref, factor_ref,
):
    length, width = decay_ref.shape[1:]
    rate = rate_ref[...]
    position = lax.broadcasted_iota(jnp.int32, (ROWS, width), 0)

    @pl.when(pl.program_id(1) == 0)
    def _():
        db_ref[...] = jnp.zeros_like(db_ref)
        dc_ref[...] = jnp.zeros_like(dc_ref)

    state_ref[0] = jnp.zeros_like(rate)

    def replay(index, state):
        start = pl.multiple_of(index * ROWS, ROWS)
        for offset in range(ROWS):
            t = start + offset
            factor = jnp.exp2(decay_ref[0, pl.ds(t, 1), :] * rate)
            state = factor * state + drive_ref[0, pl.ds(t, 1), :] * wide(b_ref[0, t], width)
            factor_ref[t] = factor
            state_ref[t + 1] = state
        return state

    lax.fori_loop(0, length // ROWS, replay, jnp.zeros_like(rate))

    def block(index, carried):
        later, drate = carried
        start = pl.multiple_of(length - ROWS - index * ROWS, ROWS)
        drive_pieces = [None] * ROWS
        decay_pieces = [None] * ROWS
        for offset in reversed(range(ROWS)):
            t = start + offset
            dout = dout_ref[0, pl.ds(t, 1), :]
            dstate = later + dout * wide(c_ref[0, t], width)
            dc_ref[t] += narrow(dout * state_ref[t + 1])
            db_ref[t] += narrow(dstate * drive_ref[0, pl.ds(t, 1), :])
            drive_pieces[offset] = dstate * wide(b_ref[0, t], width)
            later = dstate * factor_ref[t]
            power = later * state_ref[t]
            decay_pieces[offset] = power * rate
            drate = drate + power * decay_ref[0, pl.ds(t, 1), :]
        ddrive_ref[0, pl.ds(start, ROWS), :] = fold_states(drive_pieces, position)
        ddecay_ref[0, pl.ds(start, ROWS), :] = fold_states(decay_pieces, position)
        return later, drate

    zero = jnp.zeros_like(rate)
    drate_ref[0] = lax.fori_loop(0, length // ROWS, block, (zero, zero))[1]

    @pl.when(pl.program_id(1) == pl.num_programs(1) - 1)
    def _():
        ones = jnp.ones((ROWS, LANES), jnp.float32)
        for total_ref, sum_ref in ((db_ref, db_sum_ref), (dc_ref, dc_sum_ref)):
            sum_ref[0] = lax.dot_general(
                ones,
                total_ref[...].reshape(-1, LANES),
                (((1,), (1,)), ((), ())),
                precision=lax.Precision.HIGHEST,
                preferred_element_type=jnp.float32,
            )

def tile_width(width):
    for tiles in (3, 2, 1):
        if width % (tiles * LANES) == 0:
            return tiles * LANES
    return width

def scan_specs(length, states, width):
    tokens = pl.BlockSpec((1, length, width), lambda s, c: (s, 0, c))
    maps = pl.BlockSpec((1, length, states, LANES), lambda s, c: (s, 0, 0, 0))
    rates = pl.BlockSpec((states, width), lambda s, c: (0, c))
    return tokens, maps, rates

def run_forward(decay, drive, b_wide, c_wide, rate):
    count, length, channels = decay.shape
    states = rate.shape[0]
    width = tile_width(channels)
    tokens, maps, rates = scan_specs(length, states, width)
    return pl.pallas_call(
        scan_forward,
        grid=(count, channels // width),
        in_specs=[tokens, tokens, maps, maps, rates],
        out_specs=tokens,
        out_shape=jax.ShapeDtypeStruct(decay.shape, jnp.float32),
        cost_estimate=pl.CostEstimate(
            flops=decay.size, transcendentals=0,
            bytes_accessed=4 * (3 * decay.size + 2 * b_wide.size)),
        compiler_params=pltpu.CompilerParams(vmem_limit_bytes=VMEM_GRANT),
        name="scan_forward",
    )(decay, drive, b_wide, c_wide, rate)

def run_backward(decay, drive, b_wide, c_wide, rate, dout):
    count, length, channels = decay.shape
    states = rate.shape[0]
    width = tile_width(channels)
    tokens, maps, rates = scan_specs(length, states, width)
    full = jax.ShapeDtypeStruct(decay.shape, jnp.float32)
    summed = jax.ShapeDtypeStruct((count, ROWS, length * states), jnp.float32)
    sums = pl.BlockSpec((1, ROWS, length * states), lambda s, c: (s, 0, 0))
    return pl.pallas_call(
        scan_backward,
        grid=(count, channels // width),
        in_specs=[tokens, tokens, maps, maps, rates, tokens],
        out_specs=[tokens, tokens, pl.BlockSpec((1, states, width), lambda s, c: (s, 0, c)), sums, sums],
        out_shape=[full, full, jax.ShapeDtypeStruct((count, states, channels), jnp.float32),
            summed, summed],
        scratch_shapes=[pltpu.VMEM((length, states, LANES), jnp.float32), pltpu.VMEM((length, states, LANES), jnp.float32),
            pltpu.VMEM((length + 1, states, width), jnp.float32), pltpu.VMEM((length, states, width), jnp.float32)],
        cost_estimate=pl.CostEstimate(
            flops=decay.size, transcendentals=0,
            bytes_accessed=4 * (5 * decay.size + 4 * b_wide.size)),
        compiler_params=pltpu.CompilerParams(vmem_limit_bytes=VMEM_GRANT),
        name="scan_backward",
    )(decay, drive, b_wide, c_wide, rate, dout)


def product(left, right, contract):
    return lax.dot_general(left, right, (contract, ((), ())), preferred_element_type=jnp.float32)


def gate_backward(
    d_branch_ref, normed_ref, out_ref, mixed_low_ref, mixed_ref, gate_ref,
    term_ref, d_gate_ref, d_scanned_ref,
):
    model = d_branch_ref.shape[1]
    d_branch = d_branch_ref[...]
    d_mixed = product(d_branch, out_ref[...], ((1,), (1,)))
    gate = gate_ref[...]
    chance = jax.nn.sigmoid(gate)
    d_gate = d_mixed * mixed_ref[...] * (chance * (1.0 + gate * (1.0 - chance)))
    d_gate = d_gate.astype(jnp.bfloat16)
    d_gate_ref[...] = d_gate
    d_scanned_ref[...] = d_mixed * gate * chance
    term_ref[:, :model] = product(mixed_low_ref[...], d_branch, ((0,), (0,))).astype(jnp.bfloat16)
    term_ref[:, model:] = product(d_gate, normed_ref[...], ((0,), (0,))).astype(jnp.bfloat16)


def run_gate_backward(d_branch, normed, out_rows, mixed_low, mixed, gate):
    count, model = d_branch.shape
    channels = mixed.shape[1]
    width = tile_width(channels)
    whole = pl.BlockSpec((count, model), lambda c: (0, 0))
    rows = pl.BlockSpec((width, model), lambda c: (c, 0))
    tokens = pl.BlockSpec((count, width), lambda c: (0, c))
    return pl.pallas_call(
        gate_backward,
        grid=(channels // width,),
        in_specs=[whole, whole, rows, tokens, tokens, tokens],
        out_specs=[pl.BlockSpec((width, 2 * model), lambda c: (c, 0)), tokens, tokens],
        out_shape=[
            jax.ShapeDtypeStruct((channels, 2 * model), jnp.bfloat16),
            jax.ShapeDtypeStruct((count, channels), jnp.bfloat16),
            jax.ShapeDtypeStruct((count, channels), jnp.float32),
        ],
        cost_estimate=pl.CostEstimate(flops=count, transcendentals=0, bytes_accessed=count),
        compiler_params=pltpu.CompilerParams(vmem_limit_bytes=VMEM_GRANT),
        name="gate_backward",
    )(d_branch, normed, out_rows, mixed_low, mixed, gate)


def conv_backward(
    d_drive_ref, delta_ref, d_scanned_ref, inner_ref, d_gate_ref, d_proj_ref, normed_ref,
    masks_ref, conv_ref, xproj_ref, in_ref, d_dt_ref, dt_ref, rows_ref,
    term_ref, d_normed_ref, small_ref,
):
    taps = masks_ref.shape[1]
    model = normed_ref.shape[1]
    count = inner_ref.shape[0]
    d_conv = (
        d_drive_ref[...] * delta_ref[...]
        + d_scanned_ref[...] * conv_ref[taps + 1 : taps + 2]
        + product(d_proj_ref[...], xproj_ref[...], ((1,), (1,)))
    )
    inner = inner_ref[...]
    shifted = [inner] + [pltpu.roll(inner, offset, 0) for offset in range(1, taps)]
    masked = [shifted[offset] * masks_ref[:, offset : offset + 1] for offset in range(taps)]
    total = conv_ref[taps : taps + 1]
    for offset in range(taps):
        total = total + conv_ref[taps - 1 - offset : taps - offset] * masked[offset]
    chance = jax.nn.sigmoid(total)
    d_sum = d_conv * (chance * (1.0 + total * (1.0 - chance)))
    d_inner = jnp.zeros_like(inner)
    rows = []
    for offset in range(taps):
        rows.append(jnp.sum(d_sum * masked[offset], axis=0, keepdims=True))
        back = d_sum * masks_ref[:, offset : offset + 1]
        if offset:
            back = pltpu.roll(back, count - offset, 0)
        d_inner = d_inner + conv_ref[taps - 1 - offset : taps - offset] * back
    rows = rows[::-1] + [jnp.sum(d_sum, axis=0, keepdims=True)]
    rows = jnp.concatenate(
        rows + [jnp.zeros_like(rows[0])] * (ROWS - len(rows)) + [rows_ref[...]], axis=0
    ).astype(jnp.bfloat16)
    extent = rows.shape[0]
    same = lax.broadcasted_iota(jnp.int32, (extent, extent), 0) == lax.broadcasted_iota(
        jnp.int32, (extent, extent), 1
    )
    columns = product(rows, same.astype(jnp.bfloat16), ((0,), (0,)))
    conv_low = (total * chance).astype(jnp.bfloat16)
    edge = d_proj_ref.shape[1]
    middle = edge + dt_ref.shape[1]
    small_ref[:, :edge] = product(conv_low, d_proj_ref[...], ((0,), (0,))).astype(jnp.bfloat16)
    small_ref[:, edge:middle] = product(d_dt_ref[...], dt_ref[...], ((0,), (0,))).astype(
        jnp.bfloat16
    )
    small_ref[:, middle:] = columns.astype(jnp.bfloat16)
    d_inner = d_inner.astype(jnp.bfloat16)
    term_ref[...] = product(d_inner, normed_ref[...], ((0,), (0,))).astype(jnp.bfloat16)
    d_normed = product(d_inner, in_ref[:, :model], ((1,), (0,))) + product(
        d_gate_ref[...], in_ref[:, model:], ((1,), (0,))
    )

    @pl.when(pl.program_id(0) == 0)
    def _():
        d_normed_ref[...] = d_normed

    @pl.when(pl.program_id(0) > 0)
    def _():
        d_normed_ref[...] += d_normed


def run_conv_backward(
    d_drive,
    delta,
    d_scanned,
    inner,
    d_gate,
    d_proj,
    normed,
    masks,
    conv_rows,
    xproj,
    in_rows,
    d_dt,
    dt,
    more_rows,
):
    count, channels = inner.shape
    model = normed.shape[1]
    width = tile_width(channels)
    tokens = pl.BlockSpec((count, width), lambda c: (0, c))
    small_width = d_proj.shape[1] + dt.shape[1] + ROWS + more_rows.shape[0]

    def whole(values):
        return pl.BlockSpec(values.shape, lambda c: (0, 0))

    def rows(values):
        return pl.BlockSpec((width, values.shape[1]), lambda c: (c, 0))

    return pl.pallas_call(
        conv_backward,
        grid=(channels // width,),
        in_specs=[
            tokens,
            tokens,
            tokens,
            tokens,
            tokens,
            whole(d_proj),
            whole(normed),
            whole(masks),
            pl.BlockSpec((ROWS, width), lambda c: (0, c)),
            rows(xproj),
            rows(in_rows),
            tokens,
            whole(dt),
            pl.BlockSpec((more_rows.shape[0], width), lambda c: (0, c)),
        ],
        out_specs=[
            pl.BlockSpec((width, model), lambda c: (c, 0)),
            pl.BlockSpec((count, model), lambda c: (0, 0)),
            pl.BlockSpec((width, small_width), lambda c: (c, 0)),
        ],
        out_shape=[
            jax.ShapeDtypeStruct((channels, model), jnp.bfloat16),
            jax.ShapeDtypeStruct((count, model), jnp.float32),
            jax.ShapeDtypeStruct((channels, small_width), jnp.bfloat16),
        ],
        cost_estimate=pl.CostEstimate(flops=count, transcendentals=0, bytes_accessed=count),
        compiler_params=pltpu.CompilerParams(vmem_limit_bytes=VMEM_GRANT),
        name="conv_backward",
    )(
        d_drive,
        delta,
        d_scanned,
        inner,
        d_gate,
        d_proj,
        normed,
        masks,
        conv_rows,
        xproj,
        in_rows,
        d_dt,
        dt,
        more_rows,
    )


HIGHEST = lax.Precision.HIGHEST
EPSILON = 1e-05
LOG2E = 1.4426950408889634
FAR = 1e30
LOW = jnp.bfloat16
BOTH = ("dp", "expert")


def dot(left, right, contract):
    return lax.dot_general(left, right, (contract, ((), ())), preferred_element_type=jnp.float32)


def rms_scale(values, gain_row):
    return (
        values * lax.rsqrt(jnp.mean(values * values, axis=-1, keepdims=True) + EPSILON) * gain_row
    )


def gelu_tanh(values):
    return jax.nn.gelu(values, approximate=True)


def norm_route(residual, gain_two, router_full, chosen_rows):
    normed_two = rms_scale(residual, gain_two)
    logits = jnp.dot(normed_two, router_full, precision=HIGHEST, preferred_element_type=jnp.float32)
    probabilities = jax.nn.softmax(logits, axis=-1)
    return (normed_two, jnp.sum(probabilities * chosen_rows, axis=1))


def later_rows(values, offset):
    if offset == 0:
        return values
    return jnp.pad(values, ((0, 0), (offset, 0), (0, 0)))[:, : values.shape[1]]


def same_document(segments, offset):
    if offset == 0:
        return jnp.ones(segments.shape, jnp.float32)
    padded = jnp.pad(segments, ((0, 0), (offset, 0)), constant_values=-1)
    return (padded[:, : segments.shape[1]] == segments).astype(jnp.float32)


def conv_sum(inner, taps, bias_row, masks):
    count = taps.shape[0]
    total = bias_row
    for offset in range(count):
        total = total + taps[count - 1 - offset] * later_rows(inner, offset) * masks[offset]
    return total


def dispatch_matrices(order_rows, expert_count, capacity, padded_capacity):
    length = order_rows.shape[1]
    chosen = (
        order_rows[:, :, None] == jnp.arange(expert_count, dtype=jnp.int32)[None, None]
    ).astype(jnp.float32)
    before = jnp.tril(jnp.ones((length, length), jnp.float32), -1)
    earlier = jnp.einsum("tu,sue->ste", before, chosen, preferred_element_type=jnp.float32)
    slot = jnp.sum(earlier * chosen, axis=2).astype(jnp.int32)
    places = jnp.arange(padded_capacity, dtype=jnp.int32)
    taken = ((slot[:, :, None] == places) & (places < capacity)).astype(jnp.float32)
    return [(chosen[:, :, k, None] * taken).astype(LOW) for k in range(expert_count)]


def hop(values, step):
    axis_name, distance = step
    size = lax.axis_size(axis_name)
    return lax.ppermute(values, axis_name, [(i, i ^ distance) for i in range(size)])


class Ring:
    def __init__(self, axis_name, stride, size):
        self.axis_name = axis_name
        self.stride = stride
        self.size = size
        self.place = lax.axis_index(axis_name) // stride % size

    def hop(self, values, distance=1):
        pairs = []
        for i in range(lax.axis_size(self.axis_name)):
            place = i // self.stride % self.size
            pairs.append((i, i + ((place + distance) % self.size - place) * self.stride))
        return lax.ppermute(values, self.axis_name, pairs)


def mesh_rings():
    dp_size, expert_size = lax.axis_size("dp"), lax.axis_size("expert")
    return [
        Ring("dp", 2, dp_size // 2),
        Ring("dp", 1, 2),
        Ring("expert", 2, expert_size // 2),
        Ring("expert", 1, 2),
    ]


def cubes():
    expert_size = lax.axis_size("expert")
    wide = 2 * expert_size
    return [
        [place * wide + i for i in range(wide)] for place in range(lax.axis_size("dp") // 2)
    ]


def far_gather(block):
    ring = mesh_rings()[0]
    blocks = [block[None]]
    for _ in range(ring.size - 1):
        blocks.append((yield ring.hop(blocks[-1])))
    line = jnp.concatenate(blocks[::-1] + blocks[:0:-1], axis=0)
    return lax.dynamic_slice_in_dim(line, ring.size - 1 - ring.place, ring.size, axis=0)


def cube_gather(block):
    return lax.all_gather(block, BOTH, axis=0, tiled=True, axis_index_groups=cubes())


def cube_scatter(total):
    return lax.psum_scatter(
        total, BOTH, scatter_dimension=0, tiled=True, axis_index_groups=cubes()
    )


def block_of(values, place, axis):
    return lax.dynamic_index_in_dim(values, place, axis, keepdims=True)


def far_and_pair(block):
    pair = mesh_rings()[1]
    blocks = yield from far_gather(block)
    blocks = blocks.reshape((-1, 2) + block.shape)
    moved = yield pair.hop(block_of(blocks, 1 - pair.place, 1))
    kept = block_of(blocks, pair.place, 1)
    return jnp.where(
        pair.place == 0,
        jnp.concatenate([kept, moved], axis=1),
        jnp.concatenate([moved, kept], axis=1),
    )


def far_and_pair_sum(blocks):
    pair = mesh_rings()[1]
    moved = yield pair.hop(block_of(blocks, 1 - pair.place, 1))
    kept = block_of(blocks, pair.place, 1)
    values = jnp.where(
        pair.place == 0,
        jnp.concatenate([kept, moved], axis=1),
        jnp.concatenate([moved, kept], axis=1),
    )
    values = values.reshape((-1,) + blocks.shape[2:])
    return (yield from far_sum(values))


def cube_stages_gather(block):
    for ring in mesh_rings()[:0:-1]:
        blocks = [block[None]]
        for _ in range(ring.size - 1):
            blocks.append((yield ring.hop(blocks[-1])))
        line = jnp.concatenate(blocks[::-1] + blocks[:0:-1], axis=0)
        block = lax.dynamic_slice_in_dim(line, ring.size - 1 - ring.place, ring.size, axis=0)
        block = block.reshape((-1,) + block.shape[2:])
    return block


def small_gather(block):
    cube = yield from cube_stages_gather(block)
    places = yield from far_gather(cube)
    width = block.shape[1]
    places = places.reshape(-1, 2, 2, lax.axis_size("expert"), block.shape[0], width)
    return places.transpose(1, 3, 0, 2, 4, 5).reshape(-1, width)


def add_low(kept, moved):
    return (kept.astype(jnp.float32) + moved.astype(jnp.float32)).astype(LOW)


def far_sum(blocks):
    ring = mesh_rings()[0]
    moved = yield tuple(
        ring.hop(block_of(blocks, (ring.place + distance) % ring.size, 0)[0], distance)
        for distance in range(1, ring.size)
    )
    total = block_of(blocks, ring.place, 0)[0].astype(jnp.float32)
    for part in moved:
        total = total + part.astype(jnp.float32)
    return total.astype(LOW)


def ring_sum(blocks):
    ring = mesh_rings()[0]
    count = len(blocks)
    travelling = blocks[1 % count]
    for step in range(2, count + 1):
        moved = yield ring.hop(travelling.astype(LOW))
        travelling = blocks[step % count].astype(jnp.float32) + moved.astype(jnp.float32)
    return travelling


def butterfly(values):
    for axis_name in ("expert", "dp"):
        distance = 1
        while distance < lax.axis_size(axis_name):
            values = values + (yield hop(values, (axis_name, distance)))
            distance *= 2
    return values


def shared_rows(values):
    rings = mesh_rings()
    gathered = values
    for ring in rings[2:]:
        blocks = [gathered[None]]
        for _ in range(ring.size - 1):
            blocks.append((yield ring.hop(blocks[-1])))
        line = jnp.concatenate(blocks[::-1] + blocks[:0:-1], axis=0)
        gathered = lax.dynamic_slice_in_dim(line, ring.size - 1 - ring.place, ring.size, axis=0)
    parts, rows, width = values.shape
    return gathered.transpose(2, 1, 0, 3, 4).reshape(parts, -1, width)


class Streams:
    def __init__(self):
        self.under_way = {}
        self.done = {}
        self.started = set()
        self.blocks = []

    def _take(self, name, stages, value):
        try:
            self.under_way[name] = (stages, stages.send(value))
        except StopIteration as end:
            self.under_way.pop(name, None)
            self.done[name] = end.value

    def start(self, name, stages):
        self.started.add(name)
        self._take(name, stages, None)

    def advance(self, names, *anchors):
        names = [name for name in names if name in self.under_way]
        values = [self.under_way[name][1] for name in names]
        values, anchors = lax.optimization_barrier((values, anchors))
        for name, value in zip(names, values):
            self._take(name, self.under_way[name][0], value)
        return anchors[0] if len(anchors) == 1 else anchors

    def finish(self, names):
        while any(name in self.under_way for name in names):
            self.advance(names)


def part_rows(weight, start, rows):
    return lax.dynamic_slice_in_dim(weight, start, rows, axis=0)


def on_device(
    layer_input,
    segments,
    routes,
    cotangent,
    norm1_gain,
    in_weight,
    conv_weight,
    conv_bias,
    xproj_weight,
    dtproj_weight,
    dt_bias,
    a_log,
    skip_gain,
    out_weight,
    norm2_gain,
    router_weight,
    up_weight,
    down_weight,
):
    seq_len, model_width = layer_input.shape[2:]
    sequences = layer_input.shape[0] * layer_input.shape[1]
    tokens = sequences * seq_len
    expert_devices = lax.axis_size("expert")
    dp_devices = lax.axis_size("dp")
    devices = dp_devices * expert_devices
    assert up_weight.shape[0] == 1
    expert_count = expert_devices
    capacity = seq_len * 5 // (4 * expert_count)
    padded_capacity = -(-capacity // 16) * 16
    slots = sequences * padded_capacity
    taps = conv_weight.shape[0]
    rank = dtproj_weight.shape[0]
    states = a_log.shape[0]
    channels = skip_gain.shape[0]
    inner_width = channels * devices
    steps = dp_devices // 2
    expert_index = lax.axis_index("expert")
    small = jnp.concatenate(
        [
            xproj_weight,
            dtproj_weight.T,
            a_log.T,
            conv_weight.T,
            conv_bias[:, None],
            dt_bias[:, None],
            skip_gain[:, None],
        ],
        axis=1,
    )
    streams = Streams()

    def ring_blocks(block):
        ring = mesh_rings()[0]
        blocks = streams.blocks
        blocks.append(block)
        for _ in range(steps - 1):
            blocks.append((yield ring.hop(blocks[-1])))
        return blocks

    in_block = lax.dynamic_index_in_dim(
        in_weight.reshape(2, expert_devices, channels, model_width), expert_index, 1, keepdims=False
    ).reshape(2 * channels, model_width)
    streams.start("in", far_gather(in_block))
    streams.start("small", small_gather(small))
    for _ in range(steps - 1):
        streams.advance(("in", "small"))
    in_blocks = streams.done["in"].reshape(2, -1, model_width)
    with jax.named_scope("fetch_in"):
        in_cube = cube_gather(jnp.concatenate([in_blocks[0], in_blocks[1]], axis=1))
    out_block = part_rows(out_weight, expert_index * channels, channels)
    out_block = lax.optimization_barrier((out_block, in_blocks))[0]
    streams.start("out", far_and_pair(out_block))
    for _ in range(steps - 2):
        streams.advance(("out", "small"))
    expert_block = jnp.concatenate([up_weight[0], down_weight[0]], axis=0)
    expert_block = streams.advance(("out", "small"), expert_block)
    streams.start("expert", ring_blocks(expert_block))
    streams.finish(("out", "small"))
    with jax.named_scope("fetch_out"):
        out_full = cube_gather(streams.done["out"].reshape(-1, model_width))
    small_full = streams.done["small"]
    xproj_width = rank + 2 * states
    xproj_full = small_full[:, :xproj_width]
    across = small_full[:, xproj_width:].T
    dtproj_full = across[:rank]
    across = across[rank:].astype(jnp.float32)
    log_rates = across[:states]
    conv_full = across[states : states + taps]
    convb_full = across[states + taps]
    dtb_full = across[states + taps + 1]
    skip_full = across[states + taps + 2]
    conv_rows = jnp.concatenate(
        [
            conv_full,
            convb_full[None],
            skip_full[None],
            jnp.zeros((ROWS - taps - 2, inner_width), jnp.float32),
        ],
        axis=0,
    )
    segment_rows = segments.reshape(sequences, seq_len)
    masks = [same_document(segment_rows, offset)[:, :, None] for offset in range(taps)]
    mask_columns = jnp.concatenate([mask.reshape(tokens, 1) for mask in masks], axis=1)
    rate = -jnp.exp(log_rates)
    rate_two = rate * LOG2E
    route_rows = routes.reshape(sequences, seq_len)
    placed = dispatch_matrices(
        route_rows ^ expert_index.astype(jnp.int32), expert_count, capacity, padded_capacity
    )
    in_cube, conv_rows, mask_columns, xproj_full, dtproj_full, rate_two, placed, dtb_full = (
        streams.advance(
            ("expert",),
            in_cube,
            conv_rows,
            mask_columns,
            xproj_full,
            dtproj_full,
            rate_two,
            placed,
            dtb_full,
        )
    )
    inner_full = in_cube[:, :model_width]
    gate_full = in_cube[:, model_width:]
    gain_one = norm1_gain.astype(jnp.float32)
    gain_two = norm2_gain.astype(jnp.float32)
    router_full = router_weight.astype(jnp.float32)

    def split(values):
        return values.reshape(sequences, seq_len, values.shape[-1])

    def flat(values):
        return values.reshape(tokens, values.shape[-1])

    rows_in = layer_input.reshape(tokens, model_width).astype(jnp.float32)
    cot_rows = cotangent.reshape(tokens, model_width).astype(jnp.float32)
    normed_one, norm_pull = jax.vjp(rms_scale, rows_in, gain_one)
    normed_low = normed_one.astype(LOW)
    inner = split(dot(normed_low, inner_full, ((1,), (1,))))
    gate_in = split(dot(normed_low, gate_full, ((1,), (1,))))
    conv_out = jax.nn.silu(conv_sum(inner, conv_full, convb_full, masks))
    conv_low = flat(conv_out).astype(LOW)
    projected = dot(conv_low, xproj_full, ((1,), (0,)))
    dt_low = projected[:, :rank].astype(LOW)
    b_wide = jnp.broadcast_to(
        split(projected[:, rank : rank + states])[..., None], (sequences, seq_len, states, LANES)
    )
    c_wide = jnp.broadcast_to(
        split(projected[:, rank + states :])[..., None], (sequences, seq_len, states, LANES)
    )
    dt_sum = split(dot(dt_low, dtproj_full, ((1,), (0,)))) + dtb_full
    delta = jax.nn.softplus(dt_sum)
    decay = jnp.where(masks[1] > 0, delta, FAR)
    drive = delta * conv_out
    scanned = run_forward(decay, drive, b_wide, c_wide, rate_two)
    scanned = streams.advance(("expert",), scanned)
    mixed = scanned + skip_full * conv_out
    gate_silu = jax.nn.silu(gate_in)
    mixed_low = flat(mixed * gate_silu).astype(LOW)
    residual = rows_in + dot(mixed_low, out_full, ((1,), (0,)))

    chosen_rows = (
        route_rows.reshape(tokens, 1) == jnp.arange(expert_count, dtype=jnp.int32)[None]
    ).astype(jnp.float32)

    def route_piece(resid_value, gain_value, router_value):
        return norm_route(resid_value, gain_value, router_value, chosen_rows)

    (normed_two, gate_row), route_pull = jax.vjp(route_piece, residual, gain_two, router_full)
    sending = split(
        jnp.concatenate(
            [normed_two.astype(LOW), (cot_rows * gate_row[:, None]).astype(LOW)], axis=1
        )
    )

    def partners(cross, k):
        place = lambda d, e: d * expert_devices + e
        return [
            (place(d, e), place(d ^ cross, e ^ k))
            for d in range(dp_devices)
            for e in range(expert_devices)
        ]

    def exchange(piece, cross, k):
        if not cross and not k:
            return piece
        return lax.ppermute(piece, BOTH, partners(cross, k))

    pieces = [
        jnp.einsum("stk,std->skd", matrix, sending, preferred_element_type=jnp.float32).astype(LOW)
        for matrix in placed
    ]
    with jax.named_scope("send_rows"):
        received = [
            [exchange(pieces[k], cross, k).reshape(slots, -1) for k in range(expert_count)]
            for cross in (0, 1)
        ]

    units = up_weight.shape[1]
    up_terms = [0.0] * steps
    down_terms = [0.0] * steps
    kept = []
    sums = [[0.0, 0.0], [0.0, 0.0]]

    def expert_block(cross, k, rows, block):
        up, down = block[:units], block[units:]
        slot_rows, d_returned = rows[:, :model_width], rows[:, model_width:]
        hidden = dot(slot_rows, up, ((1,), (1,)))
        active, gelu_pull = jax.vjp(gelu_tanh, hidden)
        active_low = active.astype(LOW)
        d_active = dot(d_returned, down, ((1,), (1,)))
        d_hidden_low = gelu_pull(d_active)[0].astype(LOW)
        sums[cross][0] = sums[cross][0] + dot(active_low, down, ((1,), (0,)))
        sums[cross][1] = sums[cross][1] + dot(d_hidden_low, up, ((1,), (0,)))
        kept.append((k, active_low, d_hidden_low, slot_rows, d_returned))

    while len(streams.blocks) < steps - 1:
        streams.advance(("expert",))
    groups = [jnp.concatenate(received[0], axis=0), None]
    early = list(enumerate(streams.blocks[: steps - 1]))
    for k, block in early:
        expert_block(0, k, groups[0], block)
    sums[0], cross_pieces = lax.optimization_barrier((sums[0], received[1]))
    groups[1] = jnp.concatenate(cross_pieces, axis=0)
    for k, block in early:
        expert_block(1, k, groups[1], block)
    sums = list(streams.advance(("expert",), *sums))
    last = steps - 1
    for cross in (1, 0):
        expert_block(cross, last, groups[cross], streams.done["expert"][last])
    results = [
        jnp.concatenate([returned.astype(LOW), d_slots.astype(LOW)], axis=1).reshape(
            expert_count, sequences, padded_capacity, 2 * model_width
        )
        for returned, d_slots in sums
    ]
    with jax.named_scope("send_results"):
        arrived = [
            [exchange(results[cross][k], cross, k) for k in range(expert_count)]
            for cross in (0, 1)
        ]
    for k, active_low, d_hidden_low, slot_rows, d_returned in kept:
        down_terms[k] = down_terms[k] + dot(active_low, d_returned, ((0,), (0,)))
        up_terms[k] = up_terms[k] + dot(d_hidden_low, slot_rows, ((0,), (0,)))
    terms = [
        jnp.concatenate([up.astype(LOW), down.astype(LOW)], axis=0)
        for up, down in zip(up_terms, down_terms)
    ]
    terms, arrived = lax.optimization_barrier((terms, arrived))
    streams.start("expert_grad", ring_sum(terms))
    gathered_both = 0.0
    for k in range(expert_count):
        total = (arrived[0][k].astype(jnp.float32) + arrived[1][k].astype(jnp.float32)).astype(LOW)
        gathered_both = gathered_both + jnp.einsum(
            "stk,skd->std", placed[k], total, preferred_element_type=jnp.float32
        )
    gathered_both = flat(gathered_both)
    gathered = gathered_both[:, :model_width]
    d_sent = gathered_both[:, model_width:]
    layer_output = (residual + gate_row[:, None] * gathered).astype(LOW)


    d_gate = jnp.sum(cot_rows * gathered, axis=1)
    d_resid_norm, d_gain_two, d_router = route_pull((d_sent, d_gate))
    d_residual = cot_rows + d_resid_norm
    d_branch_low = d_residual.astype(LOW)

    out_gate_term, d_gate_low, d_scanned = run_gate_backward(
        d_branch_low, normed_low, out_full, mixed_low, flat(mixed), flat(gate_in)
    )
    with jax.named_scope("reduce_out_gate"):
        out_gate_blocks = cube_scatter(out_gate_term)
    d_scanned = split(d_scanned)
    d_drive, d_decay, d_rate, d_b, d_c = run_backward(
        decay, drive, b_wide, c_wide, rate_two, d_scanned
    )
    d_drive = streams.advance(("expert_grad",), d_drive)
    d_skip = jnp.sum(d_scanned * conv_out, axis=(0, 1))
    d_alog = jnp.sum(d_rate, axis=0) * rate
    d_delta = d_decay * (1.0 / LOG2E) + d_drive * conv_out
    d_dt = d_delta * jax.nn.sigmoid(dt_sum)
    d_dtb = jnp.sum(d_dt, axis=(0, 1))
    d_dt_low = flat(d_dt).astype(LOW)
    d_dt_rows = dot(d_dt_low, dtproj_full, ((1,), (1,)))
    d_proj_low = jnp.concatenate(
        [
            d_dt_rows,
            d_b[:, 0].reshape(tokens, states),
            d_c[:, 0].reshape(tokens, states),
        ],
        axis=1,
    ).astype(LOW)
    more_rows = jnp.concatenate([d_alog, d_dtb[None], d_skip[None]], axis=0)
    more_rows = jnp.pad(more_rows, ((0, -more_rows.shape[0] % ROWS), (0, 0)))
    inner_term, d_normed, small_term = run_conv_backward(
        flat(d_drive),
        flat(delta),
        flat(d_scanned),
        flat(inner),
        d_gate_low,
        d_proj_low,
        normed_low,
        mask_columns,
        conv_rows,
        xproj_full,
        in_cube,
        d_dt_low,
        dt_low,
        more_rows,
    )
    inner_term, d_normed, small_term = streams.advance(
        ("expert_grad",), inner_term, d_normed, small_term
    )
    with jax.named_scope("reduce_inner"):
        inner_blocks = cube_scatter(inner_term)
    with jax.named_scope("reduce_small"):
        small_width = small_term.shape[1]
        pieces = small_term.reshape(2, expert_devices, steps // 2, 2, channels, small_width)
        pieces = lax.all_to_all(
            pieces.transpose(2, 0, 3, 1, 4, 5).reshape(devices, channels, small_width),
            BOTH,
            split_axis=0,
            concat_axis=0,
            tiled=True,
        )
    out_blocks = out_gate_blocks[:, :model_width]
    gate_blocks = out_gate_blocks[:, model_width:]
    streams.start(
        "out_grad", far_and_pair_sum(out_blocks.reshape(-1, 2, channels, model_width))
    )
    d_rows_norm, d_gain_one = norm_pull(d_normed)
    input_grad = d_residual + d_rows_norm

    gains = jnp.concatenate([d_gain_one[None], d_gain_two[None], d_router.T], axis=0)
    streams.start("gains", butterfly(gains))
    streams.advance(("out_grad", "gains"))
    streams.advance(("gains", "expert_grad"))
    streams.finish(("out_grad",))
    streams.start("out_rows", shared_rows(streams.done["out_grad"][None]))
    streams.finish(("gains", "out_rows", "expert_grad"))
    in_places = jnp.concatenate([inner_blocks, gate_blocks], axis=0)
    streams.start("in_grad", far_sum(in_places.reshape(steps, 2, channels, model_width)))
    pieces = streams.advance(("in_grad",), pieces)
    streams.start("in_rows", shared_rows(streams.done["in_grad"]))
    streams.finish(("in_rows",))
    in_grad = streams.done["in_rows"].reshape(in_weight.shape).astype(jnp.float32)
    out_grad = streams.done["out_rows"][0].astype(jnp.float32)
    expert_grad = streams.done["expert_grad"].astype(jnp.float32)
    up_grad, down_grad = expert_grad[:units], expert_grad[units:]
    gains = streams.done["gains"]
    small_grad = jnp.sum(pieces.astype(jnp.float32), axis=0)
    xproj_grad = small_grad[:, :xproj_width]
    row_grads = small_grad[:, xproj_width:].T
    dtproj_grad = row_grads[:rank]
    row_grads = row_grads[rank:]
    conv_grad = row_grads[:taps]
    convb_grad = row_grads[taps]
    alog_grad = row_grads[ROWS : ROWS + states]
    dtb_grad, skip_grad = row_grads[ROWS + states], row_grads[ROWS + states + 1]

    return (
        layer_output.reshape(layer_input.shape),
        input_grad.reshape(layer_input.shape),
        gains[0],
        in_grad,
        conv_grad,
        convb_grad,
        xproj_grad,
        dtproj_grad,
        dtb_grad,
        alog_grad,
        skip_grad,
        out_grad,
        gains[1],
        gains[2:].T,
        up_grad[None],
        down_grad[None],
    )


def solution(mesh):
    placed = (
        P(None, ("dp", "expert"), None, None),
        P(None, ("dp", "expert"), None),
        P(None, ("dp", "expert"), None, None),
        P(None, ("dp", "expert"), None, None),
        P(),
        P("dp", None),
        P(None, ("dp", "expert")),
        P(("dp", "expert")),
        P(("dp", "expert"), None),
        P(None, ("dp", "expert")),
        P(("dp", "expert")),
        P(None, ("dp", "expert")),
        P(("dp", "expert")),
        P("dp", None),
        P(),
        P(),
        P("expert", "dp", None),
        P("expert", "dp", None),
    )
    return jax.shard_map(
        on_device,
        mesh=mesh,
        in_specs=placed,
        out_specs=(
            P(None, ("dp", "expert"), None, None),
            P(None, ("dp", "expert"), None, None),
            P(),
            P("dp", None),
            P(None, ("dp", "expert")),
            P(("dp", "expert")),
            P(("dp", "expert"), None),
            P(None, ("dp", "expert")),
            P(("dp", "expert")),
            P(None, ("dp", "expert")),
            P(("dp", "expert")),
            P("dp", None),
            P(),
            P(),
            P("expert", "dp", None),
            P("expert", "dp", None),
        ),
        check_vma=False,
    )
```

time: 783 us -> 556 us (0.71)
  waiting for transfers between devices: 379 us -> 211 us
  blocking collectives: 115 us -> 0 us
  starting transfers between devices: 24.4 us -> 71.1 us
  Pallas kernels: 40.2 us -> 73.3 us
  matrix products: 91.8 us -> 66.8 us
  other arithmetic: 42.2 us -> 59.5 us
  local copies, waits for them, and re-layouts: 62.8 us -> 51.8 us
    all_gather x3 -> x2, waiting for transfers between devices: 75.9 us -> 0.01 us  [cube_gather(): lax.all_gather(block, BOTH, axis=0, tiled=True, axis_index_groups=cubes())]
    unnamed x6 -> x4, waiting for transfers between devices: 67.4 us -> 0.07 us
    psum x1 -> x0, blocking collectives: 58.4 us -> none  [on_device(): lax.psum(jnp.concatenate([d_gain_one[None], d_gain_two[None], d_router.T]...]
    ppermute x14 -> x49, starting transfers between devices: 10.2 us -> 67.5 us  [the longest x30 44.9 us: hop(): return lax.ppermute(values, self.axis_name, pairs)]
    all_gather x2 -> x0, blocking collectives: 56.6 us -> none  [the longest x1 48.5 us: on_device(): small_full = lax.all_gather(small, BOTH, axis=0, tiled=True)]
    reduce_scatter x1 -> x2, waiting for transfers between devices: 0.02 us -> 48.1 us  [cube_scatter(): lax.psum_scatter(total, BOTH, scatter_dimension=0, tiled=True, axis_index...]
    ppermute x14 -> x49, waiting for transfers between devices: 207 us -> 162 us  [the longest x30 121 us: hop(): return lax.ppermute(values, self.axis_name, pairs)]
    all_to_all x3 -> x1, waiting for transfers between devices: 29 us -> 0.01 us  [on_device(): lax.all_to_all(pieces.transpose(2, 0, 3, 1, 4, 5).reshape(devices, channe...]
  transfers between devices with their start and end apart: 22 -> 54, of which waited for: 17 -> 28; matrix products, arithmetic and copies ran while one was open for 15% -> 27% of each run, Pallas kernels for 2% -> 11%
where the time goes in v2:
time: 556 us; the launch traced here: 549 us
  waiting for transfers between devices  211 us (38%)
  Pallas kernels  73.3 us (13%)
  starting transfers between devices  71.1 us (13%)
  matrix products  66.8 us (12%)
  other arithmetic  59.5 us (11%)
  local copies, waits for them, and re-layouts  51.8 us (9%)
  between operations  15.8 us (3%)
    ppermute x30, waiting for transfers between devices, hop(): return lax.ppermute(values, self.axis_name, pairs)  121 us
    dot_general x54, matrix products, dot(): lax.dot_general(left, right, (contract, ((), ())), preferred_element_type...  59.9 us
    reduce_scatter x2, waiting for transfers between devices, cube_scatter(): lax.psum_scatter(total, BOTH, scatter_dimension=0, tiled=True, axis_index...  48.1 us
    ppermute x30, starting transfers between devices, hop(): return lax.ppermute(values, self.axis_name, pairs)  44.9 us
    ppermute x14, waiting for transfers between devices, exchange(): return lax.ppermute(piece, BOTH, partners(cross, k))  39.5 us
    pallas_call x1, Pallas kernels, run_backward(): pl.pallas_call(scan_backward, grid=(count, channels // width), in_specs=[...  31 us
    pallas_call x1, Pallas kernels, run_conv_backward(): pl.pallas_call(conv_backward, grid=(channels // width,), in_specs=[tokens...  15.8 us
    pallas_call x1, Pallas kernels, run_forward(): pl.pallas_call(scan_forward, grid=(count, channels // width), in_specs=[t...  14.2 us
  transfers between devices with their start and end apart: 54, of which 28 were waited for; matrix products, arithmetic and copies ran while one was open for 27% of the time, Pallas kernels for 11%

profile of v2, /device:TPU:0, one launch (start us, length us, event | category | flops | bytes accessed | tf_op | source)
XLA Modules:
  0.0 548.9 jit_solution(3602094733120977352)
XLA Ops:
  8.5 3.1 collective-permute-start.1
  18.4 3.0 collective-permute-done.1
  23.1 2.8 collective-permute-done.4
  25.9 6.3 %collective-permute-done.3 = bf16[1,144,1152]{2,1,0:T(8,128)(2,1)S(1)} collective-permute-done((bf16[1,144,1152]{2,1,0:T(8,128)(2,1)S(1)}, bf16[1,144,1152]{2,1,0:T(8,128)(2,1)S(1)}, u32[]{:S(2)}, u32[]{:S(2)}) %collective-permute-start.3) | collective-permute-done | bytes 331808 | tf_op jit(solution)/shard_map/ppermute | solution.py:442
  33.6 3.9 collective-permute-done.6
  37.5 4.6 collective-permute-done.5
  45.1 10.6 %collective-permute-done = bf16[1,72,1152]{2,1,0:T(8,128)(2,1)S(1)} collective-permute-done((bf16[1,72,1152]{2,1,0:T(8,128)(2,1)S(1)}, bf16[1,72,1152]{2,1,0:T(8,128)(2,1)S(1)}, u32[]{:S(2)}, u32[]{:S(2)}) %collective-permute-start) | collective-permute-done | bytes 165920 | tf_op jit(solution)/shard_map/ppermute | solution.py:442
  58.3 8.2 %collective-permute-done.8 = bf16[1,72,1152]{2,1,0:T(8,128)(2,1)S(1)} collective-permute-done((bf16[1,72,1152]{2,1,0:T(8,128)(2,1)S(1)}, bf16[1,72,1152]{2,1,0:T(8,128)(2,1)S(1)}, u32[]{:S(2)}, u32[]{:S(2)}) %collective-permute-start.8) | collective-permute-done | bytes 165920 | tf_op jit(solution)/shard_map/ppermute | solution.py:442
  67.6 9.3 %collective-permute-done.10 = bf16[1,72,1152]{2,1,0:T(8,128)(2,1)S(1)} collective-permute-done((bf16[1,72,1152]{2,1,0:T(8,128)(2,1)S(1)}, bf16[1,72,1152]{2,1,0:T(8,128)(2,1)S(1)}, u32[]{:S(2)}, u32[]{:S(2)}) %collective-permute-start.10) | collective-permute-done | bytes 165920 | tf_op jit(solution)/shard_map/ppermute | solution.py:442
  80.4 13.8 %collective-permute-done.14 = bf16[2,1,72,1152]{3,2,1,0:T(8,128)(2,1)S(1)} collective-permute-done((bf16[2,1,72,1152]{3,2,1,0:T(8,128)(2,1)}, bf16[2,1,72,1152]{3,2,1,0:T(8,128)(2,1)S(1)}, u32[]{:S(2)}, u32[]{:S(2)}) %collective-permute-start.14) | collective-permute-done | bytes 331808 | tf_op jit(solution)/shard_map/ppermute | solution.py:442
  94.9 2.2 maximum_select_fusion
  111.0 27.9 %collective-permute-done.12 = bf16[768,1152]{1,0:T(8,128)(2,1)} collective-permute-done((bf16[768,1152]{1,0:T(8,128)(2,1)S(1)}, bf16[768,1152]{1,0:T(8,128)(2,1)}, u32[]{:S(2)}, u32[]{:S(2)}) %collective-permute-start.12) | collective-permute-done | bytes 1769504 | tf_op jit(solution)/shard_map/ppermute | solution.py:442
  139.6 4.2 fusion.2.inner_ref
  146.3 2.4 compare_select_fusion
  148.7 2.9 fusion.30
  154.8 14.2 %scan_forward.1 = f32[2,96,2304]{2,1,0:T(8,128)} custom-call(f32[2,96,2304]{2,1,0:T(8,128)} %get-tuple-element.305.decay_ref, f32[2,96,2304]{2,1,0:T(8,128)} %get-tuple-element.304.drive_ref, f32[2,96,16,128]{3,2,1,0:T(8,128)} %broadcast_in_dim.115.b_ref, f32[2,96,16,128]{3,2,1,0:T(8,128)} %broadcast_in_dim.117.c_ref, f32[16,2304]{1,0:T(8,128)} %fusion.198.rate_ref), custom_call_target="tpu_custom_call" | custom-call | flops 442368 | bytes 8454144 | tf_op jit(solution)/shard_map/scan_forward/pallas_call | solution.py:140
  169.1 4.3 fusion.gate_ref
  174.8 2.0 multiply_convert_fusion
  176.8 4.2 multiply_reduce_fusion.5
  187.5 17.2 %collective-permute-done.17 = bf16[2,32,2304]{2,1,0:T(8,128)(2,1)S(1)} collective-permute-done((bf16[2,32,2304]{2,1,0:T(8,128)(2,1)S(1)}, bf16[2,32,2304]{2,1,0:T(8,128)(2,1)S(1)}, u32[]{:S(2)}, u32[]{:S(2)}) %collective-permute-start.17) | collective-permute-done | bytes 294944 | tf_op jit(solution)/shard_map/send_rows/ppermute | solution.py:801
  204.7 2.0 collective-permute-start.21
  262.7 3.9 collective-permute-done.24
  268.2 3.8 collective-permute-done.25
  272.0 2.0 collective-permute-done.27
  274.0 7.4 %collective-permute-done.28 = bf16[2,32,2304]{2,1,0:T(8,128)(2,1)S(1)} collective-permute-done((bf16[2,32,2304]{2,1,0:T(8,128)(2,1)S(1)}, bf16[2,32,2304]{2,1,0:T(8,128)(2,1)S(1)}, u32[]{:S(2)}, u32[]{:S(2)}) %collective-permute-start.28) | collective-permute-done | bytes 294944 | tf_op jit(solution)/shard_map/send_results/ppermute | solution.py:801
  281.4 5.2 collective-permute-done.29
  293.4 12.3 %gate_backward.1 = (bf16[2304,2304]{1,0:T(8,128)(2,1)}, bf16[192,2304]{1,0:T(8,128)(2,1)}, f32[192,2304]{1,0:T(8,128)}) custom-call(bf16[192,1152]{1,0:T(8,128)(2,1)} %fusion.263.d_branch_ref, bf16[192,1152]{1,0:T(8,128)(2,1)} %copy-done.20, bf16[2304,1152]{1,0:T(8,128)(2,1)} %all-gather.5.cloned.1.call-done.out_ref, bf16[192,2304]{1,0:T(8,128)(2,1)} %bitcast.206, ...), custom_call_target="tpu_custom_call" | custom-call | flops 192 | bytes 192 | tf_op jit(solution)/shard_map/gate_backward/pallas_call | solution.py:206
  310.2 31.0 %scan_backward.1 = (f32[2,96,2304]{2,1,0:T(8,128)}, f32[2,96,2304]{2,1,0:T(8,128)}, f32[2,16,2304]{2,1,0:T(8,128)}, f32[2,8,1536]{2,1,0:T(8,128)}, f32[2,8,1536]{2,1,0:T(8,128)}) custom-call(f32[2,96,2304]{2,1,0:T(8,128)} %get-tuple-element.305.decay_ref, f32[2,96,2304]{2,1,0:T(8,128)} %get-tuple-element.304.drive_ref, ...), custom_call_target="tpu_custom_call" | custom-call | flops 442368 | bytes 15138816 | tf_op jit(solution)/shard_map/scan_backward/pallas_call | solution.py:161
  349.2 3.8 add_convert_fusion.1
  353.0 3.7 collective-permute-start.31
  358.5 2.9 fusion.264
  367.4 15.8 %conv_backward.1 = (bf16[2304,1152]{1,0:T(8,128)(2,1)}, f32[192,1152]{1,0:T(8,128)}, bf16[2304,208]{1,0:T(8,128)(2,1)}) custom-call(f32[192,2304]{1,0:T(8,128)} %bitcast.191, f32[192,2304]{1,0:T(8,128)} %get-tuple-element.351.delta_ref, f32[192,2304]{1,0:T(8,128)} %get-tuple-element.144.d_scanned_ref, f32[192,2304]{1,0:T(8,128)} %copy-done.9, ...), custom_call_target="tpu_custom_call" | custom-call | flops 192 | bytes 192 | tf_op jit(solution)/shard_map/conv_backward/pallas_call | solution.py:311
  383.2 12.3 %collective-permute-done.31 = bf16[768,1152]{1,0:T(8,128)(2,1)} collective-permute-done((bf16[768,1152]{1,0:T(8,128)(2,1)}, bf16[768,1152]{1,0:T(8,128)(2,1)}, u32[]{:S(2)}, u32[]{:S(2)}) %collective-permute-start.31) | collective-permute-done | bytes 1769504 | tf_op jit(solution)/shard_map/ppermute | solution.py:442
  397.8 2.0 multiply_reduce_fusion.2
  400.5 3.3 add_convert_fusion
  403.8 2.3 collective-permute-start.35
  407.1 3.5 all-to-all-start
  411.4 2.1 fusion.27
  416.6 48.1 %reduce-scatter.5.cloned.1.call-done = bf16[288,1152]{1,0:T(8,128)(2,1)} async-done(((bf16[2304,1152]{1,0:T(8,128)(2,1)}), bf16[288,1152]{1,0:T(8,128)(2,1)}) %reduce-scatter.5.cloned.1.call-update) | async-done | bytes 663568 | tf_op jit(solution)/shard_map/reduce_inner/reduce_scatter | solution.py:477
  473.7 4.9 collective-permute-done.44
  478.6 13.4 %collective-permute-start.37 = (bf16[72,1152]{1,0:T(8,128)(2,1)}, bf16[72,1152]{1,0:T(8,128)(2,1)}, u32[]{:S(2)}, u32[]{:S(2)}) collective-permute-start(bf16[72,1152]{1,0:T(8,128)(2,1)} %get-tuple-element.324), channel_id=1, source_target_pairs={{0,8},{4,12},{8,16},{12,20},{16,24},{20,28},{24,0},{28,4},{1,9},{5... | collective-permute-start | bytes 497672 | tf_op jit(solution)/shard_map/ppermute | solution.py:442
  492.0 5.1 collective-permute-done.45
  497.9 5.0 collective-permute-start.39
  509.5 5.0 collective-permute-start.47
  518.5 4.6 collective-permute-done.40
  523.4 2.0 slice_bitcast_fusion
  525.4 5.9 %collective-permute-start.41 = (f32[6,1152]{1,0:T(8,128)S(1)}, f32[6,1152]{1,0:T(8,128)S(1)}, u32[]{:S(2)}, u32[]{:S(2)}) collective-permute-start(f32[6,1152]{1,0:T(8,128)S(1)} %add.502), channel_id=1, source_target_pairs={{0,8},{4,12},{8,0},{12,4},{16,24},{20,28},{24,16},{28,20},{1,9},{5... | collective-permute-start | bytes 82952 | tf_op jit(solution)/shard_map/ppermute | solution.py:427
  533.5 3.1 collective-permute-start.43
  (455 shorter events, 169.6 us)
Async XLA Ops:
  7.2 131.8 %all-gather.3.cloned.1.call-start = ((), (), s32[]{:S(2)}) async-start(), calls=%async_computation.3 | async-start | bytes 11943936 | tf_op jit(solution)/shard_map/fetch_in/all_gather | solution.py:473
  8.5 12.9 %collective-permute-start.1 = (bf16[1,144,1152]{2,1,0:T(8,128)(2,1)S(1)}, bf16[1,144,1152]{2,1,0:T(8,128)(2,1)S(1)}, u32[]{:S(2)}, u32[]{:S(2)}) collective-permute-start(bf16[1,144,1152]{2,1,0:T(8,128)(2,1)S(1)} %bitcast.219), channel_id=1, source_target_pairs={{0,8},{4,12},{8,16},{12,20},{16,24},{20,28},{24,0},{28,4},{1,9},{5... | collective-permute-start | bytes 995336 | tf_op jit(solution)/shard_map/ppermute | solution.py:442
  21.4 10.8 %collective-permute-start.3 = (bf16[1,144,1152]{2,1,0:T(8,128)(2,1)S(1)}, bf16[1,144,1152]{2,1,0:T(8,128)(2,1)S(1)}, u32[]{:S(2)}, u32[]{:S(2)}) collective-permute-start(bf16[1,144,1152]{2,1,0:T(8,128)(2,1)S(1)} %collective-permute-done.1), channel_id=1, source_target_pairs={{0,8},{4,12},{8,16},{12,20},{16,24},{20,28},{24,0},{28,4},{1,9},{5... | collective-permute-start | bytes 995336 | tf_op jit(solution)/shard_map/ppermute | solution.py:442
  32.2 9.9 %collective-permute-start.5 = (bf16[1,144,1152]{2,1,0:T(8,128)(2,1)S(1)}, bf16[1,144,1152]{2,1,0:T(8,128)(2,1)S(1)}, u32[]{:S(2)}, u32[]{:S(2)}) collective-permute-start(bf16[1,144,1152]{2,1,0:T(8,128)(2,1)S(1)} %collective-permute-done.3), channel_id=1, source_target_pairs={{0,8},{4,12},{8,16},{12,20},{16,24},{20,28},{24,0},{28,4},{1,9},{5... | collective-permute-start | bytes 995336 | tf_op jit(solution)/shard_map/ppermute | solution.py:442
  43.7 133.1 %all-gather.5.cloned.1.call-start = ((), (), s32[]{:S(2)}) async-start(), calls=%async_computation.4 | async-start | bytes 5971968 | tf_op jit(solution)/shard_map/fetch_out/all_gather | solution.py:473
  44.0 11.8 %collective-permute-start.7 = (bf16[1,576,199]{2,1,0:T(8,128)(2,1)S(1)}, bf16[1,576,199]{2,1,0:T(8,128)(2,1)S(1)}, u32[]{:S(2)}, u32[]{:S(2)}) collective-permute-start(bf16[1,576,199]{2,1,0:T(8,128)(2,1)S(1)} %bitcast.224), channel_id=1, source_target_pairs={{0,8},{4,12},{8,16},{12,20},{16,24},{20,28},{24,0},{28,4},{1,9},{5... | collective-permute-start | bytes 687752 | tf_op jit(solution)/shard_map/ppermute | solution.py:442
  45.0 10.7 %collective-permute-start = (bf16[1,72,1152]{2,1,0:T(8,128)(2,1)S(1)}, bf16[1,72,1152]{2,1,0:T(8,128)(2,1)S(1)}, u32[]{:S(2)}, u32[]{:S(2)}) collective-permute-start(bf16[1,72,1152]{2,1,0:T(8,128)(2,1)S(1)} %bitcast.230), channel_id=1, source_target_pairs={{0,8},{4,12},{8,16},{12,20},{16,24},{20,28},{24,0},{28,4},{1,9},{5... | collective-permute-start | bytes 497672 | tf_op jit(solution)/shard_map/ppermute | solution.py:442
  55.7 10.8 %collective-permute-start.9 = (bf16[1,576,199]{2,1,0:T(8,128)(2,1)S(1)}, bf16[1,576,199]{2,1,0:T(8,128)(2,1)S(1)}, u32[]{:S(2)}, u32[]{:S(2)}) collective-permute-start(bf16[1,576,199]{2,1,0:T(8,128)(2,1)S(1)} %collective-permute-done.7), channel_id=1, source_target_pairs={{0,8},{4,12},{8,16},{12,20},{16,24},{20,28},{24,0},{28,4},{1,9},{5... | collective-permute-start | bytes 687752 | tf_op jit(solution)/shard_map/ppermute | solution.py:442
  57.5 9.0 %collective-permute-start.8 = (bf16[1,72,1152]{2,1,0:T(8,128)(2,1)S(1)}, bf16[1,72,1152]{2,1,0:T(8,128)(2,1)S(1)}, u32[]{:S(2)}, u32[]{:S(2)}) collective-permute-start(bf16[1,72,1152]{2,1,0:T(8,128)(2,1)S(1)} %collective-permute-done), channel_id=1, source_target_pairs={{0,8},{4,12},{8,16},{12,20},{16,24},{20,28},{24,0},{28,4},{1,9},{5... | collective-permute-start | bytes 497672 | tf_op jit(solution)/shard_map/ppermute | solution.py:442
  66.5 10.3 %collective-permute-start.11 = (bf16[1,576,199]{2,1,0:T(8,128)(2,1)S(1)}, bf16[1,576,199]{2,1,0:T(8,128)(2,1)S(1)}, u32[]{:S(2)}, u32[]{:S(2)}) collective-permute-start(bf16[1,576,199]{2,1,0:T(8,128)(2,1)S(1)} %collective-permute-done.9), channel_id=1, source_target_pairs={{0,8},{4,12},{8,16},{12,20},{16,24},{20,28},{24,0},{28,4},{1,9},{5... | collective-permute-start | bytes 687752 | tf_op jit(solution)/shard_map/ppermute | solution.py:442
  67.6 9.3 %collective-permute-start.10 = (bf16[1,72,1152]{2,1,0:T(8,128)(2,1)S(1)}, bf16[1,72,1152]{2,1,0:T(8,128)(2,1)S(1)}, u32[]{:S(2)}, u32[]{:S(2)}) collective-permute-start(bf16[1,72,1152]{2,1,0:T(8,128)(2,1)S(1)} %collective-permute-done.8), channel_id=1, source_target_pairs={{0,8},{4,12},{8,16},{12,20},{16,24},{20,28},{24,0},{28,4},{1,9},{5... | collective-permute-start | bytes 497672 | tf_op jit(solution)/shard_map/ppermute | solution.py:442
  78.5 15.7 %collective-permute-start.14 = (bf16[2,1,72,1152]{3,2,1,0:T(8,128)(2,1)}, bf16[2,1,72,1152]{3,2,1,0:T(8,128)(2,1)S(1)}, u32[]{:S(2)}, u32[]{:S(2)}) collective-permute-start(bf16[2,1,72,1152]{3,2,1,0:T(8,128)(2,1)} %get-tuple-element.328), channel_id=1, source_target_pairs={{0,4},{4,0},{8,12},{12,8},{16,20},{20,16},{24,28},{28,24},{1,5},{5... | collective-permute-start | bytes 995336 | tf_op jit(solution)/shard_map/ppermute | solution.py:442
  97.1 316.4 %reduce-scatter.3.cloned.1.call-start = ((), (), s32[]{:S(2)}) async-start(), calls=%async_computation.5 | async-start | bytes 11943936 | tf_op jit(solution)/shard_map/reduce_out_gate/reduce_scatter | solution.py:477
  101.0 38.0 %collective-permute-start.12 = (bf16[768,1152]{1,0:T(8,128)(2,1)S(1)}, bf16[768,1152]{1,0:T(8,128)(2,1)}, u32[]{:S(2)}, u32[]{:S(2)}) collective-permute-start(bf16[768,1152]{1,0:T(8,128)(2,1)S(1)} %pad_maximum_fusion), channel_id=1, source_target_pairs={{0,8},{4,12},{8,16},{12,20},{16,24},{20,28},{24,0},{28,4},{1,9},{5... | collective-permute-start | bytes 5308424 | tf_op jit(solution)/shard_map/ppermute | solution.py:442
  139.0 35.8 %collective-permute-start.13 = (bf16[768,1152]{1,0:T(8,128)(2,1)}, bf16[768,1152]{1,0:T(8,128)(2,1)}, u32[]{:S(2)}, u32[]{:S(2)}) collective-permute-start(bf16[768,1152]{1,0:T(8,128)(2,1)} %collective-permute-done.12), channel_id=1, source_target_pairs={{0,8},{4,12},{8,16},{12,20},{16,24},{20,28},{24,0},{28,4},{1,9},{5... | collective-permute-start | bytes 5308424 | tf_op jit(solution)/shard_map/ppermute | solution.py:442
  182.8 25.1 %collective-permute-start.15 = (bf16[2,32,2304]{2,1,0:T(8,128)(2,1)S(1)}, bf16[2,32,2304]{2,1,0:T(8,128)(2,1)S(1)}, u32[]{:S(2)}, u32[]{:S(2)}) collective-permute-start(bf16[2,32,2304]{2,1,0:T(8,128)(2,1)S(1)} %convolution_convert_fusion.2), channel_id=1, source_target_pairs={{0,1},{1,0},{2,3},{3,2},{4,5},{5,4},{6,7},{7,6},{8,9},{9,8},{10,11... | collective-permute-start | bytes 884744 | tf_op jit(solution)/shard_map/send_rows/ppermute | solution.py:801
  182.9 41.1 %collective-permute-start.19 = (bf16[2,32,2304]{2,1,0:T(8,128)(2,1)S(1)}, bf16[2,32,2304]{2,1,0:T(8,128)(2,1)S(1)}, u32[]{:S(2)}, u32[]{:S(2)}) collective-permute-start(bf16[2,32,2304]{2,1,0:T(8,128)(2,1)S(1)} %convolution_convert_fusion.2), channel_id=1, source_target_pairs={{0,5},{1,4},{2,7},{3,6},{4,1},{5,0},{6,3},{7,2},{8,13},{9,12},{10,... | collective-permute-start | bytes 884744 | tf_op jit(solution)/shard_map/send_rows/ppermute | solution.py:801
  183.9 22.8 %collective-permute-start.16 = (bf16[2,32,2304]{2,1,0:T(8,128)(2,1)S(1)}, bf16[2,32,2304]{2,1,0:T(8,128)(2,1)S(1)}, u32[]{:S(2)}, u32[]{:S(2)}) collective-permute-start(bf16[2,32,2304]{2,1,0:T(8,128)(2,1)S(1)} %convolution_convert_fusion.1), channel_id=1, source_target_pairs={{0,2},{1,3},{2,0},{3,1},{4,6},{5,7},{6,4},{7,5},{8,10},{9,11},{10,... | collective-permute-start | bytes 884744 | tf_op jit(solution)/shard_map/send_rows/ppermute | solution.py:801
  185.4 38.7 %collective-permute-start.20 = (bf16[2,32,2304]{2,1,0:T(8,128)(2,1)S(1)}, bf16[2,32,2304]{2,1,0:T(8,128)(2,1)S(1)}, u32[]{:S(2)}, u32[]{:S(2)}) collective-permute-start(bf16[2,32,2304]{2,1,0:T(8,128)(2,1)S(1)} %convolution_convert_fusion.1), channel_id=1, source_target_pairs={{0,6},{1,7},{2,4},{3,5},{4,2},{5,3},{6,0},{7,1},{8,14},{9,15},{10,... | collective-permute-start | bytes 884744 | tf_op jit(solution)/shard_map/send_rows/ppermute | solution.py:801
  187.1 17.5 %collective-permute-start.17 = (bf16[2,32,2304]{2,1,0:T(8,128)(2,1)S(1)}, bf16[2,32,2304]{2,1,0:T(8,128)(2,1)S(1)}, u32[]{:S(2)}, u32[]{:S(2)}) collective-permute-start(bf16[2,32,2304]{2,1,0:T(8,128)(2,1)S(1)} %convolution_convert_fusion), channel_id=1, source_target_pairs={{0,3},{1,2},{2,1},{3,0},{4,7},{5,6},{6,5},{7,4},{8,11},{9,10},{10,... | collective-permute-start | bytes 884744 | tf_op jit(solution)/shard_map/send_rows/ppermute | solution.py:801
  204.7 19.4 %collective-permute-start.21 = (bf16[2,32,2304]{2,1,0:T(8,128)(2,1)S(1)}, bf16[2,32,2304]{2,1,0:T(8,128)(2,1)S(1)}, u32[]{:S(2)}, u32[]{:S(2)}) collective-permute-start(bf16[2,32,2304]{2,1,0:T(8,128)(2,1)S(1)} %convolution_convert_fusion), channel_id=1, source_target_pairs={{0,7},{1,6},{2,5},{3,4},{4,3},{5,2},{6,1},{7,0},{8,15},{9,14},{10,... | collective-permute-start | bytes 884744 | tf_op jit(solution)/shard_map/send_rows/ppermute | solution.py:801
  206.7 17.4 %collective-permute-start.18 = (bf16[2,32,2304]{2,1,0:T(8,128)(2,1)S(1)}, bf16[2,32,2304]{2,1,0:T(8,128)(2,1)S(1)}, u32[]{:S(2)}, u32[]{:S(2)}) collective-permute-start(bf16[2,32,2304]{2,1,0:T(8,128)(2,1)S(1)} %convolution_convert_fusion.3), channel_id=1, source_target_pairs={{0,4},{1,5},{2,6},{3,7},{4,0},{5,1},{6,2},{7,3},{8,12},{9,13},{10,... | collective-permute-start | bytes 884744 | tf_op jit(solution)/shard_map/send_rows/ppermute | solution.py:801
  207.9 42.5 %collective-permute-start.22 = (bf16[768,1152]{1,0:T(8,128)(2,1)}, bf16[768,1152]{1,0:T(8,128)(2,1)S(1)}, u32[]{:S(2)}, u32[]{:S(2)}) collective-permute-start(bf16[768,1152]{1,0:T(8,128)(2,1)} %collective-permute-done.13), channel_id=1, source_target_pairs={{0,8},{4,12},{8,16},{12,20},{16,24},{20,28},{24,0},{28,4},{1,9},{5... | collective-permute-start | bytes 5308424 | tf_op jit(solution)/shard_map/ppermute | solution.py:442
  256.7 9.9 %collective-permute-start.24 = (bf16[2,32,2304]{2,1,0:T(8,128)(2,1)S(1)}, bf16[2,32,2304]{2,1,0:T(8,128)(2,1)S(1)}, u32[]{:S(2)}, u32[]{:S(2)}) collective-permute-start(bf16[2,32,2304]{2,1,0:T(8,128)(2,1)S(1)} %bitcast.237), channel_id=1, source_target_pairs={{0,2},{1,3},{2,0},{3,1},{4,6},{5,7},{6,4},{7,5},{8,10},{9,11},{10,... | collective-permute-start | bytes 884744 | tf_op jit(solution)/shard_map/send_results/ppermute | solution.py:801
  257.3 14.7 %collective-permute-start.25 = (bf16[2,32,2304]{2,1,0:T(8,128)(2,1)S(1)}, bf16[2,32,2304]{2,1,0:T(8,128)(2,1)S(1)}, u32[]{:S(2)}, u32[]{:S(2)}) collective-permute-start(bf16[2,32,2304]{2,1,0:T(8,128)(2,1)S(1)} %bitcast.236), channel_id=1, source_target_pairs={{0,3},{1,2},{2,1},{3,0},{4,7},{5,6},{6,5},{7,4},{8,11},{9,10},{10,... | collective-permute-start | bytes 884744 | tf_op jit(solution)/shard_map/send_results/ppermute | solution.py:801
  258.9 13.1 %collective-permute-start.26 = (bf16[2,32,2304]{2,1,0:T(8,128)(2,1)S(1)}, bf16[2,32,2304]{2,1,0:T(8,128)(2,1)S(1)}, u32[]{:S(2)}, u32[]{:S(2)}) collective-permute-start(bf16[2,32,2304]{2,1,0:T(8,128)(2,1)S(1)} %bitcast.243), channel_id=1, source_target_pairs={{0,4},{1,5},{2,6},{3,7},{4,0},{5,1},{6,2},{7,3},{8,12},{9,13},{10,... | collective-permute-start | bytes 884744 | tf_op jit(solution)/shard_map/send_results/ppermute | solution.py:801
  259.8 14.2 %collective-permute-start.27 = (bf16[2,32,2304]{2,1,0:T(8,128)(2,1)S(1)}, bf16[2,32,2304]{2,1,0:T(8,128)(2,1)S(1)}, u32[]{:S(2)}, u32[]{:S(2)}) collective-permute-start(bf16[2,32,2304]{2,1,0:T(8,128)(2,1)S(1)} %bitcast.240), channel_id=1, source_target_pairs={{0,5},{1,4},{2,7},{3,6},{4,1},{5,0},{6,3},{7,2},{8,13},{9,12},{10,... | collective-permute-start | bytes 884744 | tf_op jit(solution)/shard_map/send_results/ppermute | solution.py:801
  261.2 20.3 %collective-permute-start.28 = (bf16[2,32,2304]{2,1,0:T(8,128)(2,1)S(1)}, bf16[2,32,2304]{2,1,0:T(8,128)(2,1)S(1)}, u32[]{:S(2)}, u32[]{:S(2)}) collective-permute-start(bf16[2,32,2304]{2,1,0:T(8,128)(2,1)S(1)} %bitcast.239), channel_id=1, source_target_pairs={{0,6},{1,7},{2,4},{3,5},{4,2},{5,3},{6,0},{7,1},{8,14},{9,15},{10,... | collective-permute-start | bytes 884744 | tf_op jit(solution)/shard_map/send_results/ppermute | solution.py:801
  266.5 20.1 %collective-permute-start.29 = (bf16[2,32,2304]{2,1,0:T(8,128)(2,1)S(1)}, bf16[2,32,2304]{2,1,0:T(8,128)(2,1)S(1)}, u32[]{:S(2)}, u32[]{:S(2)}) collective-permute-start(bf16[2,32,2304]{2,1,0:T(8,128)(2,1)S(1)} %bitcast.238), channel_id=1, source_target_pairs={{0,7},{1,6},{2,5},{3,4},{4,3},{5,2},{6,1},{7,0},{8,15},{9,14},{10,... | collective-permute-start | bytes 884744 | tf_op jit(solution)/shard_map/send_results/ppermute | solution.py:801
  305.8 158.8 %reduce-scatter.5.cloned.1.call-start = ((), (), s32[]{:S(2)}) async-start(), calls=%async_computation.6 | async-start | bytes 5971968 | tf_op jit(solution)/shard_map/reduce_inner/reduce_scatter | solution.py:477
  305.9 43.3 %collective-permute-start.30 = (bf16[768,1152]{1,0:T(8,128)(2,1)}, bf16[768,1152]{1,0:T(8,128)(2,1)}, u32[]{:S(2)}, u32[]{:S(2)}) collective-permute-start(bf16[768,1152]{1,0:T(8,128)(2,1)} %pad_maximum_fusion.2), channel_id=1, source_target_pairs={{0,8},{4,12},{8,16},{12,20},{16,24},{20,28},{24,0},{28,4},{1,9},{5... | collective-permute-start | bytes 5308424 | tf_op jit(solution)/shard_map/ppermute | solution.py:442
  353.0 42.5 %collective-permute-start.31 = (bf16[768,1152]{1,0:T(8,128)(2,1)}, bf16[768,1152]{1,0:T(8,128)(2,1)}, u32[]{:S(2)}, u32[]{:S(2)}) collective-permute-start(bf16[768,1152]{1,0:T(8,128)(2,1)} %add_convert_fusion.1), channel_id=1, source_target_pairs={{0,8},{4,12},{8,16},{12,20},{16,24},{20,28},{24,0},{28,4},{1,9},{5... | collective-permute-start | bytes 5308424 | tf_op jit(solution)/shard_map/ppermute | solution.py:442
  400.5 68.0 %collective-permute-start.33 = (f32[6,1152]{1,0:T(8,128)}, f32[6,1152]{1,0:T(8,128)}, u32[]{:S(2)}, u32[]{:S(2)}) collective-permute-start(f32[6,1152]{1,0:T(8,128)} %pad_maximum_fusion.12), channel_id=1, source_target_pairs={{0,1},{1,0},{2,3},{3,2},{4,5},{5,4},{6,7},{7,6},{8,9},{9,8},{10,11... | collective-permute-start | bytes 82952 | tf_op jit(solution)/shard_map/ppermute | solution.py:427
  403.8 105.7 %collective-permute-start.35 = (bf16[768,1152]{1,0:T(8,128)(2,1)}, bf16[768,1152]{1,0:T(8,128)(2,1)}, u32[]{:S(2)}, u32[]{:S(2)}) collective-permute-start(bf16[768,1152]{1,0:T(8,128)(2,1)} %add_convert_fusion), channel_id=1, source_target_pairs={{0,8},{4,12},{8,16},{12,20},{16,24},{20,28},{24,0},{28,4},{1,9},{5... | collective-permute-start | bytes 5308424 | tf_op jit(solution)/shard_map/ppermute | solution.py:442
  407.1 95.8 %all-to-all-start = ((bf16[32,72,208]{2,1,0:T(8,128)(2,1)}), bf16[32,72,208]{2,1,0:T(8,128)(2,1)}, u32[]{:S(2)}, u32[]{:S(2)}) async-start(bf16[32,72,208]{2,1,0:T(8,128)(2,1)} %bitcast.202), calls=%async_computation.2 | async-start | bytes 2359296 | tf_op jit(solution)/shard_map/reduce_small/all_to_all | solution.py:933
  414.9 55.1 %collective-permute-start.32 = (bf16[2,1,72,1152]{3,2,1,0:T(8,128)(2,1)S(1)}, bf16[2,1,72,1152]{3,2,1,0:T(8,128)(2,1)S(1)}, u32[]{:S(2)}, u32[]{:S(2)}) collective-permute-start(bf16[2,1,72,1152]{3,2,1,0:T(8,128)(2,1)S(1)} %get-tuple-element.326), channel_id=1, source_target_pairs={{0,4},{4,0},{8,12},{12,8},{16,20},{20,16},{24,28},{28,24},{1,5},{5... | collective-permute-start | bytes 995336 | tf_op jit(solution)/shard_map/ppermute | solution.py:442
  466.0 12.6 %collective-permute-start.44 = (bf16[2,72,1152]{2,1,0:T(8,128)(2,1)S(1)}, bf16[2,72,1152]{2,1,0:T(8,128)(2,1)S(1)}, u32[]{:S(2)}, u32[]{:S(2)}) collective-permute-start(bf16[2,72,1152]{2,1,0:T(8,128)(2,1)S(1)} %get-tuple-element.311), channel_id=1, source_target_pairs={{0,8},{4,12},{8,16},{12,20},{16,24},{20,28},{24,0},{28,4},{1,9},{5... | collective-permute-start | bytes 995336 | tf_op jit(solution)/shard_map/ppermute | solution.py:442
  466.9 30.2 %collective-permute-start.45 = (bf16[2,72,1152]{2,1,0:T(8,128)(2,1)S(1)}, bf16[2,72,1152]{2,1,0:T(8,128)(2,1)S(1)}, u32[]{:S(2)}, u32[]{:S(2)}) collective-permute-start(bf16[2,72,1152]{2,1,0:T(8,128)(2,1)S(1)} %get-tuple-element.310), channel_id=1, source_target_pairs={{0,16},{4,20},{8,24},{12,28},{16,0},{20,4},{24,8},{28,12},{1,17},{... | collective-permute-start | bytes 995336 | tf_op jit(solution)/shard_map/ppermute | solution.py:442
  468.5 28.7 %collective-permute-start.46 = (bf16[2,72,1152]{2,1,0:T(8,128)(2,1)S(1)}, bf16[2,72,1152]{2,1,0:T(8,128)(2,1)S(1)}, u32[]{:S(2)}, u32[]{:S(2)}) collective-permute-start(bf16[2,72,1152]{2,1,0:T(8,128)(2,1)S(1)} %get-tuple-element.309), channel_id=1, source_target_pairs={{0,24},{4,28},{8,0},{12,4},{16,8},{20,12},{24,16},{28,20},{1,25},{... | collective-permute-start | bytes 995336 | tf_op jit(solution)/shard_map/ppermute | solution.py:442
  470.9 43.6 %collective-permute-start.34 = (f32[6,1152]{1,0:T(8,128)S(1)}, f32[6,1152]{1,0:T(8,128)S(1)}, u32[]{:S(2)}, u32[]{:S(2)}) collective-permute-start(f32[6,1152]{1,0:T(8,128)S(1)} %fusion.262), channel_id=1, source_target_pairs={{0,2},{1,3},{2,0},{3,1},{4,6},{5,7},{6,4},{7,5},{8,10},{9,11},{10,... | collective-permute-start | bytes 82952 | tf_op jit(solution)/shard_map/ppermute | solution.py:427
  478.6 35.9 %collective-permute-start.37 = (bf16[72,1152]{1,0:T(8,128)(2,1)}, bf16[72,1152]{1,0:T(8,128)(2,1)}, u32[]{:S(2)}, u32[]{:S(2)}) collective-permute-start(bf16[72,1152]{1,0:T(8,128)(2,1)} %get-tuple-element.324), channel_id=1, source_target_pairs={{0,8},{4,12},{8,16},{12,20},{16,24},{20,28},{24,0},{28,4},{1,9},{5... | collective-permute-start | bytes 497672 | tf_op jit(solution)/shard_map/ppermute | solution.py:442
  497.1 17.5 %collective-permute-start.38 = (bf16[72,1152]{1,0:T(8,128)(2,1)}, bf16[72,1152]{1,0:T(8,128)(2,1)}, u32[]{:S(2)}, u32[]{:S(2)}) collective-permute-start(bf16[72,1152]{1,0:T(8,128)(2,1)} %get-tuple-element.323), channel_id=1, source_target_pairs={{0,16},{4,20},{8,24},{12,28},{16,0},{20,4},{24,8},{28,12},{1,17},{... | collective-permute-start | bytes 497672 | tf_op jit(solution)/shard_map/ppermute | solution.py:442
  497.9 17.0 %collective-permute-start.39 = (bf16[72,1152]{1,0:T(8,128)(2,1)}, bf16[72,1152]{1,0:T(8,128)(2,1)}, u32[]{:S(2)}, u32[]{:S(2)}) collective-permute-start(bf16[72,1152]{1,0:T(8,128)(2,1)} %get-tuple-element.322), channel_id=1, source_target_pairs={{0,24},{4,28},{8,0},{12,4},{16,8},{20,12},{24,16},{28,20},{1,25},{... | collective-permute-start | bytes 497672 | tf_op jit(solution)/shard_map/ppermute | solution.py:442
  509.5 21.9 %collective-permute-start.47 = (bf16[1,2,72,1152]{3,2,1,0:T(8,128)(2,1)S(1)}, bf16[1,2,72,1152]{3,2,1,0:T(8,128)(2,1)S(1)}, u32[]{:S(2)}, u32[]{:S(2)}) collective-permute-start(bf16[1,2,72,1152]{3,2,1,0:T(8,128)(2,1)S(1)} %fusion.178), channel_id=1, source_target_pairs={{0,2},{1,3},{2,0},{3,1},{4,6},{5,7},{6,4},{7,5},{8,10},{9,11},{10,... | collective-permute-start | bytes 995336 | tf_op jit(solution)/shard_map/ppermute | solution.py:442
  516.2 6.9 %collective-permute-start.40 = (bf16[1,1,72,1152]{3,2,1,0:T(8,128)(2,1)S(1)}, bf16[1,1,72,1152]{3,2,1,0:T(8,128)(2,1)S(1)}, u32[]{:S(2)}, u32[]{:S(2)}) collective-permute-start(bf16[1,1,72,1152]{3,2,1,0:T(8,128)(2,1)S(1)} %fusion.193), channel_id=1, source_target_pairs={{0,2},{1,3},{2,0},{3,1},{4,6},{5,7},{6,4},{7,5},{8,10},{9,11},{10,... | collective-permute-start | bytes 497672 | tf_op jit(solution)/shard_map/ppermute | solution.py:442
  523.3 10.2 %collective-permute-start.42 = (bf16[1,2,1,72,1152]{4,3,0,1,2:T(8,128)(2,1)S(1)}, bf16[1,2,1,72,1152]{4,3,0,1,2:T(8,128)(2,1)S(1)}, u32[]{:S(2)}, u32[]{:S(2)}) collective-permute-start(bf16[1,2,1,72,1152]{4,3,0,1,2:T(8,128)(2,1)S(1)} %fusion.177), channel_id=1, source_target_pairs={{0,1},{1,0},{2,3},{3,2},{4,5},{5,4},{6,7},{7,6},{8,9},{9,8},{10,11... | collective-permute-start | bytes 995336 | tf_op jit(solution)/shard_map/ppermute | solution.py:442
  525.4 8.1 %collective-permute-start.41 = (f32[6,1152]{1,0:T(8,128)S(1)}, f32[6,1152]{1,0:T(8,128)S(1)}, u32[]{:S(2)}, u32[]{:S(2)}) collective-permute-start(f32[6,1152]{1,0:T(8,128)S(1)} %add.502), channel_id=1, source_target_pairs={{0,8},{4,12},{8,0},{12,4},{16,24},{20,28},{24,16},{28,20},{1,9},{5... | collective-permute-start | bytes 82952 | tf_op jit(solution)/shard_map/ppermute | solution.py:427
  531.7 8.0 %collective-permute-start.48 = (bf16[1,2,2,72,1152]{4,3,2,1,0:T(8,128)(2,1)S(1)}, bf16[1,2,2,72,1152]{4,3,2,1,0:T(8,128)(2,1)S(1)}, u32[]{:S(2)}, u32[]{:S(2)}) collective-permute-start(bf16[1,2,2,72,1152]{4,3,2,1,0:T(8,128)(2,1)S(1)} %fusion.39), channel_id=1, source_target_pairs={{0,1},{1,0},{2,3},{3,2},{4,5},{5,4},{6,7},{7,6},{8,9},{9,8},{10,11... | collective-permute-start | bytes 1990664 | tf_op jit(solution)/shard_map/ppermute | solution.py:442
  (87 other events, 1038.4 us)
Sparse Core Ops, SparseCore 0:
  43.8 68.2 all-gather.2
  114.0 40.7 all-gather.4
  305.9 83.2 reduce-scatter.2
  395.6 68.9 reduce-scatter.4

commit v3 on v2

--- a/solution.py
+++ b/solution.py
@@ -1,3 +1,5 @@
+import functools
+
 import jax
 import jax.numpy as jnp
 from jax import lax
@@ -6,7 +8,7 @@
 from jax.sharding import PartitionSpec as P
 
 LANES = 128
-VMEM_GRANT = 60 << 20
+VMEM_GRANT = 40 << 20
 ROWS = 8
 
 def wide(tile, width):
@@ -222,7 +224,7 @@
 def conv_backward(
     d_drive_ref, delta_ref, d_scanned_ref, inner_ref, d_gate_ref, d_proj_ref, normed_ref,
     masks_ref, conv_ref, xproj_ref, in_ref, d_dt_ref, dt_ref, rows_ref,
-    term_ref, d_normed_ref, small_ref,
+    term_ref, d_normed_ref,
 ):
     taps = masks_ref.shape[1]
     model = normed_ref.shape[1]
@@ -258,15 +260,15 @@
     )
     columns = product(rows, same.astype(jnp.bfloat16), ((0,), (0,)))
     conv_low = (total * chance).astype(jnp.bfloat16)
-    edge = d_proj_ref.shape[1]
+    edge = model + d_proj_ref.shape[1]
     middle = edge + dt_ref.shape[1]
-    small_ref[:, :edge] = product(conv_low, d_proj_ref[...], ((0,), (0,))).astype(jnp.bfloat16)
-    small_ref[:, edge:middle] = product(d_dt_ref[...], dt_ref[...], ((0,), (0,))).astype(
+    term_ref[:, model:edge] = product(conv_low, d_proj_ref[...], ((0,), (0,))).astype(jnp.bfloat16)
+    term_ref[:, edge:middle] = product(d_dt_ref[...], dt_ref[...], ((0,), (0,))).astype(
         jnp.bfloat16
     )
-    small_ref[:, middle:] = columns.astype(jnp.bfloat16)
+    term_ref[:, middle:] = columns.astype(jnp.bfloat16)
     d_inner = d_inner.astype(jnp.bfloat16)
-    term_ref[...] = product(d_inner, normed_ref[...], ((0,), (0,))).astype(jnp.bfloat16)
+    term_ref[:, :model] = product(d_inner, normed_ref[...], ((0,), (0,))).astype(jnp.bfloat16)
     d_normed = product(d_inner, in_ref[:, :model], ((1,), (0,))) + product(
         d_gate_ref[...], in_ref[:, model:], ((1,), (0,))
     )
@@ -328,14 +330,12 @@
             pl.BlockSpec((more_rows.shape[0], width), lambda c: (0, c)),
         ],
         out_specs=[
-            pl.BlockSpec((width, model), lambda c: (c, 0)),
+            pl.BlockSpec((width, model + small_width), lambda c: (c, 0)),
             pl.BlockSpec((count, model), lambda c: (0, 0)),
-            pl.BlockSpec((width, small_width), lambda c: (c, 0)),
         ],
         out_shape=[
-            jax.ShapeDtypeStruct((channels, model), jnp.bfloat16),
+            jax.ShapeDtypeStruct((channels, model + small_width), jnp.bfloat16),
             jax.ShapeDtypeStruct((count, model), jnp.float32),
-            jax.ShapeDtypeStruct((channels, small_width), jnp.bfloat16),
         ],
         cost_estimate=pl.CostEstimate(flops=count, transcendentals=0, bytes_accessed=count),
         compiler_params=pltpu.CompilerParams(vmem_limit_bytes=VMEM_GRANT),
@@ -358,6 +358,84 @@
     )
 
 
+GELU_SCALE = 0.7978845608028654
+GELU_CUBE = 0.044715
+
+
+def expert_pass(pieces, blocks, *refs):
+    piece_refs, block_refs = refs[:pieces], refs[pieces : pieces + blocks]
+    refs = refs[pieces + blocks :]
+    result_refs, (rows_ref, active_ref, d_hidden_ref) = refs[:pieces], refs[pieces : pieces + 3]
+    total_ref, held_ref, sems = refs[pieces + 3 :]
+    copies = [
+        pltpu.make_async_copy(block_refs[k], held_ref.at[k], sems.at[k]) for k in range(blocks)
+    ]
+    for copy in copies:
+        copy.start()
+    length = piece_refs[0].shape[0]
+    for n in range(pieces):
+        rows_ref[n * length : (n + 1) * length, :] = piece_refs[n][...]
+    model = rows_ref.shape[1] // 2
+    units = held_ref.shape[1] // 2
+    slot_rows, d_returned = rows_ref[:, :model], rows_ref[:, model:]
+    for k in range(blocks):
+        copies[k].wait()
+        up, down = held_ref[k, :units, :], held_ref[k, units:, :]
+        hidden = product(slot_rows, up, ((1,), (1,)))
+        square = hidden * hidden
+        bend = jnp.tanh(GELU_SCALE * (hidden + GELU_CUBE * (square * hidden)))
+        share = 0.5 * (1.0 + bend)
+        active = (hidden * share).astype(jnp.bfloat16)
+        slope = share + hidden * (0.5 * GELU_SCALE) * (1.0 - bend * bend) * (
+            1.0 + 3.0 * GELU_CUBE * square
+        )
+        d_active = product(d_returned, down, ((1,), (1,)))
+        d_hidden = (d_active * slope).astype(jnp.bfloat16)
+        active_ref[:, k * units : (k + 1) * units] = active
+        d_hidden_ref[:, k * units : (k + 1) * units] = d_hidden
+        returned = product(active, down, ((1,), (0,)))
+        d_slots = product(d_hidden, up, ((1,), (0,)))
+        if k:
+            returned = returned + total_ref[:, :model]
+            d_slots = d_slots + total_ref[:, model:]
+        if k < blocks - 1:
+            total_ref[:, :model] = returned
+            total_ref[:, model:] = d_slots
+        else:
+            for n in range(pieces):
+                part = slice(n * length, (n + 1) * length)
+                result_refs[n][:, :model] = returned[part].astype(jnp.bfloat16)
+                result_refs[n][:, model:] = d_slots[part].astype(jnp.bfloat16)
+
+
+def run_expert(pieces, blocks):
+    length, width = pieces[0].shape
+    rows = length * len(pieces)
+    units = blocks[0].shape[0] // 2
+    low = jnp.bfloat16
+    vmem = pl.BlockSpec(memory_space=pltpu.VMEM)
+    out = pl.pallas_call(
+        functools.partial(expert_pass, len(pieces), len(blocks)),
+        in_specs=[vmem] * len(pieces) + [pl.BlockSpec(memory_space=pl.ANY)] * len(blocks),
+        out_specs=[vmem] * (len(pieces) + 3),
+        out_shape=[jax.ShapeDtypeStruct((length, width), low)] * len(pieces)
+        + [
+            jax.ShapeDtypeStruct((rows, width), low),
+            jax.ShapeDtypeStruct((rows, units * len(blocks)), low),
+            jax.ShapeDtypeStruct((rows, units * len(blocks)), low),
+        ],
+        scratch_shapes=[
+            pltpu.VMEM((rows, width), jnp.float32),
+            pltpu.VMEM((len(blocks),) + blocks[0].shape, low),
+            pltpu.SemaphoreType.DMA((len(blocks),)),
+        ],
+        cost_estimate=pl.CostEstimate(flops=rows, transcendentals=0, bytes_accessed=rows),
+        compiler_params=pltpu.CompilerParams(vmem_limit_bytes=VMEM_GRANT),
+        name="expert_pass",
+    )(*pieces, *blocks)
+    return out[: len(pieces)], out[len(pieces) :]
+
+
 HIGHEST = lax.Precision.HIGHEST
 EPSILON = 1e-05
 LOG2E = 1.4426950408889634
@@ -521,24 +599,30 @@
 
 
 def small_gather(block):
-    cube = yield from cube_stages_gather(block)
-    places = yield from far_gather(cube)
-    width = block.shape[1]
-    places = places.reshape(-1, 2, 2, lax.axis_size("expert"), block.shape[0], width)
-    return places.transpose(1, 3, 0, 2, 4, 5).reshape(-1, width)
+    block = yield from far_and_pair(block)
+    return (yield from cube_stages_gather(block.reshape(-1, block.shape[-1])))
 
 
 def add_low(kept, moved):
     return (kept.astype(jnp.float32) + moved.astype(jnp.float32)).astype(LOW)
 
 
-def far_sum(blocks):
+def far_sum(blocks, more=None):
     ring = mesh_rings()[0]
-    moved = yield tuple(
-        ring.hop(block_of(blocks, (ring.place + distance) % ring.size, 0)[0], distance)
-        for distance in range(1, ring.size)
-    )
-    total = block_of(blocks, ring.place, 0)[0].astype(jnp.float32)
+
+    def block(distance):
+        place = (ring.place + distance) % ring.size
+        if more is None:
+            return block_of(blocks, place, 0)[0]
+        middle = ring.size // 2
+        return jnp.where(
+            place < middle,
+            block_of(blocks, place % middle, 0)[0],
+            block_of(more, place % middle, 0)[0],
+        )
+
+    moved = yield tuple(ring.hop(block(distance), distance) for distance in range(1, ring.size))
+    total = block(0).astype(jnp.float32)
     for part in moved:
         total = total + part.astype(jnp.float32)
     return total.astype(LOW)
@@ -549,18 +633,23 @@
     count = len(blocks)
     travelling = blocks[1 % count]
     for step in range(2, count + 1):
-        moved = yield ring.hop(travelling.astype(LOW))
+        travelling = yield travelling.astype(LOW)
+        moved = yield ring.hop(travelling)
         travelling = blocks[step % count].astype(jnp.float32) + moved.astype(jnp.float32)
     return travelling
 
 
-def butterfly(values):
-    for axis_name in ("expert", "dp"):
-        distance = 1
-        while distance < lax.axis_size(axis_name):
-            values = values + (yield hop(values, (axis_name, distance)))
-            distance *= 2
+def butterfly(values, axis_name, first, last):
+    distance = first
+    while distance < last:
+        values = values + (yield hop(values, (axis_name, distance)))
+        distance *= 2
     return values
+
+
+def near_sum(values):
+    values = yield from butterfly(values, "expert", 1, lax.axis_size("expert"))
+    return (yield from butterfly(values, "dp", 1, 2))
 
 
 def shared_rows(values):
@@ -681,14 +770,14 @@
     in_blocks = streams.done["in"].reshape(2, -1, model_width)
     with jax.named_scope("fetch_in"):
         in_cube = cube_gather(jnp.concatenate([in_blocks[0], in_blocks[1]], axis=1))
+    expert_block = jnp.concatenate([up_weight[0], down_weight[0]], axis=0)
+    expert_block = lax.optimization_barrier((expert_block, in_blocks))[0]
+    streams.start("expert", ring_blocks(expert_block))
+    for _ in range(3):
+        streams.advance(("small",))
     out_block = part_rows(out_weight, expert_index * channels, channels)
-    out_block = lax.optimization_barrier((out_block, in_blocks))[0]
+    out_block = streams.advance(("small", "expert"), out_block)
     streams.start("out", far_and_pair(out_block))
-    for _ in range(steps - 2):
-        streams.advance(("out", "small"))
-    expert_block = jnp.concatenate([up_weight[0], down_weight[0]], axis=0)
-    expert_block = streams.advance(("out", "small"), expert_block)
-    streams.start("expert", ring_blocks(expert_block))
     streams.finish(("out", "small"))
     with jax.named_scope("fetch_out"):
         out_full = cube_gather(streams.done["out"].reshape(-1, model_width))
@@ -722,16 +811,8 @@
         route_rows ^ expert_index.astype(jnp.int32), expert_count, capacity, padded_capacity
     )
     in_cube, conv_rows, mask_columns, xproj_full, dtproj_full, rate_two, placed, dtb_full = (
-        streams.advance(
-            ("expert",),
-            in_cube,
-            conv_rows,
-            mask_columns,
-            xproj_full,
-            dtproj_full,
-            rate_two,
-            placed,
-            dtb_full,
+        lax.optimization_barrier(
+            (in_cube, conv_rows, mask_columns, xproj_full, dtproj_full, rate_two, placed, dtb_full)
         )
     )
     inner_full = in_cube[:, :model_width]
@@ -811,57 +892,42 @@
         ]
 
     units = up_weight.shape[1]
-    up_terms = [0.0] * steps
-    down_terms = [0.0] * steps
-    kept = []
-    sums = [[0.0, 0.0], [0.0, 0.0]]
-
-    def expert_block(cross, k, rows, block):
-        up, down = block[:units], block[units:]
-        slot_rows, d_returned = rows[:, :model_width], rows[:, model_width:]
-        hidden = dot(slot_rows, up, ((1,), (1,)))
-        active, gelu_pull = jax.vjp(gelu_tanh, hidden)
-        active_low = active.astype(LOW)
-        d_active = dot(d_returned, down, ((1,), (1,)))
-        d_hidden_low = gelu_pull(d_active)[0].astype(LOW)
-        sums[cross][0] = sums[cross][0] + dot(active_low, down, ((1,), (0,)))
-        sums[cross][1] = sums[cross][1] + dot(d_hidden_low, up, ((1,), (0,)))
-        kept.append((k, active_low, d_hidden_low, slot_rows, d_returned))
-
     while len(streams.blocks) < steps - 1:
         streams.advance(("expert",))
-    groups = [jnp.concatenate(received[0], axis=0), None]
-    early = list(enumerate(streams.blocks[: steps - 1]))
-    for k, block in early:
-        expert_block(0, k, groups[0], block)
-    sums[0], cross_pieces = lax.optimization_barrier((sums[0], received[1]))
-    groups[1] = jnp.concatenate(cross_pieces, axis=0)
-    for k, block in early:
-        expert_block(1, k, groups[1], block)
-    sums = list(streams.advance(("expert",), *sums))
-    last = steps - 1
-    for cross in (1, 0):
-        expert_block(cross, last, groups[cross], streams.done["expert"][last])
+    received[0] = list(streams.advance(("expert",), *received[0]))
+    blocks = streams.done["expert"]
+    own_results, own_kept = run_expert(received[0], blocks)
+    cross_results, cross_kept = run_expert(received[1], blocks)
     results = [
-        jnp.concatenate([returned.astype(LOW), d_slots.astype(LOW)], axis=1).reshape(
-            expert_count, sequences, padded_capacity, 2 * model_width
-        )
-        for returned, d_slots in sums
+        [piece.reshape(sequences, padded_capacity, 2 * model_width) for piece in group]
+        for group in (own_results, cross_results)
     ]
+    kept = [own_kept, cross_kept]
+    kept, results = lax.optimization_barrier((kept, results))
     with jax.named_scope("send_results"):
         arrived = [
             [exchange(results[cross][k], cross, k) for k in range(expert_count)]
             for cross in (0, 1)
         ]
-    for k, active_low, d_hidden_low, slot_rows, d_returned in kept:
-        down_terms[k] = down_terms[k] + dot(active_low, d_returned, ((0,), (0,)))
-        up_terms[k] = up_terms[k] + dot(d_hidden_low, slot_rows, ((0,), (0,)))
+    kept, arrived[0] = lax.optimization_barrier((kept, arrived[0]))
+    up_terms = [0.0] * steps
+    down_terms = [0.0] * steps
+    for rows, active_rows, d_hidden_rows in kept:
+        for k in range(steps):
+            part = slice(k * units, (k + 1) * units)
+            up_terms[k] = up_terms[k] + dot(
+                d_hidden_rows[:, part], rows[:, :model_width], ((0,), (0,))
+            )
+            down_terms[k] = down_terms[k] + dot(
+                active_rows[:, part], rows[:, model_width:], ((0,), (0,))
+            )
     terms = [
         jnp.concatenate([up.astype(LOW), down.astype(LOW)], axis=0)
         for up, down in zip(up_terms, down_terms)
     ]
-    terms, arrived = lax.optimization_barrier((terms, arrived))
+    terms, arrived[1] = lax.optimization_barrier((terms, arrived[1]))
     streams.start("expert_grad", ring_sum(terms))
+    streams.advance(("expert_grad",))
     gathered_both = 0.0
     for k in range(expert_count):
         total = (arrived[0][k].astype(jnp.float32) + arrived[1][k].astype(jnp.float32)).astype(LOW)
@@ -889,6 +955,7 @@
         decay, drive, b_wide, c_wide, rate_two, d_scanned
     )
     d_drive = streams.advance(("expert_grad",), d_drive)
+    streams.advance(("expert_grad",))
     d_skip = jnp.sum(d_scanned * conv_out, axis=(0, 1))
     d_alog = jnp.sum(d_rate, axis=0) * rate
     d_delta = d_decay * (1.0 / LOG2E) + d_drive * conv_out
@@ -906,7 +973,7 @@
     ).astype(LOW)
     more_rows = jnp.concatenate([d_alog, d_dtb[None], d_skip[None]], axis=0)
     more_rows = jnp.pad(more_rows, ((0, -more_rows.shape[0] % ROWS), (0, 0)))
-    inner_term, d_normed, small_term = run_conv_backward(
+    inner_term, d_normed = run_conv_backward(
         flat(d_drive),
         flat(delta),
         flat(d_scanned),
@@ -922,21 +989,11 @@
         dt_low,
         more_rows,
     )
-    inner_term, d_normed, small_term = streams.advance(
-        ("expert_grad",), inner_term, d_normed, small_term
+    inner_term, d_normed, out_gate_blocks = streams.advance(
+        ("expert_grad",), inner_term, d_normed, out_gate_blocks
     )
     with jax.named_scope("reduce_inner"):
         inner_blocks = cube_scatter(inner_term)
-    with jax.named_scope("reduce_small"):
-        small_width = small_term.shape[1]
-        pieces = small_term.reshape(2, expert_devices, steps // 2, 2, channels, small_width)
-        pieces = lax.all_to_all(
-            pieces.transpose(2, 0, 3, 1, 4, 5).reshape(devices, channels, small_width),
-            BOTH,
-            split_axis=0,
-            concat_axis=0,
-            tiled=True,
-        )
     out_blocks = out_gate_blocks[:, :model_width]
     gate_blocks = out_gate_blocks[:, model_width:]
     streams.start(
@@ -946,23 +1003,36 @@
     input_grad = d_residual + d_rows_norm
 
     gains = jnp.concatenate([d_gain_one[None], d_gain_two[None], d_router.T], axis=0)
-    streams.start("gains", butterfly(gains))
-    streams.advance(("out_grad", "gains"))
-    streams.advance(("gains", "expert_grad"))
+    streams.start("gains", near_sum(gains))
+    streams.advance(("out_grad",))
     streams.finish(("out_grad",))
-    streams.start("out_rows", shared_rows(streams.done["out_grad"][None]))
-    streams.finish(("gains", "out_rows", "expert_grad"))
-    in_places = jnp.concatenate([inner_blocks, gate_blocks], axis=0)
-    streams.start("in_grad", far_sum(in_places.reshape(steps, 2, channels, model_width)))
-    pieces = streams.advance(("in_grad",), pieces)
+    out_part = streams.advance(("expert_grad",), streams.done["out_grad"])
+    streams.finish(("gains",))
+    gains = streams.done["gains"]
+    inner_blocks = streams.advance(("expert_grad",), inner_blocks)
+    half = (steps // 2, 2, channels, model_width)
+    streams.start(
+        "in_grad",
+        far_sum(inner_blocks[:, :model_width].reshape(half), gate_blocks.reshape(half)),
+    )
+    small_blocks = inner_blocks[:, model_width:]
+    streams.start(
+        "small_grad",
+        far_and_pair_sum(small_blocks.reshape(-1, 2, channels, small_blocks.shape[1])),
+    )
+    streams.advance(("small_grad",))
+    streams.start("out_rows", shared_rows(out_part[None]))
+    gains = streams.advance(("in_grad",), gains)
     streams.start("in_rows", shared_rows(streams.done["in_grad"]))
-    streams.finish(("in_rows",))
+    streams.start("gains", butterfly(gains, "dp", 2, dp_devices))
+    streams.advance(("in_rows", "out_rows", "gains"))
+    streams.finish(("in_rows", "out_rows", "gains", "small_grad", "expert_grad"))
+    gains = streams.done["gains"]
     in_grad = streams.done["in_rows"].reshape(in_weight.shape).astype(jnp.float32)
     out_grad = streams.done["out_rows"][0].astype(jnp.float32)
     expert_grad = streams.done["expert_grad"].astype(jnp.float32)
     up_grad, down_grad = expert_grad[:units], expert_grad[units:]
-    gains = streams.done["gains"]
-    small_grad = jnp.sum(pieces.astype(jnp.float32), axis=0)
+    small_grad = streams.done["small_grad"].astype(jnp.float32)
     xproj_grad = small_grad[:, :xproj_width]
     row_grads = small_grad[:, xproj_width:].T
     dtproj_grad = row_grads[:rank]

time: 556 us -> 513 us (0.923)
  matrix products: 66.8 us -> 27.3 us
  local copies, waits for them, and re-layouts: 51.8 us -> 68.9 us
  other arithmetic: 59.5 us -> 51.2 us
  waiting for transfers between devices: 211 us -> 203 us
  starting transfers between devices: 71.1 us -> 64.8 us
    ppermute x30 -> x35, waiting for transfers between devices: 121 us -> 178 us  [hop(): return lax.ppermute(values, self.axis_name, pairs)]
    reduce_scatter x2, waiting for transfers between devices: 48.1 us -> 0.01 us  [cube_scatter(): lax.psum_scatter(total, BOTH, scatter_dimension=0, tiled=True, axis_index...]
    dot_general x54 -> x22, matrix products: 59.9 us -> 21.5 us  [dot(): lax.dot_general(left, right, (contract, ((), ())), preferred_element_type...]
    unnamed x189 -> x263, local copies, waits for them, and re-layouts: 14 us -> 36.3 us
    ppermute x14, waiting for transfers between devices: 39.5 us -> 18.9 us  [exchange(): return lax.ppermute(piece, BOTH, partners(cross, k))]
    pallas_call x0 -> x2, Pallas kernels: none -> 13.3 us  [run_expert(): pl.pallas_call(functools.partial(expert_pass, len(pieces), len(blocks)),...]
    ppermute x30 -> x35, starting transfers between devices: 44.9 us -> 35.6 us  [hop(): return lax.ppermute(values, self.axis_name, pairs)]
  transfers between devices with their start and end apart: 54 -> 58, of which waited for: 28 -> 29; matrix products, arithmetic and copies ran while one was open for 27% -> 20% of each run, Pallas kernels for 11% -> 12%
where the time goes in v3:
time: 513 us; the launch traced here: 506 us
  waiting for transfers between devices  203 us (40%)
  Pallas kernels  74.7 us (15%)
  local copies, waits for them, and re-layouts  68.9 us (13%)
  starting transfers between devices  64.8 us (13%)
  other arithmetic  51.2 us (10%)
  matrix products  27.3 us (5%)
  between operations  16.2 us (3%)
    ppermute x35, waiting for transfers between devices, hop(): return lax.ppermute(values, self.axis_name, pairs)  178 us
    unnamed x263, local copies, waits for them, and re-layouts  36.3 us
    ppermute x35, starting transfers between devices, hop(): return lax.ppermute(values, self.axis_name, pairs)  35.6 us
    pallas_call x1, Pallas kernels, run_backward(): pl.pallas_call(scan_backward, grid=(count, channels // width), in_specs=[...  28.6 us
    dot_general x22, matrix products, dot(): lax.dot_general(left, right, (contract, ((), ())), preferred_element_type...  21.5 us
    ppermute x14, waiting for transfers between devices, exchange(): return lax.ppermute(piece, BOTH, partners(cross, k))  18.9 us
    ppermute x14, starting transfers between devices, exchange(): return lax.ppermute(piece, BOTH, partners(cross, k))  17.8 us
    pallas_call x1, Pallas kernels, run_conv_backward(): pl.pallas_call(conv_backward, grid=(channels // width,), in_specs=[tokens...  13.5 us
  transfers between devices with their start and end apart: 58, of which 29 were waited for; matrix products, arithmetic and copies ran while one was open for 20% of the time, Pallas kernels for 12%

profile of v3, /device:TPU:0, one launch (start us, length us, event | category | flops | bytes accessed | tf_op | source)
XLA Modules:
  0.0 505.6 jit_solution(287929455761899423)
XLA Ops:
  8.5 3.1 collective-permute-start
  18.8 4.2 collective-permute-done.1
  24.4 9.7 %collective-permute-done.3 = bf16[1,72,199]{2,1,0:T(8,128)(2,1)S(1)} collective-permute-done((bf16[1,72,199]{2,1,0:T(8,128)(2,1)S(1)}, bf16[1,72,199]{2,1,0:T(8,128)(2,1)S(1)}, u32[]{:S(2)}, u32[]{:S(2)}) %collective-permute-start.3) | collective-permute-done | bytes 28688 | tf_op jit(solution)/shard_map/ppermute | solution.py:520
  34.3 10.1 %collective-permute-done.5 = bf16[1,72,199]{2,1,0:T(8,128)(2,1)S(1)} collective-permute-done((bf16[1,72,199]{2,1,0:T(8,128)(2,1)S(1)}, bf16[1,72,199]{2,1,0:T(8,128)(2,1)S(1)}, u32[]{:S(2)}, u32[]{:S(2)}) %collective-permute-start.5) | collective-permute-done | bytes 28688 | tf_op jit(solution)/shard_map/ppermute | solution.py:520
  54.3 4.1 collective-permute-done.6
  61.7 14.4 %collective-permute-done.8 = bf16[1,576,199]{2,1,0:T(8,128)(2,1)S(1)} collective-permute-done((bf16[1,576,199]{2,1,0:T(8,128)(2,1)S(1)}, bf16[1,576,199]{2,1,0:T(8,128)(2,1)S(1)}, u32[]{:S(2)}, u32[]{:S(2)}) %collective-permute-start.8) | collective-permute-done | bytes 229280 | tf_op jit(solution)/shard_map/ppermute | solution.py:520
  80.1 6.5 %collective-permute-done.10.refs_5_ = bf16[768,1152]{1,0:T(8,128)(2,1)} collective-permute-done((bf16[768,1152]{1,0:T(8,128)(2,1)S(1)}, bf16[768,1152]{1,0:T(8,128)(2,1)}, u32[]{:S(2)}, u32[]{:S(2)}) %collective-permute-start.10) | collective-permute-done | bytes 1769504 | tf_op jit(solution)/shard_map/ppermute | solution.py:520
  86.7 10.4 %collective-permute-done.9 = bf16[1,1152,199]{1,2,0:T(8,128)(2,1)S(1)} collective-permute-done((bf16[1,1152,199]{1,2,0:T(8,128)(2,1)}, bf16[1,1152,199]{1,2,0:T(8,128)(2,1)S(1)}, u32[]{:S(2)}, u32[]{:S(2)}) %collective-permute-start.9) | collective-permute-done | bytes 458528 | tf_op jit(solution)/shard_map/ppermute | solution.py:520
  97.9 6.9 %collective-permute-done.12 = bf16[1,72,1152]{2,1,0:T(8,128)(2,1)S(1)} collective-permute-done((bf16[1,72,1152]{2,1,0:T(8,128)(2,1)S(1)}, bf16[1,72,1152]{2,1,0:T(8,128)(2,1)S(1)}, u32[]{:S(2)}, u32[]{:S(2)}) %collective-permute-start.12) | collective-permute-done | bytes 165920 | tf_op jit(solution)/shard_map/ppermute | solution.py:520
  105.4 8.3 %collective-permute-done.13 = bf16[1,72,1152]{2,1,0:T(8,128)(2,1)S(1)} collective-permute-done((bf16[1,72,1152]{2,1,0:T(8,128)(2,1)S(1)}, bf16[1,72,1152]{2,1,0:T(8,128)(2,1)S(1)}, u32[]{:S(2)}, u32[]{:S(2)}) %collective-permute-start.13) | collective-permute-done | bytes 165920 | tf_op jit(solution)/shard_map/ppermute | solution.py:520
  113.7 7.1 %collective-permute-done.14 = bf16[1,72,1152]{2,1,0:T(8,128)(2,1)S(1)} collective-permute-done((bf16[1,72,1152]{2,1,0:T(8,128)(2,1)S(1)}, bf16[1,72,1152]{2,1,0:T(8,128)(2,1)S(1)}, u32[]{:S(2)}, u32[]{:S(2)}) %collective-permute-start.14) | collective-permute-done | bytes 165920 | tf_op jit(solution)/shard_map/ppermute | solution.py:520
  121.2 2.2 collective-permute-start.15
  124.6 4.0 collective-permute-done.15
  128.6 2.1 maximum_select_fusion
  139.3 4.2 fusion.2.inner_ref
  145.5 2.4 compare_select_fusion
  151.0 11.3 %scan_forward.1 = f32[2,96,2304]{2,1,0:T(8,128)S(1)} custom-call(f32[2,96,2304]{2,1,0:T(8,128)S(1)} %get-tuple-element.340.decay_ref, f32[2,96,2304]{2,1,0:T(8,128)S(1)} %get-tuple-element.339.drive_ref, f32[2,96,16,128]{3,2,1,0:T(8,128)S(1)} %broadcast_in_dim.114.b_ref, f32[2,96,16,128]{3,2,1,0:T(8,128)S(1)} %broadcast_in_dim.116.c_ref, ...), custom_call_target="tpu_custom_call" | custom-call | flops 442368 | bytes 8454144 | tf_op jit(solution)/shard_map/scan_forward/pallas_call | solution.py:142
  162.3 11.9 %collective-permute-done.11.refs_6_ = bf16[768,1152]{1,0:T(8,128)(2,1)} collective-permute-done((bf16[768,1152]{1,0:T(8,128)(2,1)}, bf16[768,1152]{1,0:T(8,128)(2,1)}, u32[]{:S(2)}, u32[]{:S(2)}) %collective-permute-start.11) | collective-permute-done | bytes 1769504 | tf_op jit(solution)/shard_map/ppermute | solution.py:520
  179.7 4.3 multiply_reduce_fusion.5
  191.7 5.4 %collective-permute-done.18 = bf16[2,32,2304]{2,1,0:T(8,128)(2,1)S(1)} collective-permute-done((bf16[2,32,2304]{2,1,0:T(8,128)(2,1)S(1)}, bf16[2,32,2304]{2,1,0:T(8,128)(2,1)S(1)}, u32[]{:S(2)}, u32[]{:S(2)}) %collective-permute-start.18) | collective-permute-done | bytes 294944 | tf_op jit(solution)/shard_map/send_rows/ppermute | solution.py:882
  197.1 2.8 collective-permute-start.22
  199.9 2.9 collective-permute-done.19
  202.8 2.8 collective-permute-start.23
  205.6 6.4 %collective-permute-done.16.refs_7_ = bf16[768,1152]{1,0:T(8,128)(2,1)} collective-permute-done((bf16[768,1152]{1,0:T(8,128)(2,1)}, bf16[768,1152]{1,0:T(8,128)(2,1)}, u32[]{:S(2)}, u32[]{:S(2)}) %collective-permute-start.16) | collective-permute-done | bytes 1769504 | tf_op jit(solution)/shard_map/ppermute | solution.py:520
  212.1 6.6 %expert_pass.2 = (bf16[64,2304]{1,0:T(8,128)(2,1)S(1)}, bf16[64,2304]{1,0:T(8,128)(2,1)S(1)}, bf16[64,2304]{1,0:T(8,128)(2,1)S(1)}, bf16[64,2304]{1,0:T(8,128)(2...) custom-call(bf16[64,2304]{1,0:T(8,128)(2,1)S(1)} %bitcast.192, ...), custom_call_target="tpu_custom_call" | custom-call | flops 256 | bytes 256 | tf_op jit(solution)/shard_map/expert_pass/pallas_call | solution.py:417
  218.7 6.8 %expert_pass.3 = (bf16[64,2304]{1,0:T(8,128)(2,1)S(1)}, bf16[64,2304]{1,0:T(8,128)(2,1)S(1)}, bf16[64,2304]{1,0:T(8,128)(2,1)S(1)}, bf16[64,2304]{1,0:T(8,128)(2...) custom-call(bf16[64,2304]{1,0:T(8,128)(2,1)S(1)} %bitcast.195, ...), custom_call_target="tpu_custom_call" | custom-call | flops 256 | bytes 256 | tf_op jit(solution)/shard_map/expert_pass/pallas_call | solution.py:417
  225.6 3.1 collective-permute-start.25
  230.3 2.2 collective-permute-start.29
  232.6 4.0 collective-permute-done.25
  237.7 4.7 collective-permute-done.26
  265.0 8.0 %gate_backward.1 = (bf16[2304,2304]{1,0:T(8,128)(2,1)}, bf16[192,2304]{1,0:T(8,128)(2,1)S(1)}, f32[192,2304]{1,0:T(8,128)S(1)}) custom-call(bf16[192,1152]{1,0:T(8,128)(2,1)S(1)} %fusion.128.d_branch_ref, bf16[192,1152]{1,0:T(8,128)(2,1)S(1)} %copy-done.18, bf16[2304,1152]{1,0:T(8,128)(2,1)S(1)} %bitcast.189, bf16[192,2304]{1,0:T(8,128)(2,1)S(1)} %bitcast.191, ...), custom_call_target="tpu_custom_call" | custom-call | flops 192 | bytes 192 | tf_op jit(solution)/shard_map/gate_backward/pallas_call | solution.py:208
  285.2 28.6 %scan_backward.1 = (f32[2,96,2304]{2,1,0:T(8,128)S(1)}, f32[2,96,2304]{2,1,0:T(8,128)S(1)}, f32[2,16,2304]{2,1,0:T(8,128)S(1)}, f32[2,8,1536]{2,1,0:T(8,128)S(1)}, f32[2,8,1536]{2,1,0:T(8,128)S(1)}) custom-call(f32[2,96,2304]{2,1,0:T(8,128)S(1)} %copy-done.3, f32[2,96,2304]{2,1,0:T(8,128)S(1)} %get-tuple-element.339.drive_ref, ...), custom_call_target="tpu_custom_call" | custom-call | flops 442368 | bytes 15138816 | tf_op jit(solution)/shard_map/scan_backward/pallas_call | solution.py:163
  320.4 4.0 add_convert_fusion.1
  324.5 3.1 fusion.129
  338.7 13.5 %conv_backward.1 = (bf16[2304,1360]{1,0:T(8,128)(2,1)}, f32[192,1152]{1,0:T(8,128)S(1)}) custom-call(f32[192,2304]{1,0:T(8,128)S(1)} %bitcast.185, f32[192,2304]{1,0:T(8,128)S(1)} %copy-done.24, f32[192,2304]{1,0:T(8,128)S(1)} %get-tuple-element.194.d_scanned_ref, f32[192,2304]{1,0:T(8,128)S(1)} %copy-done.9, bf16[192,2304]{1,0:T(8,128)(2,1)S(1)} %copy-done.30, ...), custom_call_target="tpu_custom_call" | custom-call | flops 192 | bytes 192 | tf_op jit(solution)/shard_map/conv_backward/pallas_call | solution.py:313
  353.1 14.2 %collective-permute-done.32 = bf16[768,1152]{1,0:T(8,128)(2,1)} collective-permute-done((bf16[768,1152]{1,0:T(8,128)(2,1)}, bf16[768,1152]{1,0:T(8,128)(2,1)}, u32[]{:S(2)}, u32[]{:S(2)}) %collective-permute-start.32) | collective-permute-done | bytes 1769504 | tf_op jit(solution)/shard_map/ppermute | solution.py:520
  370.7 8.2 %collective-permute-done.33 = bf16[2,1,72,1152]{3,2,1,0:T(8,128)(2,1)S(1)} collective-permute-done((bf16[2,1,72,1152]{3,2,1,0:T(8,128)(2,1)S(1)}, bf16[2,1,72,1152]{3,2,1,0:T(8,128)(2,1)S(1)}, u32[]{:S(2)}, u32[]{:S(2)}) %collective-permute-start.33) | collective-permute-done | bytes 331808 | tf_op jit(solution)/shard_map/ppermute | solution.py:520
  383.1 3.1 add_convert_fusion
  388.2 4.7 collective-permute-done.35
  393.7 3.4 collective-permute-start.37
  401.3 3.1 collective-permute-done.42
  405.7 29.4 %collective-permute-done.37 = bf16[768,1152]{1,0:T(8,128)(2,1)} collective-permute-done((bf16[768,1152]{1,0:T(8,128)(2,1)}, bf16[768,1152]{1,0:T(8,128)(2,1)}, u32[]{:S(2)}, u32[]{:S(2)}) %collective-permute-start.37) | collective-permute-done | bytes 1769504 | tf_op jit(solution)/shard_map/ppermute | solution.py:520
  438.9 2.3 collective-permute-start.40
  446.0 3.2 collective-permute-done.38
  449.2 11.0 %collective-permute-done.39 = bf16[2,72,1152]{2,1,0:T(8,128)(2,1)S(1)} collective-permute-done((bf16[2,72,1152]{2,1,0:T(8,128)(2,1)S(1)}, bf16[2,72,1152]{2,1,0:T(8,128)(2,1)S(1)}, u32[]{:S(2)}, u32[]{:S(2)}) %collective-permute-start.39) | collective-permute-done | bytes 331808 | tf_op jit(solution)/shard_map/ppermute | solution.py:520
  466.8 7.6 %collective-permute-start.46 = (f32[6,1152]{1,0:T(8,128)}, f32[6,1152]{1,0:T(8,128)S(1)}, u32[]{:S(2)}, u32[]{:S(2)}) collective-permute-start(f32[6,1152]{1,0:T(8,128)} %add.451), channel_id=1, source_target_pairs={{0,8},{4,12},{8,0},{12,4},{16,24},{20,28},{24,16},{28,20},{1,9},{5... | collective-permute-start | bytes 82952 | tf_op jit(solution)/shard_map/ppermute | solution.py:505
  476.8 2.8 collective-permute-start.53
  496.3 2.4 fusion.36
  (511 shorter events, 161.9 us)
Async XLA Ops:
  7.2 132.1 %all-gather.3.cloned.1.call-start = ((), (), s32[]{:S(2)}) async-start(), calls=%async_computation.2 | async-start | bytes 11943936 | tf_op jit(solution)/shard_map/fetch_in/all_gather | solution.py:551
  8.5 14.4 %collective-permute-start = (bf16[1,144,1152]{2,1,0:T(8,128)(2,1)S(1)}, bf16[1,144,1152]{2,1,0:T(8,128)(2,1)S(1)}, u32[]{:S(2)}, u32[]{:S(2)}) collective-permute-start(bf16[1,144,1152]{2,1,0:T(8,128)(2,1)S(1)} %bitcast.239), channel_id=1, source_target_pairs={{0,8},{4,12},{8,16},{12,20},{16,24},{20,28},{24,0},{28,4},{1,9},{5... | collective-permute-start | bytes 995336 | tf_op jit(solution)/shard_map/ppermute | solution.py:520
  23.0 11.2 %collective-permute-start.2 = (bf16[1,144,1152]{2,1,0:T(8,128)(2,1)S(1)}, bf16[1,144,1152]{2,1,0:T(8,128)(2,1)S(1)}, u32[]{:S(2)}, u32[]{:S(2)}) collective-permute-start(bf16[1,144,1152]{2,1,0:T(8,128)(2,1)S(1)} %collective-permute-done), channel_id=1, source_target_pairs={{0,8},{4,12},{8,16},{12,20},{16,24},{20,28},{24,0},{28,4},{1,9},{5... | collective-permute-start | bytes 995336 | tf_op jit(solution)/shard_map/ppermute | solution.py:520
  23.0 11.1 %collective-permute-start.3 = (bf16[1,72,199]{2,1,0:T(8,128)(2,1)S(1)}, bf16[1,72,199]{2,1,0:T(8,128)(2,1)S(1)}, u32[]{:S(2)}, u32[]{:S(2)}) collective-permute-start(bf16[1,72,199]{2,1,0:T(8,128)(2,1)S(1)} %collective-permute-done.1), channel_id=1, source_target_pairs={{0,8},{4,12},{8,16},{12,20},{16,24},{20,28},{24,0},{28,4},{1,9},{5... | collective-permute-start | bytes 85976 | tf_op jit(solution)/shard_map/ppermute | solution.py:520
  34.1 10.2 %collective-permute-start.4 = (bf16[1,144,1152]{2,1,0:T(8,128)(2,1)S(1)}, bf16[1,144,1152]{2,1,0:T(8,128)(2,1)S(1)}, u32[]{:S(2)}, u32[]{:S(2)}) collective-permute-start(bf16[1,144,1152]{2,1,0:T(8,128)(2,1)S(1)} %collective-permute-done.2), channel_id=1, source_target_pairs={{0,8},{4,12},{8,16},{12,20},{16,24},{20,28},{24,0},{28,4},{1,9},{5... | collective-permute-start | bytes 995336 | tf_op jit(solution)/shard_map/ppermute | solution.py:520
  34.2 10.2 %collective-permute-start.5 = (bf16[1,72,199]{2,1,0:T(8,128)(2,1)S(1)}, bf16[1,72,199]{2,1,0:T(8,128)(2,1)S(1)}, u32[]{:S(2)}, u32[]{:S(2)}) collective-permute-start(bf16[1,72,199]{2,1,0:T(8,128)(2,1)S(1)} %collective-permute-done.3), channel_id=1, source_target_pairs={{0,8},{4,12},{8,16},{12,20},{16,24},{20,28},{24,0},{28,4},{1,9},{5... | collective-permute-start | bytes 85976 | tf_op jit(solution)/shard_map/ppermute | solution.py:520
  46.4 133.3 %all-gather.5.cloned.1.call-start = ((), (), s32[]{:S(2)}) async-start(), calls=%async_computation.3 | async-start | bytes 5971968 | tf_op jit(solution)/shard_map/fetch_out/all_gather | solution.py:551
  47.2 39.4 %collective-permute-start.10 = (bf16[768,1152]{1,0:T(8,128)(2,1)S(1)}, bf16[768,1152]{1,0:T(8,128)(2,1)}, u32[]{:S(2)}, u32[]{:S(2)}) collective-permute-start(bf16[768,1152]{1,0:T(8,128)(2,1)S(1)} %pad_maximum_fusion.refs_4_), channel_id=1, source_target_pairs={{0,8},{4,12},{8,16},{12,20},{16,24},{20,28},{24,0},{28,4},{1,9},{5... | collective-permute-start | bytes 5308424 | tf_op jit(solution)/shard_map/ppermute | solution.py:520
  60.1 16.0 %collective-permute-start.8 = (bf16[1,576,199]{2,1,0:T(8,128)(2,1)S(1)}, bf16[1,576,199]{2,1,0:T(8,128)(2,1)S(1)}, u32[]{:S(2)}, u32[]{:S(2)}) collective-permute-start(bf16[1,576,199]{2,1,0:T(8,128)(2,1)S(1)} %bitcast.242), channel_id=1, source_target_pairs={{0,2},{1,3},{2,0},{3,1},{4,6},{5,7},{6,4},{7,5},{8,10},{9,11},{10,... | collective-permute-start | bytes 687752 | tf_op jit(solution)/shard_map/ppermute | solution.py:520
  77.4 19.7 %collective-permute-start.9 = (bf16[1,1152,199]{1,2,0:T(8,128)(2,1)}, bf16[1,1152,199]{1,2,0:T(8,128)(2,1)S(1)}, u32[]{:S(2)}, u32[]{:S(2)}) collective-permute-start(bf16[1,1152,199]{1,2,0:T(8,128)(2,1)} %copy.113), channel_id=1, source_target_pairs={{0,4},{4,0},{8,12},{12,8},{16,20},{20,16},{24,28},{28,24},{1,5},{5... | collective-permute-start | bytes 1375496 | tf_op jit(solution)/shard_map/ppermute | solution.py:520
  97.1 7.7 %collective-permute-start.12 = (bf16[1,72,1152]{2,1,0:T(8,128)(2,1)S(1)}, bf16[1,72,1152]{2,1,0:T(8,128)(2,1)S(1)}, u32[]{:S(2)}, u32[]{:S(2)}) collective-permute-start(bf16[1,72,1152]{2,1,0:T(8,128)(2,1)S(1)} %bitcast.250), channel_id=1, source_target_pairs={{0,8},{4,12},{8,16},{12,20},{16,24},{20,28},{24,0},{28,4},{1,9},{5... | collective-permute-start | bytes 497672 | tf_op jit(solution)/shard_map/ppermute | solution.py:520
  104.8 8.9 %collective-permute-start.13 = (bf16[1,72,1152]{2,1,0:T(8,128)(2,1)S(1)}, bf16[1,72,1152]{2,1,0:T(8,128)(2,1)S(1)}, u32[]{:S(2)}, u32[]{:S(2)}) collective-permute-start(bf16[1,72,1152]{2,1,0:T(8,128)(2,1)S(1)} %collective-permute-done.12), channel_id=1, source_target_pairs={{0,8},{4,12},{8,16},{12,20},{16,24},{20,28},{24,0},{28,4},{1,9},{5... | collective-permute-start | bytes 497672 | tf_op jit(solution)/shard_map/ppermute | solution.py:520
  113.7 7.1 %collective-permute-start.14 = (bf16[1,72,1152]{2,1,0:T(8,128)(2,1)S(1)}, bf16[1,72,1152]{2,1,0:T(8,128)(2,1)S(1)}, u32[]{:S(2)}, u32[]{:S(2)}) collective-permute-start(bf16[1,72,1152]{2,1,0:T(8,128)(2,1)S(1)} %collective-permute-done.13), channel_id=1, source_target_pairs={{0,8},{4,12},{8,16},{12,20},{16,24},{20,28},{24,0},{28,4},{1,9},{5... | collective-permute-start | bytes 497672 | tf_op jit(solution)/shard_map/ppermute | solution.py:520
  121.2 7.4 %collective-permute-start.15 = (bf16[2,1,72,1152]{3,2,1,0:T(8,128)(2,1)S(1)}, bf16[2,1,72,1152]{3,2,1,0:T(8,128)(2,1)}, u32[]{:S(2)}, u32[]{:S(2)}) collective-permute-start(bf16[2,1,72,1152]{3,2,1,0:T(8,128)(2,1)S(1)} %get-tuple-element.355), channel_id=1, source_target_pairs={{0,4},{4,0},{8,12},{12,8},{16,20},{20,16},{24,28},{28,24},{1,5},{5... | collective-permute-start | bytes 995336 | tf_op jit(solution)/shard_map/ppermute | solution.py:520
  130.7 236.6 %reduce-scatter.3.cloned.1.call-start = ((), (), s32[]{:S(2)}) async-start(), calls=%async_computation.4 | async-start | bytes 11943936 | tf_op jit(solution)/shard_map/reduce_out_gate/reduce_scatter | solution.py:555
  136.8 37.3 %collective-permute-start.11 = (bf16[768,1152]{1,0:T(8,128)(2,1)}, bf16[768,1152]{1,0:T(8,128)(2,1)}, u32[]{:S(2)}, u32[]{:S(2)}) collective-permute-start(bf16[768,1152]{1,0:T(8,128)(2,1)} %collective-permute-done.10.refs_5_), channel_id=1, source_target_pairs={{0,8},{4,12},{8,16},{12,20},{16,24},{20,28},{24,0},{28,4},{1,9},{5... | collective-permute-start | bytes 5308424 | tf_op jit(solution)/shard_map/ppermute | solution.py:520
  174.2 37.9 %collective-permute-start.16 = (bf16[768,1152]{1,0:T(8,128)(2,1)}, bf16[768,1152]{1,0:T(8,128)(2,1)}, u32[]{:S(2)}, u32[]{:S(2)}) collective-permute-start(bf16[768,1152]{1,0:T(8,128)(2,1)} %collective-permute-done.11.refs_6_), channel_id=1, source_target_pairs={{0,8},{4,12},{8,16},{12,20},{16,24},{20,28},{24,0},{28,4},{1,9},{5... | collective-permute-start | bytes 5308424 | tf_op jit(solution)/shard_map/ppermute | solution.py:520
  187.2 9.9 %collective-permute-start.18 = (bf16[2,32,2304]{2,1,0:T(8,128)(2,1)S(1)}, bf16[2,32,2304]{2,1,0:T(8,128)(2,1)S(1)}, u32[]{:S(2)}, u32[]{:S(2)}) collective-permute-start(bf16[2,32,2304]{2,1,0:T(8,128)(2,1)S(1)} %convolution_convert_fusion.1), channel_id=1, source_target_pairs={{0,2},{1,3},{2,0},{3,1},{4,6},{5,7},{6,4},{7,5},{8,10},{9,11},{10,... | collective-permute-start | bytes 884744 | tf_op jit(solution)/shard_map/send_rows/ppermute | solution.py:882
  189.4 13.4 %collective-permute-start.19 = (bf16[2,32,2304]{2,1,0:T(8,128)(2,1)S(1)}, bf16[2,32,2304]{2,1,0:T(8,128)(2,1)S(1)}, u32[]{:S(2)}, u32[]{:S(2)}) collective-permute-start(bf16[2,32,2304]{2,1,0:T(8,128)(2,1)S(1)} %convolution_convert_fusion), channel_id=1, source_target_pairs={{0,3},{1,2},{2,1},{3,0},{4,7},{5,6},{6,5},{7,4},{8,11},{9,10},{10,... | collective-permute-start | bytes 884744 | tf_op jit(solution)/shard_map/send_rows/ppermute | solution.py:882
  189.6 29.1 %collective-permute-start.21 = (bf16[2,32,2304]{2,1,0:T(8,128)(2,1)S(1)}, bf16[2,32,2304]{2,1,0:T(8,128)(2,1)S(1)}, u32[]{:S(2)}, u32[]{:S(2)}) collective-permute-start(bf16[2,32,2304]{2,1,0:T(8,128)(2,1)S(1)} %convolution_convert_fusion.2), channel_id=1, source_target_pairs={{0,5},{1,4},{2,7},{3,6},{4,1},{5,0},{6,3},{7,2},{8,13},{9,12},{10,... | collective-permute-start | bytes 884744 | tf_op jit(solution)/shard_map/send_rows/ppermute | solution.py:882
  191.5 27.1 %collective-permute-start.20 = (bf16[2,32,2304]{2,1,0:T(8,128)(2,1)S(1)}, bf16[2,32,2304]{2,1,0:T(8,128)(2,1)S(1)}, u32[]{:S(2)}, u32[]{:S(2)}) collective-permute-start(bf16[2,32,2304]{2,1,0:T(8,128)(2,1)S(1)} %convolution_convert_fusion.3), channel_id=1, source_target_pairs={{0,4},{1,5},{2,6},{3,7},{4,0},{5,1},{6,2},{7,3},{8,12},{9,13},{10,... | collective-permute-start | bytes 884744 | tf_op jit(solution)/shard_map/send_rows/ppermute | solution.py:882
  197.1 21.6 %collective-permute-start.22 = (bf16[2,32,2304]{2,1,0:T(8,128)(2,1)S(1)}, bf16[2,32,2304]{2,1,0:T(8,128)(2,1)S(1)}, u32[]{:S(2)}, u32[]{:S(2)}) collective-permute-start(bf16[2,32,2304]{2,1,0:T(8,128)(2,1)S(1)} %convolution_convert_fusion.1), channel_id=1, source_target_pairs={{0,6},{1,7},{2,4},{3,5},{4,2},{5,3},{6,0},{7,1},{8,14},{9,15},{10,... | collective-permute-start | bytes 884744 | tf_op jit(solution)/shard_map/send_rows/ppermute | solution.py:882
  202.8 15.8 %collective-permute-start.23 = (bf16[2,32,2304]{2,1,0:T(8,128)(2,1)S(1)}, bf16[2,32,2304]{2,1,0:T(8,128)(2,1)S(1)}, u32[]{:S(2)}, u32[]{:S(2)}) collective-permute-start(bf16[2,32,2304]{2,1,0:T(8,128)(2,1)S(1)} %convolution_convert_fusion), channel_id=1, source_target_pairs={{0,7},{1,6},{2,5},{3,4},{4,3},{5,2},{6,1},{7,0},{8,15},{9,14},{10,... | collective-permute-start | bytes 884744 | tf_op jit(solution)/shard_map/send_rows/ppermute | solution.py:882
  225.6 11.0 %collective-permute-start.25 = (bf16[2,32,2304]{2,1,0:T(8,128)(2,1)S(1)}, bf16[2,32,2304]{2,1,0:T(8,128)(2,1)S(1)}, u32[]{:S(2)}, u32[]{:S(2)}) collective-permute-start(bf16[2,32,2304]{2,1,0:T(8,128)(2,1)S(1)} %bitcast.206), channel_id=1, source_target_pairs={{0,2},{1,3},{2,0},{3,1},{4,6},{5,7},{6,4},{7,5},{8,10},{9,11},{10,... | collective-permute-start | bytes 884744 | tf_op jit(solution)/shard_map/send_results/ppermute | solution.py:882
  228.7 13.7 %collective-permute-start.26 = (bf16[2,32,2304]{2,1,0:T(8,128)(2,1)S(1)}, bf16[2,32,2304]{2,1,0:T(8,128)(2,1)S(1)}, u32[]{:S(2)}, u32[]{:S(2)}) collective-permute-start(bf16[2,32,2304]{2,1,0:T(8,128)(2,1)S(1)} %bitcast.205), channel_id=1, source_target_pairs={{0,3},{1,2},{2,1},{3,0},{4,7},{5,6},{6,5},{7,4},{8,11},{9,10},{10,... | collective-permute-start | bytes 884744 | tf_op jit(solution)/shard_map/send_results/ppermute | solution.py:882
  228.8 26.9 %collective-permute-start.27 = (bf16[2,32,2304]{2,1,0:T(8,128)(2,1)S(1)}, bf16[2,32,2304]{2,1,0:T(8,128)(2,1)S(1)}, u32[]{:S(2)}, u32[]{:S(2)}) collective-permute-start(bf16[2,32,2304]{2,1,0:T(8,128)(2,1)S(1)} %bitcast.204), channel_id=1, source_target_pairs={{0,4},{1,5},{2,6},{3,7},{4,0},{5,1},{6,2},{7,3},{8,12},{9,13},{10,... | collective-permute-start | bytes 884744 | tf_op jit(solution)/shard_map/send_results/ppermute | solution.py:882
  229.7 26.1 %collective-permute-start.28 = (bf16[2,32,2304]{2,1,0:T(8,128)(2,1)S(1)}, bf16[2,32,2304]{2,1,0:T(8,128)(2,1)S(1)}, u32[]{:S(2)}, u32[]{:S(2)}) collective-permute-start(bf16[2,32,2304]{2,1,0:T(8,128)(2,1)S(1)} %bitcast.203), channel_id=1, source_target_pairs={{0,5},{1,4},{2,7},{3,6},{4,1},{5,0},{6,3},{7,2},{8,13},{9,12},{10,... | collective-permute-start | bytes 884744 | tf_op jit(solution)/shard_map/send_results/ppermute | solution.py:882
  230.3 25.4 %collective-permute-start.29 = (bf16[2,32,2304]{2,1,0:T(8,128)(2,1)S(1)}, bf16[2,32,2304]{2,1,0:T(8,128)(2,1)S(1)}, u32[]{:S(2)}, u32[]{:S(2)}) collective-permute-start(bf16[2,32,2304]{2,1,0:T(8,128)(2,1)S(1)} %bitcast.202), channel_id=1, source_target_pairs={{0,6},{1,7},{2,4},{3,5},{4,2},{5,3},{6,0},{7,1},{8,14},{9,15},{10,... | collective-permute-start | bytes 884744 | tf_op jit(solution)/shard_map/send_results/ppermute | solution.py:882
  236.6 21.0 %collective-permute-start.30 = (bf16[2,32,2304]{2,1,0:T(8,128)(2,1)S(1)}, bf16[2,32,2304]{2,1,0:T(8,128)(2,1)S(1)}, u32[]{:S(2)}, u32[]{:S(2)}) collective-permute-start(bf16[2,32,2304]{2,1,0:T(8,128)(2,1)S(1)} %bitcast.201), channel_id=1, source_target_pairs={{0,7},{1,6},{2,5},{3,4},{4,3},{5,2},{6,1},{7,0},{8,15},{9,14},{10,... | collective-permute-start | bytes 884744 | tf_op jit(solution)/shard_map/send_results/ppermute | solution.py:882
  273.9 161.2 %reduce-scatter.5.cloned.1.call-start = ((), (), s32[]{:S(2)}) async-start(), calls=%async_computation.5 | async-start | bytes 7299072 | tf_op jit(solution)/shard_map/reduce_inner/reduce_scatter | solution.py:555
  274.0 46.4 %collective-permute-start.31 = (bf16[768,1152]{1,0:T(8,128)(2,1)}, bf16[768,1152]{1,0:T(8,128)(2,1)}, u32[]{:S(2)}, u32[]{:S(2)}) collective-permute-start(bf16[768,1152]{1,0:T(8,128)(2,1)} %pad_maximum_fusion.2), channel_id=1, source_target_pairs={{0,8},{4,12},{8,16},{12,20},{16,24},{20,28},{24,0},{28,4},{1,9},{5... | collective-permute-start | bytes 5308424 | tf_op jit(solution)/shard_map/ppermute | solution.py:520
  324.4 42.9 %collective-permute-start.32 = (bf16[768,1152]{1,0:T(8,128)(2,1)}, bf16[768,1152]{1,0:T(8,128)(2,1)}, u32[]{:S(2)}, u32[]{:S(2)}) collective-permute-start(bf16[768,1152]{1,0:T(8,128)(2,1)} %add_convert_fusion.1), channel_id=1, source_target_pairs={{0,8},{4,12},{8,16},{12,20},{16,24},{20,28},{24,0},{28,4},{1,9},{5... | collective-permute-start | bytes 5308424 | tf_op jit(solution)/shard_map/ppermute | solution.py:520
  369.6 9.2 %collective-permute-start.33 = (bf16[2,1,72,1152]{3,2,1,0:T(8,128)(2,1)S(1)}, bf16[2,1,72,1152]{3,2,1,0:T(8,128)(2,1)S(1)}, u32[]{:S(2)}, u32[]{:S(2)}) collective-permute-start(bf16[2,1,72,1152]{3,2,1,0:T(8,128)(2,1)S(1)} %get-tuple-element.353), channel_id=1, source_target_pairs={{0,4},{4,0},{8,12},{12,8},{16,20},{20,16},{24,28},{28,24},{1,5},{5... | collective-permute-start | bytes 995336 | tf_op jit(solution)/shard_map/ppermute | solution.py:520
  379.1 9.1 %collective-permute-start.34 = (bf16[72,1152]{1,0:T(8,128)(2,1)S(1)}, bf16[72,1152]{1,0:T(8,128)(2,1)S(1)}, u32[]{:S(2)}, u32[]{:S(2)}) collective-permute-start(bf16[72,1152]{1,0:T(8,128)(2,1)S(1)} %get-tuple-element.351), channel_id=1, source_target_pairs={{0,8},{4,12},{8,16},{12,20},{16,24},{20,28},{24,0},{28,4},{1,9},{5... | collective-permute-start | bytes 497672 | tf_op jit(solution)/shard_map/ppermute | solution.py:520
  379.2 13.8 %collective-permute-start.35 = (bf16[72,1152]{1,0:T(8,128)(2,1)S(1)}, bf16[72,1152]{1,0:T(8,128)(2,1)S(1)}, u32[]{:S(2)}, u32[]{:S(2)}) collective-permute-start(bf16[72,1152]{1,0:T(8,128)(2,1)S(1)} %get-tuple-element.350), channel_id=1, source_target_pairs={{0,16},{4,20},{8,24},{12,28},{16,0},{20,4},{24,8},{28,12},{1,17},{... | collective-permute-start | bytes 497672 | tf_op jit(solution)/shard_map/ppermute | solution.py:520
  381.3 11.6 %collective-permute-start.36 = (bf16[72,1152]{1,0:T(8,128)(2,1)S(1)}, bf16[72,1152]{1,0:T(8,128)(2,1)S(1)}, u32[]{:S(2)}, u32[]{:S(2)}) collective-permute-start(bf16[72,1152]{1,0:T(8,128)(2,1)S(1)} %get-tuple-element.349), channel_id=1, source_target_pairs={{0,24},{4,28},{8,0},{12,4},{16,8},{20,12},{24,16},{28,20},{1,25},{... | collective-permute-start | bytes 497672 | tf_op jit(solution)/shard_map/ppermute | solution.py:520
  393.7 41.4 %collective-permute-start.37 = (bf16[768,1152]{1,0:T(8,128)(2,1)}, bf16[768,1152]{1,0:T(8,128)(2,1)}, u32[]{:S(2)}, u32[]{:S(2)}) collective-permute-start(bf16[768,1152]{1,0:T(8,128)(2,1)} %add_convert_fusion), channel_id=1, source_target_pairs={{0,8},{4,12},{8,16},{12,20},{16,24},{20,28},{24,0},{28,4},{1,9},{5... | collective-permute-start | bytes 5308424 | tf_op jit(solution)/shard_map/ppermute | solution.py:520
  405.0 37.7 %collective-permute-start.43 = (f32[6,1152]{1,0:T(8,128)}, f32[6,1152]{1,0:T(8,128)}, u32[]{:S(2)}, u32[]{:S(2)}) collective-permute-start(f32[6,1152]{1,0:T(8,128)} %add.450), channel_id=1, source_target_pairs={{0,4},{4,0},{8,12},{12,8},{16,20},{20,16},{24,28},{28,24},{1,5},{5... | collective-permute-start | bytes 82952 | tf_op jit(solution)/shard_map/ppermute | solution.py:505
  436.5 12.7 %collective-permute-start.38 = (bf16[2,72,1152]{2,1,0:T(8,128)(2,1)S(1)}, bf16[2,72,1152]{2,1,0:T(8,128)(2,1)S(1)}, u32[]{:S(2)}, u32[]{:S(2)}) collective-permute-start(bf16[2,72,1152]{2,1,0:T(8,128)(2,1)S(1)} %get-tuple-element.346), channel_id=1, source_target_pairs={{0,8},{4,12},{8,16},{12,20},{16,24},{20,28},{24,0},{28,4},{1,9},{5... | collective-permute-start | bytes 995336 | tf_op jit(solution)/shard_map/ppermute | solution.py:520
  438.5 21.7 %collective-permute-start.39 = (bf16[2,72,1152]{2,1,0:T(8,128)(2,1)S(1)}, bf16[2,72,1152]{2,1,0:T(8,128)(2,1)S(1)}, u32[]{:S(2)}, u32[]{:S(2)}) collective-permute-start(bf16[2,72,1152]{2,1,0:T(8,128)(2,1)S(1)} %get-tuple-element.345), channel_id=1, source_target_pairs={{0,16},{4,20},{8,24},{12,28},{16,0},{20,4},{24,8},{28,12},{1,17},{... | collective-permute-start | bytes 995336 | tf_op jit(solution)/shard_map/ppermute | solution.py:520
  438.9 21.4 %collective-permute-start.40 = (bf16[2,72,1152]{2,1,0:T(8,128)(2,1)S(1)}, bf16[2,72,1152]{2,1,0:T(8,128)(2,1)S(1)}, u32[]{:S(2)}, u32[]{:S(2)}) collective-permute-start(bf16[2,72,1152]{2,1,0:T(8,128)(2,1)S(1)} %get-tuple-element.344), channel_id=1, source_target_pairs={{0,24},{4,28},{8,0},{12,4},{16,8},{20,12},{24,16},{28,20},{1,25},{... | collective-permute-start | bytes 995336 | tf_op jit(solution)/shard_map/ppermute | solution.py:520
  444.2 32.6 %collective-permute-start.45 = (bf16[1,1,72,1152]{3,2,1,0:T(8,128)(2,1)}, bf16[1,1,72,1152]{3,2,1,0:T(8,128)(2,1)}, u32[]{:S(2)}, u32[]{:S(2)}) collective-permute-start(bf16[1,1,72,1152]{3,2,1,0:T(8,128)(2,1)} %bitcast.78), channel_id=1, source_target_pairs={{0,2},{1,3},{2,0},{3,1},{4,6},{5,7},{6,4},{7,5},{8,10},{9,11},{10,... | collective-permute-start | bytes 497672 | tf_op jit(solution)/shard_map/ppermute | solution.py:520
  445.4 19.0 %collective-permute-start.50 = (bf16[2,1,72,208]{3,2,1,0:T(8,128)(2,1)S(1)}, bf16[2,1,72,208]{3,2,1,0:T(8,128)(2,1)S(1)}, u32[]{:S(2)}, u32[]{:S(2)}) collective-permute-start(bf16[2,1,72,208]{3,2,1,0:T(8,128)(2,1)S(1)} %get-tuple-element.361), channel_id=1, source_target_pairs={{0,4},{4,0},{8,12},{12,8},{16,20},{20,16},{24,28},{28,24},{1,5},{5... | collective-permute-start | bytes 179720 | tf_op jit(solution)/shard_map/ppermute | solution.py:520
  461.2 18.5 %collective-permute-start.44 = (bf16[1,2,72,1152]{3,2,1,0:T(8,128)(2,1)}, bf16[1,2,72,1152]{3,2,1,0:T(8,128)(2,1)}, u32[]{:S(2)}, u32[]{:S(2)}) collective-permute-start(bf16[1,2,72,1152]{3,2,1,0:T(8,128)(2,1)} %fusion.76), channel_id=1, source_target_pairs={{0,2},{1,3},{2,0},{3,1},{4,6},{5,7},{6,4},{7,5},{8,10},{9,11},{10,... | collective-permute-start | bytes 995336 | tf_op jit(solution)/shard_map/ppermute | solution.py:520
  466.8 12.8 %collective-permute-start.46 = (f32[6,1152]{1,0:T(8,128)}, f32[6,1152]{1,0:T(8,128)S(1)}, u32[]{:S(2)}, u32[]{:S(2)}) collective-permute-start(f32[6,1152]{1,0:T(8,128)} %add.451), channel_id=1, source_target_pairs={{0,8},{4,12},{8,0},{12,4},{16,24},{20,28},{24,16},{28,20},{1,9},{5... | collective-permute-start | bytes 82952 | tf_op jit(solution)/shard_map/ppermute | solution.py:505
  475.3 8.4 %collective-permute-start.51 = (bf16[72,208]{0,1:T(8,128)(2,1)S(1)}, bf16[72,208]{0,1:T(8,128)(2,1)S(1)}, u32[]{:S(2)}, u32[]{:S(2)}) collective-permute-start(bf16[72,208]{0,1:T(8,128)(2,1)S(1)} %get-tuple-element.359), channel_id=1, source_target_pairs={{0,8},{4,12},{8,16},{12,20},{16,24},{20,28},{24,0},{28,4},{1,9},{5... | collective-permute-start | bytes 89864 | tf_op jit(solution)/shard_map/ppermute | solution.py:520
  475.3 11.9 %collective-permute-start.52 = (bf16[72,208]{0,1:T(8,128)(2,1)S(1)}, bf16[72,208]{0,1:T(8,128)(2,1)S(1)}, u32[]{:S(2)}, u32[]{:S(2)}) collective-permute-start(bf16[72,208]{0,1:T(8,128)(2,1)S(1)} %get-tuple-element.358), channel_id=1, source_target_pairs={{0,16},{4,20},{8,24},{12,28},{16,0},{20,4},{24,8},{28,12},{1,17},{... | collective-permute-start | bytes 89864 | tf_op jit(solution)/shard_map/ppermute | solution.py:520
  476.8 10.5 %collective-permute-start.53 = (bf16[72,208]{0,1:T(8,128)(2,1)S(1)}, bf16[72,208]{0,1:T(8,128)(2,1)S(1)}, u32[]{:S(2)}, u32[]{:S(2)}) collective-permute-start(bf16[72,208]{0,1:T(8,128)(2,1)S(1)} %get-tuple-element.357), channel_id=1, source_target_pairs={{0,24},{4,28},{8,0},{12,4},{16,8},{20,12},{24,16},{28,20},{1,25},{... | collective-permute-start | bytes 89864 | tf_op jit(solution)/shard_map/ppermute | solution.py:520
  (131 other events, 1007.9 us)
Sparse Core Ops, SparseCore 0:
  46.5 73.5 all-gather.2
  130.8 39.1 all-gather.4
  274.1 81.2 reduce-scatter.2
  367.4 61.3 reduce-scatter.4

commit v4 on v3

--- a/solution.py
+++ b/solution.py
@@ -60,9 +60,10 @@
     lax.fori_loop(0, length // ROWS, block, jnp.zeros_like(rate))
 
 def scan_backward(
-    decay_ref, drive_ref, b_ref, c_ref, rate_ref, dout_ref,
-    ddrive_ref, ddecay_ref, drate_ref, db_sum_ref, dc_sum_ref,
-    db_ref, dc_ref, state_ref, factor_ref,
+    decay_ref, drive_ref, b_ref, c_ref, rate_ref, dout_ref, delta_ref, conv_out_ref, dt_sum_ref,
+    skip_ref, dtproj_ref,
+    d_conv_ref, d_dt_ref, d_low_ref, rows_ref, db_sum_ref, dc_sum_ref,
+    db_ref, dc_ref, state_ref, factor_ref, ddrive_ref, ddecay_ref,
 ):
     length, width = decay_ref.shape[1:]
     rate = rate_ref[...]
@@ -103,12 +104,39 @@
             power = later * state_ref[t]
             decay_pieces[offset] = power * rate
             drate = drate + power * decay_ref[0, pl.ds(t, 1), :]
-        ddrive_ref[0, pl.ds(start, ROWS), :] = fold_states(drive_pieces, position)
-        ddecay_ref[0, pl.ds(start, ROWS), :] = fold_states(decay_pieces, position)
+        ddrive_ref[pl.ds(start, ROWS), :] = fold_states(drive_pieces, position)
+        ddecay_ref[pl.ds(start, ROWS), :] = fold_states(decay_pieces, position)
         return later, drate
 
     zero = jnp.zeros_like(rate)
-    drate_ref[0] = lax.fori_loop(0, length // ROWS, block, (zero, zero))[1]
+    drate = lax.fori_loop(0, length // ROWS, block, (zero, zero))[1]
+    states = rate.shape[0]
+    ddrive = ddrive_ref[...]
+    dout = dout_ref[0]
+    conv_out = conv_out_ref[0]
+    d_conv_ref[0] = ddrive * delta_ref[0] + dout * skip_ref[...]
+    d_delta = ddecay_ref[...] * (1.0 / LOG2E) + ddrive * conv_out
+    d_dt = d_delta * jax.nn.sigmoid(dt_sum_ref[0])
+    d_dt_low = d_dt.astype(jnp.bfloat16)
+    d_dt_ref[0] = d_dt_low
+    rows_ref[0, :states, :] = drate * rate * (1.0 / LOG2E)
+    rows_ref[0, states:, :] = jnp.concatenate(
+        [
+            jnp.sum(d_dt, axis=0, keepdims=True),
+            jnp.sum(dout * conv_out, axis=0, keepdims=True),
+            jnp.zeros((rows_ref.shape[1] - states - 2, width), jnp.float32),
+        ],
+        axis=0,
+    )
+    d_low = product(d_dt_low, dtproj_ref[...], ((1,), (1,)))
+
+    @pl.when(pl.program_id(1) == 0)
+    def _():
+        d_low_ref[0] = d_low
+
+    @pl.when(pl.program_id(1) > 0)
+    def _():
+        d_low_ref[0] += d_low
 
     @pl.when(pl.program_id(1) == pl.num_programs(1) - 1)
     def _():
@@ -152,33 +180,121 @@
         name="scan_forward",
     )(decay, drive, b_wide, c_wide, rate)
 
-def run_backward(decay, drive, b_wide, c_wide, rate, dout):
+def run_backward(
+    decay, drive, b_wide, c_wide, rate, dout, delta, conv_out, dt_sum, skip, dtproj
+):
     count, length, channels = decay.shape
     states = rate.shape[0]
+    rank = dtproj.shape[0]
     width = tile_width(channels)
+    extra = states + ROWS
     tokens, maps, rates = scan_specs(length, states, width)
-    full = jax.ShapeDtypeStruct(decay.shape, jnp.float32)
     summed = jax.ShapeDtypeStruct((count, ROWS, length * states), jnp.float32)
     sums = pl.BlockSpec((1, ROWS, length * states), lambda s, c: (s, 0, 0))
     return pl.pallas_call(
         scan_backward,
         grid=(count, channels // width),
-        in_specs=[tokens, tokens, maps, maps, rates, tokens],
-        out_specs=[tokens, tokens, pl.BlockSpec((1, states, width), lambda s, c: (s, 0, c)), sums, sums],
-        out_shape=[full, full, jax.ShapeDtypeStruct((count, states, channels), jnp.float32),
-            summed, summed],
-        scratch_shapes=[pltpu.VMEM((length, states, LANES), jnp.float32), pltpu.VMEM((length, states, LANES), jnp.float32),
-            pltpu.VMEM((length + 1, states, width), jnp.float32), pltpu.VMEM((length, states, width), jnp.float32)],
+        in_specs=[tokens, tokens, maps, maps, rates, tokens, tokens, tokens, tokens]
+        + [
+            pl.BlockSpec((1, width), lambda s, c: (0, c)),
+            pl.BlockSpec((rank, width), lambda s, c: (0, c)),
+        ],
+        out_specs=[
+            tokens,
+            tokens,
+            pl.BlockSpec((1, length, rank), lambda s, c: (s, 0, 0)),
+            pl.BlockSpec((1, extra, width), lambda s, c: (s, 0, c)),
+            sums,
+            sums,
+        ],
+        out_shape=[
+            jax.ShapeDtypeStruct(decay.shape, jnp.float32),
+            jax.ShapeDtypeStruct(decay.shape, jnp.bfloat16),
+            jax.ShapeDtypeStruct((count, length, rank), jnp.float32),
+            jax.ShapeDtypeStruct((count, extra, channels), jnp.float32),
+            summed,
+            summed,
+        ],
+        scratch_shapes=[
+            pltpu.VMEM((length, states, LANES), jnp.float32),
+            pltpu.VMEM((length, states, LANES), jnp.float32),
+            pltpu.VMEM((length + 1, states, width), jnp.float32),
+            pltpu.VMEM((length, states, width), jnp.float32),
+            pltpu.VMEM((length, width), jnp.float32),
+            pltpu.VMEM((length, width), jnp.float32),
+        ],
         cost_estimate=pl.CostEstimate(
-            flops=decay.size, transcendentals=0,
-            bytes_accessed=4 * (5 * decay.size + 4 * b_wide.size)),
-        compiler_params=pltpu.CompilerParams(vmem_limit_bytes=VMEM_GRANT),
+            flops=decay.size, transcendentals=0, bytes_accessed=decay.size
+        ),
+        compiler_params=pltpu.CompilerParams(vmem_limit_bytes=60 << 20),
         name="scan_backward",
-    )(decay, drive, b_wide, c_wide, rate, dout)
+    )(decay, drive, b_wide, c_wide, rate, dout, delta, conv_out, dt_sum, skip, dtproj)
 
 
 def product(left, right, contract):
     return lax.dot_general(left, right, (contract, ((), ())), preferred_element_type=jnp.float32)
+
+
+def conv_forward(
+    normed_ref, in_ref, masks_ref, conv_ref, xproj_ref, inner_ref, gate_ref, conv_out_ref, maps_ref
+):
+    taps = masks_ref.shape[1]
+    model = normed_ref.shape[1]
+    inner = product(normed_ref[...], in_ref[:, :model], ((1,), (1,)))
+    inner_ref[...] = inner
+    gate_ref[...] = product(normed_ref[...], in_ref[:, model:], ((1,), (1,)))
+    total = conv_ref[taps : taps + 1] + conv_ref[taps - 1 : taps] * inner
+    for offset in range(1, taps):
+        total = total + conv_ref[taps - 1 - offset : taps - offset] * (
+            pltpu.roll(inner, offset, 0) * masks_ref[:, offset : offset + 1]
+        )
+    conv_out = total * jax.nn.sigmoid(total)
+    conv_out_ref[...] = conv_out
+    maps = product(conv_out.astype(jnp.bfloat16), xproj_ref[...], ((1,), (0,)))
+
+    @pl.when(pl.program_id(0) == 0)
+    def _():
+        maps_ref[...] = maps
+
+    @pl.when(pl.program_id(0) > 0)
+    def _():
+        maps_ref[...] += maps
+
+
+def run_conv_forward(normed, in_rows, masks, conv_rows, xproj):
+    count, model = normed.shape
+    channels = in_rows.shape[0]
+    width = tile_width(channels)
+    tokens = pl.BlockSpec((count, width), lambda c: (0, c))
+    full = jax.ShapeDtypeStruct((count, channels), jnp.float32)
+
+    def whole(values):
+        return pl.BlockSpec(values.shape, lambda c: (0, 0))
+
+    def rows(values):
+        return pl.BlockSpec((width, values.shape[1]), lambda c: (c, 0))
+
+    return pl.pallas_call(
+        conv_forward,
+        grid=(channels // width,),
+        in_specs=[
+            whole(normed),
+            rows(in_rows),
+            whole(masks),
+            pl.BlockSpec((ROWS, width), lambda c: (0, c)),
+            rows(xproj),
+        ],
+        out_specs=[
+            tokens,
+            tokens,
+            tokens,
+            pl.BlockSpec((count, xproj.shape[1]), lambda c: (0, 0)),
+        ],
+        out_shape=[full, full, full, jax.ShapeDtypeStruct((count, xproj.shape[1]), jnp.float32)],
+        cost_estimate=pl.CostEstimate(flops=count, transcendentals=0, bytes_accessed=count),
+        compiler_params=pltpu.CompilerParams(vmem_limit_bytes=VMEM_GRANT),
+        name="conv_forward",
+    )(normed, in_rows, masks, conv_rows, xproj)
 
 
 def gate_backward(
@@ -222,18 +338,14 @@
 
 
 def conv_backward(
-    d_drive_ref, delta_ref, d_scanned_ref, inner_ref, d_gate_ref, d_proj_ref, normed_ref,
+    d_scan_ref, inner_ref, d_gate_ref, d_proj_ref, normed_ref,
     masks_ref, conv_ref, xproj_ref, in_ref, d_dt_ref, dt_ref, rows_ref,
     term_ref, d_normed_ref,
 ):
     taps = masks_ref.shape[1]
     model = normed_ref.shape[1]
     count = inner_ref.shape[0]
-    d_conv = (
-        d_drive_ref[...] * delta_ref[...]
-        + d_scanned_ref[...] * conv_ref[taps + 1 : taps + 2]
-        + product(d_proj_ref[...], xproj_ref[...], ((1,), (1,)))
-    )
+    d_conv = d_scan_ref[...] + product(d_proj_ref[...], xproj_ref[...], ((1,), (1,)))
     inner = inner_ref[...]
     shifted = [inner] + [pltpu.roll(inner, offset, 0) for offset in range(1, taps)]
     masked = [shifted[offset] * masks_ref[:, offset : offset + 1] for offset in range(taps)]
@@ -283,9 +395,7 @@
 
 
 def run_conv_backward(
-    d_drive,
-    delta,
-    d_scanned,
+    d_scan,
     inner,
     d_gate,
     d_proj,
@@ -317,8 +427,6 @@
             tokens,
             tokens,
             tokens,
-            tokens,
-            tokens,
             whole(d_proj),
             whole(normed),
             whole(masks),
@@ -341,9 +449,7 @@
         compiler_params=pltpu.CompilerParams(vmem_limit_bytes=VMEM_GRANT),
         name="conv_backward",
     )(
-        d_drive,
-        delta,
-        d_scanned,
+        d_scan,
         inner,
         d_gate,
         d_proj,
@@ -362,11 +468,25 @@
 GELU_CUBE = 0.044715
 
 
-def expert_pass(pieces, blocks, *refs):
+def expert_units(slot_rows, d_returned, up, down):
+    hidden = product(slot_rows, up, ((1,), (1,)))
+    square = hidden * hidden
+    bend = jnp.tanh(GELU_SCALE * (hidden + GELU_CUBE * (square * hidden)))
+    share = 0.5 * (1.0 + bend)
+    active = (hidden * share).astype(jnp.bfloat16)
+    slope = share + hidden * (0.5 * GELU_SCALE) * (1.0 - bend * bend) * (
+        1.0 + 3.0 * GELU_CUBE * square
+    )
+    d_active = product(d_returned, down, ((1,), (1,)))
+    d_hidden = (d_active * slope).astype(jnp.bfloat16)
+    returned = product(active, down, ((1,), (0,)))
+    d_slots = product(d_hidden, up, ((1,), (0,)))
+    return active, d_hidden, returned, d_slots
+
+
+def expert_first(pieces, blocks, *refs):
     piece_refs, block_refs = refs[:pieces], refs[pieces : pieces + blocks]
-    refs = refs[pieces + blocks :]
-    result_refs, (rows_ref, active_ref, d_hidden_ref) = refs[:pieces], refs[pieces : pieces + 3]
-    total_ref, held_ref, sems = refs[pieces + 3 :]
+    rows_ref, active_ref, d_hidden_ref, total_ref, held_ref, sems = refs[pieces + blocks :]
     copies = [
         pltpu.make_async_copy(block_refs[k], held_ref.at[k], sems.at[k]) for k in range(blocks)
     ]
@@ -380,60 +500,86 @@
     slot_rows, d_returned = rows_ref[:, :model], rows_ref[:, model:]
     for k in range(blocks):
         copies[k].wait()
-        up, down = held_ref[k, :units, :], held_ref[k, units:, :]
-        hidden = product(slot_rows, up, ((1,), (1,)))
-        square = hidden * hidden
-        bend = jnp.tanh(GELU_SCALE * (hidden + GELU_CUBE * (square * hidden)))
-        share = 0.5 * (1.0 + bend)
-        active = (hidden * share).astype(jnp.bfloat16)
-        slope = share + hidden * (0.5 * GELU_SCALE) * (1.0 - bend * bend) * (
-            1.0 + 3.0 * GELU_CUBE * square
+        active, d_hidden, returned, d_slots = expert_units(
+            slot_rows, d_returned, held_ref[k, :units, :], held_ref[k, units:, :]
         )
-        d_active = product(d_returned, down, ((1,), (1,)))
-        d_hidden = (d_active * slope).astype(jnp.bfloat16)
         active_ref[:, k * units : (k + 1) * units] = active
         d_hidden_ref[:, k * units : (k + 1) * units] = d_hidden
-        returned = product(active, down, ((1,), (0,)))
-        d_slots = product(d_hidden, up, ((1,), (0,)))
         if k:
             returned = returned + total_ref[:, :model]
             d_slots = d_slots + total_ref[:, model:]
-        if k < blocks - 1:
-            total_ref[:, :model] = returned
-            total_ref[:, model:] = d_slots
-        else:
-            for n in range(pieces):
-                part = slice(n * length, (n + 1) * length)
-                result_refs[n][:, :model] = returned[part].astype(jnp.bfloat16)
-                result_refs[n][:, model:] = d_slots[part].astype(jnp.bfloat16)
-
-
-def run_expert(pieces, blocks):
+        total_ref[:, :model] = returned
+        total_ref[:, model:] = d_slots
+
+
+def run_expert_first(pieces, blocks):
     length, width = pieces[0].shape
     rows = length * len(pieces)
     units = blocks[0].shape[0] // 2
     low = jnp.bfloat16
     vmem = pl.BlockSpec(memory_space=pltpu.VMEM)
-    out = pl.pallas_call(
-        functools.partial(expert_pass, len(pieces), len(blocks)),
+    return pl.pallas_call(
+        functools.partial(expert_first, len(pieces), len(blocks)),
         in_specs=[vmem] * len(pieces) + [pl.BlockSpec(memory_space=pl.ANY)] * len(blocks),
-        out_specs=[vmem] * (len(pieces) + 3),
-        out_shape=[jax.ShapeDtypeStruct((length, width), low)] * len(pieces)
-        + [
+        out_specs=[vmem] * 4,
+        out_shape=[
             jax.ShapeDtypeStruct((rows, width), low),
             jax.ShapeDtypeStruct((rows, units * len(blocks)), low),
             jax.ShapeDtypeStruct((rows, units * len(blocks)), low),
+            jax.ShapeDtypeStruct((rows, width), jnp.float32),
         ],
         scratch_shapes=[
-            pltpu.VMEM((rows, width), jnp.float32),
             pltpu.VMEM((len(blocks),) + blocks[0].shape, low),
             pltpu.SemaphoreType.DMA((len(blocks),)),
         ],
         cost_estimate=pl.CostEstimate(flops=rows, transcendentals=0, bytes_accessed=rows),
         compiler_params=pltpu.CompilerParams(vmem_limit_bytes=VMEM_GRANT),
-        name="expert_pass",
+        name="expert_first",
     )(*pieces, *blocks)
-    return out[: len(pieces)], out[len(pieces) :]
+
+
+def expert_last(pieces, rows_refs, total_refs, block_ref, result_refs, active_ref, d_hidden_ref):
+    model = rows_refs[0].shape[1] // 2
+    units = block_ref.shape[0] // 2
+    extent = rows_refs[0].shape[0]
+    length = extent // pieces
+    for n in range(2):
+        active, d_hidden, returned, d_slots = expert_units(
+            rows_refs[n][:, :model],
+            rows_refs[n][:, model:],
+            block_ref[:units, :],
+            block_ref[units:, :],
+        )
+        active_ref[n * extent : (n + 1) * extent, :] = active
+        d_hidden_ref[n * extent : (n + 1) * extent, :] = d_hidden
+        returned = (returned + total_refs[n][:, :model]).astype(jnp.bfloat16)
+        d_slots = (d_slots + total_refs[n][:, model:]).astype(jnp.bfloat16)
+        for m in range(pieces):
+            part = slice(m * length, (m + 1) * length)
+            result_refs[n * pieces + m][:, :model] = returned[part]
+            result_refs[n * pieces + m][:, model:] = d_slots[part]
+
+
+def run_expert_last(pieces, rows, totals, block):
+    extent, width = rows[0].shape
+    units = block.shape[0] // 2
+    low = jnp.bfloat16
+    vmem = pl.BlockSpec(memory_space=pltpu.VMEM)
+
+    def kernel(*refs):
+        expert_last(pieces, refs[:2], refs[2:4], refs[4], refs[5:-2], refs[-2], refs[-1])
+
+    out = pl.pallas_call(
+        kernel,
+        in_specs=[vmem] * 5,
+        out_specs=[vmem] * (2 * pieces + 2),
+        out_shape=[jax.ShapeDtypeStruct((extent // pieces, width), low)] * (2 * pieces)
+        + [jax.ShapeDtypeStruct((2 * extent, units), low)] * 2,
+        cost_estimate=pl.CostEstimate(flops=extent, transcendentals=0, bytes_accessed=extent),
+        compiler_params=pltpu.CompilerParams(vmem_limit_bytes=VMEM_GRANT),
+        name="expert_last",
+    )(*rows, *totals, block)
+    return [out[:pieces], out[pieces:-2]], out[-2], out[-1]
 
 
 HIGHEST = lax.Precision.HIGHEST
@@ -454,10 +600,6 @@
     )
 
 
-def gelu_tanh(values):
-    return jax.nn.gelu(values, approximate=True)
-
-
 def norm_route(residual, gain_two, router_full, chosen_rows):
     normed_two = rms_scale(residual, gain_two)
     logits = jnp.dot(normed_two, router_full, precision=HIGHEST, preferred_element_type=jnp.float32)
@@ -465,25 +607,11 @@
     return (normed_two, jnp.sum(probabilities * chosen_rows, axis=1))
 
 
-def later_rows(values, offset):
-    if offset == 0:
-        return values
-    return jnp.pad(values, ((0, 0), (offset, 0), (0, 0)))[:, : values.shape[1]]
-
-
 def same_document(segments, offset):
     if offset == 0:
         return jnp.ones(segments.shape, jnp.float32)
     padded = jnp.pad(segments, ((0, 0), (offset, 0)), constant_values=-1)
     return (padded[:, : segments.shape[1]] == segments).astype(jnp.float32)
-
-
-def conv_sum(inner, taps, bias_row, masks):
-    count = taps.shape[0]
-    total = bias_row
-    for offset in range(count):
-        total = total + taps[count - 1 - offset] * later_rows(inner, offset) * masks[offset]
-    return total
 
 
 def dispatch_matrices(order_rows, expert_count, capacity, padded_capacity):
@@ -778,9 +906,7 @@
     out_block = part_rows(out_weight, expert_index * channels, channels)
     out_block = streams.advance(("small", "expert"), out_block)
     streams.start("out", far_and_pair(out_block))
-    streams.finish(("out", "small"))
-    with jax.named_scope("fetch_out"):
-        out_full = cube_gather(streams.done["out"].reshape(-1, model_width))
+    streams.finish(("small",))
     small_full = streams.done["small"]
     xproj_width = rank + 2 * states
     xproj_full = small_full[:, :xproj_width]
@@ -810,13 +936,12 @@
     placed = dispatch_matrices(
         route_rows ^ expert_index.astype(jnp.int32), expert_count, capacity, padded_capacity
     )
-    in_cube, conv_rows, mask_columns, xproj_full, dtproj_full, rate_two, placed, dtb_full = (
-        lax.optimization_barrier(
-            (in_cube, conv_rows, mask_columns, xproj_full, dtproj_full, rate_two, placed, dtb_full)
-        )
-    )
-    inner_full = in_cube[:, :model_width]
-    gate_full = in_cube[:, model_width:]
+    conv_rows, mask_columns, xproj_full, dtproj_full, rate_two, placed, dtb_full = streams.advance(
+        ("out",), conv_rows, mask_columns, xproj_full, dtproj_full, rate_two, placed, dtb_full
+    )
+    streams.finish(("out",))
+    with jax.named_scope("fetch_out"):
+        out_full = cube_gather(streams.done["out"].reshape(-1, model_width))
     gain_one = norm1_gain.astype(jnp.float32)
     gain_two = norm2_gain.astype(jnp.float32)
     router_full = router_weight.astype(jnp.float32)
@@ -831,11 +956,10 @@
     cot_rows = cotangent.reshape(tokens, model_width).astype(jnp.float32)
     normed_one, norm_pull = jax.vjp(rms_scale, rows_in, gain_one)
     normed_low = normed_one.astype(LOW)
-    inner = split(dot(normed_low, inner_full, ((1,), (1,))))
-    gate_in = split(dot(normed_low, gate_full, ((1,), (1,))))
-    conv_out = jax.nn.silu(conv_sum(inner, conv_full, convb_full, masks))
-    conv_low = flat(conv_out).astype(LOW)
-    projected = dot(conv_low, xproj_full, ((1,), (0,)))
+    inner, gate_in, conv_out, projected = run_conv_forward(
+        normed_low, in_cube, mask_columns, conv_rows, xproj_full
+    )
+    gate_in, conv_out = split(gate_in), split(conv_out)
     dt_low = projected[:, :rank].astype(LOW)
     b_wide = jnp.broadcast_to(
         split(projected[:, rank : rank + states])[..., None], (sequences, seq_len, states, LANES)
@@ -894,15 +1018,25 @@
     units = up_weight.shape[1]
     while len(streams.blocks) < steps - 1:
         streams.advance(("expert",))
-    received[0] = list(streams.advance(("expert",), *received[0]))
-    blocks = streams.done["expert"]
-    own_results, own_kept = run_expert(received[0], blocks)
-    cross_results, cross_kept = run_expert(received[1], blocks)
+    early = streams.blocks[: steps - 1]
+    own_rows, own_active, own_d_hidden, own_total = run_expert_first(received[0], early)
+    cross_rows, cross_active, cross_d_hidden, cross_total = run_expert_first(received[1], early)
+    own_total, cross_total = streams.advance(("expert",), own_total, cross_total)
+    results, last_active, last_d_hidden = run_expert_last(
+        expert_count,
+        [own_rows, cross_rows],
+        [own_total, cross_total],
+        streams.done["expert"][steps - 1],
+    )
     results = [
         [piece.reshape(sequences, padded_capacity, 2 * model_width) for piece in group]
-        for group in (own_results, cross_results)
+        for group in results
     ]
-    kept = [own_kept, cross_kept]
+    extent = own_rows.shape[0]
+    kept = [
+        (own_rows, own_active, own_d_hidden, last_active[:extent], last_d_hidden[:extent]),
+        (cross_rows, cross_active, cross_d_hidden, last_active[extent:], last_d_hidden[extent:]),
+    ]
     kept, results = lax.optimization_barrier((kept, results))
     with jax.named_scope("send_results"):
         arrived = [
@@ -912,15 +1046,13 @@
     kept, arrived[0] = lax.optimization_barrier((kept, arrived[0]))
     up_terms = [0.0] * steps
     down_terms = [0.0] * steps
-    for rows, active_rows, d_hidden_rows in kept:
+    for rows, active_rows, d_hidden_rows, last_active, last_d_hidden in kept:
         for k in range(steps):
             part = slice(k * units, (k + 1) * units)
-            up_terms[k] = up_terms[k] + dot(
-                d_hidden_rows[:, part], rows[:, :model_width], ((0,), (0,))
-            )
-            down_terms[k] = down_terms[k] + dot(
-                active_rows[:, part], rows[:, model_width:], ((0,), (0,))
-            )
+            active_k = active_rows[:, part] if k < steps - 1 else last_active
+            d_hidden_k = d_hidden_rows[:, part] if k < steps - 1 else last_d_hidden
+            up_terms[k] = up_terms[k] + dot(d_hidden_k, rows[:, :model_width], ((0,), (0,)))
+            down_terms[k] = down_terms[k] + dot(active_k, rows[:, model_width:], ((0,), (0,)))
     terms = [
         jnp.concatenate([up.astype(LOW), down.astype(LOW)], axis=0)
         for up, down in zip(up_terms, down_terms)
@@ -951,33 +1083,34 @@
     with jax.named_scope("reduce_out_gate"):
         out_gate_blocks = cube_scatter(out_gate_term)
     d_scanned = split(d_scanned)
-    d_drive, d_decay, d_rate, d_b, d_c = run_backward(
-        decay, drive, b_wide, c_wide, rate_two, d_scanned
-    )
-    d_drive = streams.advance(("expert_grad",), d_drive)
+    d_scan, d_dt_low, d_dt_rows, more_rows, d_b, d_c = run_backward(
+        decay,
+        drive,
+        b_wide,
+        c_wide,
+        rate_two,
+        d_scanned,
+        delta,
+        conv_out,
+        dt_sum,
+        skip_full[None],
+        dtproj_full,
+    )
+    d_scan = streams.advance(("expert_grad",), d_scan)
     streams.advance(("expert_grad",))
-    d_skip = jnp.sum(d_scanned * conv_out, axis=(0, 1))
-    d_alog = jnp.sum(d_rate, axis=0) * rate
-    d_delta = d_decay * (1.0 / LOG2E) + d_drive * conv_out
-    d_dt = d_delta * jax.nn.sigmoid(dt_sum)
-    d_dtb = jnp.sum(d_dt, axis=(0, 1))
-    d_dt_low = flat(d_dt).astype(LOW)
-    d_dt_rows = dot(d_dt_low, dtproj_full, ((1,), (1,)))
+    d_dt_low = flat(d_dt_low)
     d_proj_low = jnp.concatenate(
         [
-            d_dt_rows,
+            flat(d_dt_rows),
             d_b[:, 0].reshape(tokens, states),
             d_c[:, 0].reshape(tokens, states),
         ],
         axis=1,
     ).astype(LOW)
-    more_rows = jnp.concatenate([d_alog, d_dtb[None], d_skip[None]], axis=0)
-    more_rows = jnp.pad(more_rows, ((0, -more_rows.shape[0] % ROWS), (0, 0)))
+    more_rows = jnp.sum(more_rows, axis=0)
     inner_term, d_normed = run_conv_backward(
-        flat(d_drive),
-        flat(delta),
-        flat(d_scanned),
-        flat(inner),
+        flat(d_scan),
+        inner,
         d_gate_low,
         d_proj_low,
         normed_low,

time: 513 us -> 488 us (0.951)
  waiting for transfers between devices: 203 us -> 223 us
  local copies, waits for them, and re-layouts: 68.9 us -> 51.5 us
  other arithmetic: 51.2 us -> 36.2 us
  starting transfers between devices: 64.8 us -> 50.5 us
  Pallas kernels: 74.7 us -> 86.2 us
  matrix products: 27.3 us -> 17.3 us
    unnamed x263 -> x167, local copies, waits for them, and re-layouts: 36.3 us -> 23 us
    ppermute x14, waiting for transfers between devices: 18.9 us -> 29.9 us  [exchange(): return lax.ppermute(piece, BOTH, partners(cross, k))]
    dot_general x22 -> x18, matrix products: 21.5 us -> 12.1 us  [dot(): lax.dot_general(left, right, (contract, ((), ())), preferred_element_type...]
    ppermute x35, waiting for transfers between devices: 178 us -> 187 us  [hop(): return lax.ppermute(values, self.axis_name, pairs)]
    pallas_call x2 -> x4, Pallas kernels: 13.3 us -> 21.5 us  [the longest x2 10.3 us: run_expert_first(): pl.pallas_call(functools.partial(expert_first, len(pieces), len(blocks)),...]
    ppermute x5, starting transfers between devices: 11.2 us -> 5.53 us  [hop(): lax.ppermute(values, axis_name, [(i, i ^ distance) for i in range(size)])]
    ppermute x14, starting transfers between devices: 17.8 us -> 12.4 us  [exchange(): return lax.ppermute(piece, BOTH, partners(cross, k))]
  transfers between devices with their start and end apart: 58 -> 58, of which waited for: 29 -> 32; matrix products, arithmetic and copies ran while one was open for 20% -> 15% of each run, Pallas kernels for 12% -> 16%
where the time goes in v4:
time: 488 us; the launch traced here: 480 us
  waiting for transfers between devices  223 us (46%)
  Pallas kernels  86.2 us (18%)
  local copies, waits for them, and re-layouts  51.5 us (11%)
  starting transfers between devices  50.5 us (10%)
  other arithmetic  36.2 us (7%)
  matrix products  17.3 us (4%)
  between operations  15.9 us (3%)
    ppermute x35, waiting for transfers between devices, hop(): return lax.ppermute(values, self.axis_name, pairs)  187 us
    pallas_call x1, Pallas kernels, run_backward(): pl.pallas_call(scan_backward, grid=(count, channels // width), in_specs=[...  33.4 us
    ppermute x35, starting transfers between devices, hop(): return lax.ppermute(values, self.axis_name, pairs)  32.4 us
    ppermute x14, waiting for transfers between devices, exchange(): return lax.ppermute(piece, BOTH, partners(cross, k))  29.9 us
    unnamed x167, local copies, waits for them, and re-layouts  23 us
    ppermute x14, starting transfers between devices, exchange(): return lax.ppermute(piece, BOTH, partners(cross, k))  12.4 us
    dot_general x18, matrix products, dot(): lax.dot_general(left, right, (contract, ((), ())), preferred_element_type...  12.1 us
    pallas_call x1, Pallas kernels, run_conv_backward(): pl.pallas_call(conv_backward, grid=(channels // width,), in_specs=[tokens...  12 us
  transfers between devices with their start and end apart: 58, of which 32 were waited for; matrix products, arithmetic and copies ran while one was open for 15% of the time, Pallas kernels for 16%

profile of v4, /device:TPU:0, one launch (start us, length us, event | category | flops | bytes accessed | tf_op | source)
XLA Modules:
  0.0 480.4 jit_solution(4981057616684178664)
XLA Ops:
  8.5 3.1 collective-permute-start
  18.8 4.2 collective-permute-done.1
  24.3 9.8 %collective-permute-done.3 = bf16[1,72,199]{2,1,0:T(8,128)(2,1)S(1)} collective-permute-done((bf16[1,72,199]{2,1,0:T(8,128)(2,1)S(1)}, bf16[1,72,199]{2,1,0:T(8,128)(2,1)S(1)}, u32[]{:S(2)}, u32[]{:S(2)}) %collective-permute-start.3) | collective-permute-done | bytes 28688 | tf_op jit(solution)/shard_map/ppermute | solution.py:648
  34.1 10.2 %collective-permute-done.5 = bf16[1,72,199]{2,1,0:T(8,128)(2,1)S(1)} collective-permute-done((bf16[1,72,199]{2,1,0:T(8,128)(2,1)S(1)}, bf16[1,72,199]{2,1,0:T(8,128)(2,1)S(1)}, u32[]{:S(2)}, u32[]{:S(2)}) %collective-permute-start.5) | collective-permute-done | bytes 28688 | tf_op jit(solution)/shard_map/ppermute | solution.py:648
  51.8 2.6 collective-permute-done.6
  57.8 14.2 %collective-permute-done.8 = bf16[1,576,199]{2,1,0:T(8,128)(2,1)S(1)} collective-permute-done((bf16[1,576,199]{2,1,0:T(8,128)(2,1)S(1)}, bf16[1,576,199]{2,1,0:T(8,128)(2,1)S(1)}, u32[]{:S(2)}, u32[]{:S(2)}) %collective-permute-start.8) | collective-permute-done | bytes 229280 | tf_op jit(solution)/shard_map/ppermute | solution.py:648
  72.6 2.5 collective-permute-start.9
  77.6 10.3 %collective-permute-done.10.refs_5_ = bf16[768,1152]{1,0:T(8,128)(2,1)} collective-permute-done((bf16[768,1152]{1,0:T(8,128)(2,1)S(1)}, bf16[768,1152]{1,0:T(8,128)(2,1)}, u32[]{:S(2)}, u32[]{:S(2)}) %collective-permute-start.10) | collective-permute-done | bytes 1769504 | tf_op jit(solution)/shard_map/ppermute | solution.py:648
  96.4 8.6 %collective-permute-done.13 = bf16[1,72,1152]{2,1,0:T(8,128)(2,1)S(1)} collective-permute-done((bf16[1,72,1152]{2,1,0:T(8,128)(2,1)}, bf16[1,72,1152]{2,1,0:T(8,128)(2,1)S(1)}, u32[]{:S(2)}, u32[]{:S(2)}) %collective-permute-start.13) | collective-permute-done | bytes 165920 | tf_op jit(solution)/shard_map/ppermute | solution.py:648
  105.1 7.1 %collective-permute-done.14 = bf16[1,72,1152]{2,1,0:T(8,128)(2,1)S(1)} collective-permute-done((bf16[1,72,1152]{2,1,0:T(8,128)(2,1)S(1)}, bf16[1,72,1152]{2,1,0:T(8,128)(2,1)S(1)}, u32[]{:S(2)}, u32[]{:S(2)}) %collective-permute-start.14) | collective-permute-done | bytes 165920 | tf_op jit(solution)/shard_map/ppermute | solution.py:648
  115.3 2.7 collective-permute-start.15
  118.0 5.1 %collective-permute-done.15 = bf16[2,1,72,1152]{3,2,1,0:T(8,128)(2,1)S(1)} collective-permute-done((bf16[2,1,72,1152]{3,2,1,0:T(8,128)(2,1)S(1)}, bf16[2,1,72,1152]{3,2,1,0:T(8,128)(2,1)S(1)}, u32[]{:S(2)}, u32[]{:S(2)}) %collective-permute-start.15) | collective-permute-done | bytes 331808 | tf_op jit(solution)/shard_map/ppermute | solution.py:648
  127.7 8.4 %conv_forward.1 = (f32[192,2304]{1,0:T(8,128)S(1)}, f32[192,2304]{1,0:T(8,128)S(1)}, f32[192,2304]{1,0:T(8,128)S(1)}, f32[192,104]{1,0:T(8,128)S(1)}) custom-call(bf16[192,1152]{1,0:T(8,128)(2,1)S(1)} %multiply_convert_fusion.1.normed_ref, bf16[2304,2304]{1,0:T(8,128)(2,1)} %all-gather.3.cloned.1.call-done.in_ref, f32[192,4]{1,0:T(8,128)S(1)} %copy.143.masks_ref, ...), custom_call_target="tpu_custom_call" | custom-call | flops 192 | bytes 192 | tf_op jit(solution)/shard_map/conv_forward/pallas_call | solution.py:277
  136.6 2.4 compare_select_fusion
  141.2 11.3 %scan_forward.1 = f32[2,96,2304]{2,1,0:T(8,128)S(1)} custom-call(f32[2,96,2304]{2,1,0:T(8,128)S(1)} %get-tuple-element.381.decay_ref, f32[2,96,2304]{2,1,0:T(8,128)S(1)} %get-tuple-element.380.drive_ref, f32[2,96,16,128]{3,2,1,0:T(8,128)S(1)} %broadcast_in_dim.107.b_ref, f32[2,96,16,128]{3,2,1,0:T(8,128)S(1)} %broadcast_in_dim.109.c_ref, ...), custom_call_target="tpu_custom_call" | custom-call | flops 442368 | bytes 8454144 | tf_op jit(solution)/shard_map/scan_forward/pallas_call | solution.py:170
  152.6 11.8 %collective-permute-done.11.refs_6_ = bf16[768,1152]{1,0:T(8,128)(2,1)} collective-permute-done((bf16[768,1152]{1,0:T(8,128)(2,1)}, bf16[768,1152]{1,0:T(8,128)(2,1)}, u32[]{:S(2)}, u32[]{:S(2)}) %collective-permute-start.11) | collective-permute-done | bytes 1769504 | tf_op jit(solution)/shard_map/ppermute | solution.py:648
  165.4 4.0 multiply_reduce_fusion.4
  177.4 5.4 %collective-permute-done.17 = bf16[2,32,2304]{2,1,0:T(8,128)(2,1)S(1)} collective-permute-done((bf16[2,32,2304]{2,1,0:T(8,128)(2,1)S(1)}, bf16[2,32,2304]{2,1,0:T(8,128)(2,1)S(1)}, u32[]{:S(2)}, u32[]{:S(2)}) %collective-permute-start.17) | collective-permute-done | bytes 294944 | tf_op jit(solution)/shard_map/send_rows/ppermute | solution.py:1006
  184.2 4.1 collective-permute-done.18
  189.9 5.0 %expert_first.2 = (bf16[256,2304]{1,0:T(8,128)(2,1)S(1)}, bf16[256,1152]{1,0:T(8,128)(2,1)S(1)}, bf16[256,1152]{1,0:T(8,128)(2,1)S(1)}, f32[256,2304]{1,0:T(8,128)S(1)}) custom-call(bf16[64,2304]{1,0:T(8,128)(2,1)S(1)} %bitcast.184, bf16[64,2304]{1,0:T(8,128)(2,1)S(1)} %bitcast.188, bf16[64,2304]{1,0:T(8,128)(2,1)S(1)} %bitcast.190, ...), custom_call_target="tpu_custom_call" | custom-call | flops 256 | bytes 256 | tf_op jit(solution)/shard_map/expert_first/pallas_call | solution.py:521
  194.9 3.2 collective-permute-done.21
  198.2 5.5 %collective-permute-done.22 = bf16[2,32,2304]{2,1,0:T(8,128)(2,1)S(1)} collective-permute-done((bf16[2,32,2304]{2,1,0:T(8,128)(2,1)S(1)}, bf16[2,32,2304]{2,1,0:T(8,128)(2,1)S(1)}, u32[]{:S(2)}, u32[]{:S(2)}) %collective-permute-start.22) | collective-permute-done | bytes 294944 | tf_op jit(solution)/shard_map/send_rows/ppermute | solution.py:1006
  203.7 5.2 %expert_first.3 = (bf16[256,2304]{1,0:T(8,128)(2,1)S(1)}, bf16[256,1152]{1,0:T(8,128)(2,1)S(1)}, bf16[256,1152]{1,0:T(8,128)(2,1)S(1)}, f32[256,2304]{1,0:T(8,128)S(1)}) custom-call(bf16[64,2304]{1,0:T(8,128)(2,1)S(1)} %bitcast.187, bf16[64,2304]{1,0:T(8,128)(2,1)S(1)} %bitcast.186, bf16[64,2304]{1,0:T(8,128)(2,1)S(1)} %bitcast.189, ...), custom_call_target="tpu_custom_call" | custom-call | flops 256 | bytes 256 | tf_op jit(solution)/shard_map/expert_first/pallas_call | solution.py:521
  208.9 3.1 collective-permute-done.23.refs_4_
  212.0 2.8 expert_last.1
  220.1 4.8 %collective-permute-done.25 = bf16[2,32,2304]{2,1,0:T(8,128)(2,1)S(1)} collective-permute-done((bf16[2,32,2304]{2,1,0:T(8,128)(2,1)S(1)}, bf16[2,32,2304]{2,1,0:T(8,128)(2,1)S(1)}, u32[]{:S(2)}, u32[]{:S(2)}) %collective-permute-start.25) | collective-permute-done | bytes 294944 | tf_op jit(solution)/shard_map/send_results/ppermute | solution.py:1006
  225.2 5.1 %collective-permute-done.26 = bf16[2,32,2304]{2,1,0:T(8,128)(2,1)S(1)} collective-permute-done((bf16[2,32,2304]{2,1,0:T(8,128)(2,1)S(1)}, bf16[2,32,2304]{2,1,0:T(8,128)(2,1)S(1)}, u32[]{:S(2)}, u32[]{:S(2)}) %collective-permute-start.26) | collective-permute-done | bytes 294944 | tf_op jit(solution)/shard_map/send_results/ppermute | solution.py:1006
  251.3 8.0 %gate_backward.1 = (bf16[2304,2304]{1,0:T(8,128)(2,1)}, bf16[192,2304]{1,0:T(8,128)(2,1)S(1)}, f32[192,2304]{1,0:T(8,128)S(1)}) custom-call(bf16[192,1152]{1,0:T(8,128)(2,1)S(1)} %fusion.113.d_branch_ref, bf16[192,1152]{1,0:T(8,128)(2,1)S(1)} %copy-done.10, bf16[2304,1152]{1,0:T(8,128)(2,1)S(1)} %bitcast.179, bf16[192,2304]{1,0:T(8,128)(2,1)S(1)} %bitcast.181, ...), custom_call_target="tpu_custom_call" | custom-call | flops 192 | bytes 192 | tf_op jit(solution)/shard_map/gate_backward/pallas_call | solution.py:324
  263.5 33.4 %scan_backward.1 = (f32[2,96,2304]{2,1,0:T(8,128)}, bf16[2,96,2304]{2,1,0:T(8,128)(2,1)}, f32[2,96,72]{2,1,0:T(8,128)}, f32[2,24,2304]{2,1,0:T(8,128)}, f32[2,8,1536]{2,1,0:T(8,128)}, /*index=5*/f32[2,8,1536]{2,1,0:T(8,128)}) custom-call(f32[2,96,2304]{2,1,0:T(8,128)} %copy-done.4, f32[2,96,2304]{2,1,0:T(8,128)} %copy-done.3, f32[2,96,16,128]{3,2,1,0:T(8,128)} %copy-done.7, ...), custom_call_target="tpu_custom_call" | custom-call | flops 442368 | bytes 442368 | tf_op jit(solution)/shard_map/scan_backward/pallas_call | solution.py:194
  296.9 7.7 %collective-permute-done.31 = bf16[768,1152]{1,0:T(8,128)(2,1)} collective-permute-done((bf16[768,1152]{1,0:T(8,128)(2,1)}, bf16[768,1152]{1,0:T(8,128)(2,1)}, u32[]{:S(2)}, u32[]{:S(2)}) %collective-permute-start.31) | collective-permute-done | bytes 1769504 | tf_op jit(solution)/shard_map/ppermute | solution.py:648
  304.6 3.3 add_convert_fusion.1
  315.5 12.0 %conv_backward.1 = (bf16[2304,1360]{1,0:T(8,128)(2,1)S(1)}, f32[192,1152]{1,0:T(8,128)S(1)}) custom-call(f32[192,2304]{1,0:T(8,128)S(1)} %bitcast.182, f32[192,2304]{1,0:T(8,128)S(1)} %copy-done.19, bf16[192,2304]{1,0:T(8,128)(2,1)S(1)} %copy-done.24, bf16[192,104]{1,0:T(8,128)(2,1)S(1)} %pad_maximum_fusion.7.d_proj_ref, bf16[192,1152]{1,0:T(8,128)(2,1)S(1)} %copy-done.10, ...), custom_call_target="tpu_custom_call" | custom-call | flops 192 | bytes 192 | tf_op jit(solution)/shard_map/conv_backward/pallas_call | solution.py:423
  327.5 2.6 copy-done.13
  330.2 19.9 %collective-permute-done.32 = bf16[768,1152]{1,0:T(8,128)(2,1)} collective-permute-done((bf16[768,1152]{1,0:T(8,128)(2,1)}, bf16[768,1152]{1,0:T(8,128)(2,1)}, u32[]{:S(2)}, u32[]{:S(2)}) %collective-permute-start.32) | collective-permute-done | bytes 1769504 | tf_op jit(solution)/shard_map/ppermute | solution.py:648
  352.6 7.5 %collective-permute-done.33 = bf16[2,1,72,1152]{3,2,1,0:T(8,128)(2,1)S(1)} collective-permute-done((bf16[2,1,72,1152]{3,2,1,0:T(8,128)(2,1)S(1)}, bf16[2,1,72,1152]{3,2,1,0:T(8,128)(2,1)S(1)}, u32[]{:S(2)}, u32[]{:S(2)}) %collective-permute-start.33) | collective-permute-done | bytes 331808 | tf_op jit(solution)/shard_map/ppermute | solution.py:648
  360.7 1.8 collective-permute-start.34
  362.5 3.8 add_convert_fusion
  367.5 6.7 %collective-permute-done.35 = bf16[72,1152]{1,0:T(8,128)(2,1)S(1)} collective-permute-done((bf16[72,1152]{1,0:T(8,128)(2,1)S(1)}, bf16[72,1152]{1,0:T(8,128)(2,1)S(1)}, u32[]{:S(2)}, u32[]{:S(2)}) %collective-permute-start.35) | collective-permute-done | bytes 165920 | tf_op jit(solution)/shard_map/ppermute | solution.py:648
  377.9 3.9 collective-permute-done.42
  382.7 32.1 %collective-permute-done.37 = bf16[768,1152]{1,0:T(8,128)(2,1)} collective-permute-done((bf16[768,1152]{1,0:T(8,128)(2,1)}, bf16[768,1152]{1,0:T(8,128)(2,1)}, u32[]{:S(2)}, u32[]{:S(2)}) %collective-permute-start.37) | collective-permute-done | bytes 1769504 | tf_op jit(solution)/shard_map/ppermute | solution.py:648
  416.1 2.3 collective-permute-start.40
  418.8 1.9 collective-permute-start.38
  424.5 2.3 collective-permute-done.40
  426.8 20.4 %collective-permute-done.39 = bf16[2,72,1152]{2,1,0:T(8,128)(2,1)S(1)} collective-permute-done((bf16[2,72,1152]{2,1,0:T(8,128)(2,1)S(1)}, bf16[2,72,1152]{2,1,0:T(8,128)(2,1)S(1)}, u32[]{:S(2)}, u32[]{:S(2)}) %collective-permute-start.39) | collective-permute-done | bytes 331808 | tf_op jit(solution)/shard_map/ppermute | solution.py:648
  448.4 3.6 convert_add_fusion
  453.0 3.4 collective-permute-start.53
  457.1 2.8 collective-permute-start.49
  461.1 4.0 slice_bitcast_fusion
  (409 shorter events, 118.4 us)
Async XLA Ops:
  7.2 120.4 %all-gather.3.cloned.1.call-start = ((), (), s32[]{:S(2)}) async-start(), calls=%async_computation.2 | async-start | bytes 11943936 | tf_op jit(solution)/shard_map/fetch_in/all_gather | solution.py:679
  8.5 14.4 %collective-permute-start = (bf16[1,144,1152]{2,1,0:T(8,128)(2,1)S(1)}, bf16[1,144,1152]{2,1,0:T(8,128)(2,1)S(1)}, u32[]{:S(2)}, u32[]{:S(2)}) collective-permute-start(bf16[1,144,1152]{2,1,0:T(8,128)(2,1)S(1)} %bitcast.228), channel_id=1, source_target_pairs={{0,8},{4,12},{8,16},{12,20},{16,24},{20,28},{24,0},{28,4},{1,9},{5... | collective-permute-start | bytes 995336 | tf_op jit(solution)/shard_map/ppermute | solution.py:648
  23.0 11.1 %collective-permute-start.2 = (bf16[1,144,1152]{2,1,0:T(8,128)(2,1)S(1)}, bf16[1,144,1152]{2,1,0:T(8,128)(2,1)S(1)}, u32[]{:S(2)}, u32[]{:S(2)}) collective-permute-start(bf16[1,144,1152]{2,1,0:T(8,128)(2,1)S(1)} %collective-permute-done), channel_id=1, source_target_pairs={{0,8},{4,12},{8,16},{12,20},{16,24},{20,28},{24,0},{28,4},{1,9},{5... | collective-permute-start | bytes 995336 | tf_op jit(solution)/shard_map/ppermute | solution.py:648
  23.0 11.1 %collective-permute-start.3 = (bf16[1,72,199]{2,1,0:T(8,128)(2,1)S(1)}, bf16[1,72,199]{2,1,0:T(8,128)(2,1)S(1)}, u32[]{:S(2)}, u32[]{:S(2)}) collective-permute-start(bf16[1,72,199]{2,1,0:T(8,128)(2,1)S(1)} %collective-permute-done.1), channel_id=1, source_target_pairs={{0,8},{4,12},{8,16},{12,20},{16,24},{20,28},{24,0},{28,4},{1,9},{5... | collective-permute-start | bytes 85976 | tf_op jit(solution)/shard_map/ppermute | solution.py:648
  34.1 10.2 %collective-permute-start.4 = (bf16[1,144,1152]{2,1,0:T(8,128)(2,1)S(1)}, bf16[1,144,1152]{2,1,0:T(8,128)(2,1)S(1)}, u32[]{:S(2)}, u32[]{:S(2)}) collective-permute-start(bf16[1,144,1152]{2,1,0:T(8,128)(2,1)S(1)} %collective-permute-done.2), channel_id=1, source_target_pairs={{0,8},{4,12},{8,16},{12,20},{16,24},{20,28},{24,0},{28,4},{1,9},{5... | collective-permute-start | bytes 995336 | tf_op jit(solution)/shard_map/ppermute | solution.py:648
  34.1 10.2 %collective-permute-start.5 = (bf16[1,72,199]{2,1,0:T(8,128)(2,1)S(1)}, bf16[1,72,199]{2,1,0:T(8,128)(2,1)S(1)}, u32[]{:S(2)}, u32[]{:S(2)}) collective-permute-start(bf16[1,72,199]{2,1,0:T(8,128)(2,1)S(1)} %collective-permute-done.3), channel_id=1, source_target_pairs={{0,8},{4,12},{8,16},{12,20},{16,24},{20,28},{24,0},{28,4},{1,9},{5... | collective-permute-start | bytes 85976 | tf_op jit(solution)/shard_map/ppermute | solution.py:648
  45.9 119.3 %all-gather.5.cloned.1.call-start = ((), (), s32[]{:S(2)}) async-start(), calls=%async_computation.3 | async-start | bytes 5971968 | tf_op jit(solution)/shard_map/fetch_out/all_gather | solution.py:679
  48.4 39.5 %collective-permute-start.10 = (bf16[768,1152]{1,0:T(8,128)(2,1)S(1)}, bf16[768,1152]{1,0:T(8,128)(2,1)}, u32[]{:S(2)}, u32[]{:S(2)}) collective-permute-start(bf16[768,1152]{1,0:T(8,128)(2,1)S(1)} %pad_maximum_fusion.refs_4_), channel_id=1, source_target_pairs={{0,8},{4,12},{8,16},{12,20},{16,24},{20,28},{24,0},{28,4},{1,9},{5... | collective-permute-start | bytes 5308424 | tf_op jit(solution)/shard_map/ppermute | solution.py:648
  56.1 16.0 %collective-permute-start.8 = (bf16[1,576,199]{2,1,0:T(8,128)(2,1)S(1)}, bf16[1,576,199]{2,1,0:T(8,128)(2,1)S(1)}, u32[]{:S(2)}, u32[]{:S(2)}) collective-permute-start(bf16[1,576,199]{2,1,0:T(8,128)(2,1)S(1)} %bitcast.231), channel_id=1, source_target_pairs={{0,2},{1,3},{2,0},{3,1},{4,6},{5,7},{6,4},{7,5},{8,10},{9,11},{10,... | collective-permute-start | bytes 687752 | tf_op jit(solution)/shard_map/ppermute | solution.py:648
  72.6 16.3 %collective-permute-start.9 = (bf16[1,1152,199]{1,2,0:T(8,128)(2,1)S(1)}, bf16[1,1152,199]{1,2,0:T(8,128)(2,1)S(1)}, u32[]{:S(2)}, u32[]{:S(2)}) collective-permute-start(bf16[1,1152,199]{1,2,0:T(8,128)(2,1)S(1)} %copy.154), channel_id=1, source_target_pairs={{0,4},{4,0},{8,12},{12,8},{16,20},{20,16},{24,28},{28,24},{1,5},{5... | collective-permute-start | bytes 1375496 | tf_op jit(solution)/shard_map/ppermute | solution.py:648
  89.0 7.5 %collective-permute-start.12 = (bf16[1,72,1152]{2,1,0:T(8,128)(2,1)}, bf16[1,72,1152]{2,1,0:T(8,128)(2,1)}, u32[]{:S(2)}, u32[]{:S(2)}) collective-permute-start(bf16[1,72,1152]{2,1,0:T(8,128)(2,1)} %bitcast.19), channel_id=1, source_target_pairs={{0,8},{4,12},{8,16},{12,20},{16,24},{20,28},{24,0},{28,4},{1,9},{5... | collective-permute-start | bytes 497672 | tf_op jit(solution)/shard_map/ppermute | solution.py:648
  96.4 8.6 %collective-permute-start.13 = (bf16[1,72,1152]{2,1,0:T(8,128)(2,1)}, bf16[1,72,1152]{2,1,0:T(8,128)(2,1)S(1)}, u32[]{:S(2)}, u32[]{:S(2)}) collective-permute-start(bf16[1,72,1152]{2,1,0:T(8,128)(2,1)} %collective-permute-done.12), channel_id=1, source_target_pairs={{0,8},{4,12},{8,16},{12,20},{16,24},{20,28},{24,0},{28,4},{1,9},{5... | collective-permute-start | bytes 497672 | tf_op jit(solution)/shard_map/ppermute | solution.py:648
  105.1 7.1 %collective-permute-start.14 = (bf16[1,72,1152]{2,1,0:T(8,128)(2,1)S(1)}, bf16[1,72,1152]{2,1,0:T(8,128)(2,1)S(1)}, u32[]{:S(2)}, u32[]{:S(2)}) collective-permute-start(bf16[1,72,1152]{2,1,0:T(8,128)(2,1)S(1)} %collective-permute-done.13), channel_id=1, source_target_pairs={{0,8},{4,12},{8,16},{12,20},{16,24},{20,28},{24,0},{28,4},{1,9},{5... | collective-permute-start | bytes 497672 | tf_op jit(solution)/shard_map/ppermute | solution.py:648
  115.3 7.8 %collective-permute-start.15 = (bf16[2,1,72,1152]{3,2,1,0:T(8,128)(2,1)S(1)}, bf16[2,1,72,1152]{3,2,1,0:T(8,128)(2,1)S(1)}, u32[]{:S(2)}, u32[]{:S(2)}) collective-permute-start(bf16[2,1,72,1152]{3,2,1,0:T(8,128)(2,1)S(1)} %get-tuple-element.394), channel_id=1, source_target_pairs={{0,4},{4,0},{8,12},{12,8},{16,20},{20,16},{24,28},{28,24},{1,5},{5... | collective-permute-start | bytes 995336 | tf_op jit(solution)/shard_map/ppermute | solution.py:648
  124.1 226.0 %reduce-scatter.3.cloned.1.call-start = ((), (), s32[]{:S(2)}) async-start(), calls=%async_computation.4 | async-start | bytes 11943936 | tf_op jit(solution)/shard_map/reduce_out_gate/reduce_scatter | solution.py:683
  125.4 39.0 %collective-permute-start.11 = (bf16[768,1152]{1,0:T(8,128)(2,1)}, bf16[768,1152]{1,0:T(8,128)(2,1)}, u32[]{:S(2)}, u32[]{:S(2)}) collective-permute-start(bf16[768,1152]{1,0:T(8,128)(2,1)} %collective-permute-done.10.refs_5_), channel_id=1, source_target_pairs={{0,8},{4,12},{8,16},{12,20},{16,24},{20,28},{24,0},{28,4},{1,9},{5... | collective-permute-start | bytes 5308424 | tf_op jit(solution)/shard_map/ppermute | solution.py:648
  169.4 42.6 %collective-permute-start.23 = (bf16[768,1152]{1,0:T(8,128)(2,1)}, bf16[768,1152]{1,0:T(8,128)(2,1)S(1)}, u32[]{:S(2)}, u32[]{:S(2)}) collective-permute-start(bf16[768,1152]{1,0:T(8,128)(2,1)} %collective-permute-done.11.refs_6_), channel_id=1, source_target_pairs={{0,8},{4,12},{8,16},{12,20},{16,24},{20,28},{24,0},{28,4},{1,9},{5... | collective-permute-start | bytes 5308424 | tf_op jit(solution)/shard_map/ppermute | solution.py:648
  172.9 9.9 %collective-permute-start.17 = (bf16[2,32,2304]{2,1,0:T(8,128)(2,1)S(1)}, bf16[2,32,2304]{2,1,0:T(8,128)(2,1)S(1)}, u32[]{:S(2)}, u32[]{:S(2)}) collective-permute-start(bf16[2,32,2304]{2,1,0:T(8,128)(2,1)S(1)} %convolution_convert_fusion.1), channel_id=1, source_target_pairs={{0,2},{1,3},{2,0},{3,1},{4,6},{5,7},{6,4},{7,5},{8,10},{9,11},{10,... | collective-permute-start | bytes 884744 | tf_op jit(solution)/shard_map/send_rows/ppermute | solution.py:1006
  174.5 13.8 %collective-permute-start.18 = (bf16[2,32,2304]{2,1,0:T(8,128)(2,1)S(1)}, bf16[2,32,2304]{2,1,0:T(8,128)(2,1)S(1)}, u32[]{:S(2)}, u32[]{:S(2)}) collective-permute-start(bf16[2,32,2304]{2,1,0:T(8,128)(2,1)S(1)} %convolution_convert_fusion), channel_id=1, source_target_pairs={{0,3},{1,2},{2,1},{3,0},{4,7},{5,6},{6,5},{7,4},{8,11},{9,10},{10,... | collective-permute-start | bytes 884744 | tf_op jit(solution)/shard_map/send_rows/ppermute | solution.py:1006
  175.1 19.8 %collective-permute-start.20 = (bf16[2,32,2304]{2,1,0:T(8,128)(2,1)S(1)}, bf16[2,32,2304]{2,1,0:T(8,128)(2,1)S(1)}, u32[]{:S(2)}, u32[]{:S(2)}) collective-permute-start(bf16[2,32,2304]{2,1,0:T(8,128)(2,1)S(1)} %convolution_convert_fusion.2), channel_id=1, source_target_pairs={{0,5},{1,4},{2,7},{3,6},{4,1},{5,0},{6,3},{7,2},{8,13},{9,12},{10,... | collective-permute-start | bytes 884744 | tf_op jit(solution)/shard_map/send_rows/ppermute | solution.py:1006
  176.8 18.2 %collective-permute-start.19 = (bf16[2,32,2304]{2,1,0:T(8,128)(2,1)S(1)}, bf16[2,32,2304]{2,1,0:T(8,128)(2,1)S(1)}, u32[]{:S(2)}, u32[]{:S(2)}) collective-permute-start(bf16[2,32,2304]{2,1,0:T(8,128)(2,1)S(1)} %convolution_convert_fusion.3), channel_id=1, source_target_pairs={{0,4},{1,5},{2,6},{3,7},{4,0},{5,1},{6,2},{7,3},{8,12},{9,13},{10,... | collective-permute-start | bytes 884744 | tf_op jit(solution)/shard_map/send_rows/ppermute | solution.py:1006
  182.8 15.4 %collective-permute-start.21 = (bf16[2,32,2304]{2,1,0:T(8,128)(2,1)S(1)}, bf16[2,32,2304]{2,1,0:T(8,128)(2,1)S(1)}, u32[]{:S(2)}, u32[]{:S(2)}) collective-permute-start(bf16[2,32,2304]{2,1,0:T(8,128)(2,1)S(1)} %convolution_convert_fusion.1), channel_id=1, source_target_pairs={{0,6},{1,7},{2,4},{3,5},{4,2},{5,3},{6,0},{7,1},{8,14},{9,15},{10,... | collective-permute-start | bytes 884744 | tf_op jit(solution)/shard_map/send_rows/ppermute | solution.py:1006
  188.3 15.4 %collective-permute-start.22 = (bf16[2,32,2304]{2,1,0:T(8,128)(2,1)S(1)}, bf16[2,32,2304]{2,1,0:T(8,128)(2,1)S(1)}, u32[]{:S(2)}, u32[]{:S(2)}) collective-permute-start(bf16[2,32,2304]{2,1,0:T(8,128)(2,1)S(1)} %convolution_convert_fusion), channel_id=1, source_target_pairs={{0,7},{1,6},{2,5},{3,4},{4,3},{5,2},{6,1},{7,0},{8,15},{9,14},{10,... | collective-permute-start | bytes 884744 | tf_op jit(solution)/shard_map/send_rows/ppermute | solution.py:1006
  215.1 9.9 %collective-permute-start.25 = (bf16[2,32,2304]{2,1,0:T(8,128)(2,1)S(1)}, bf16[2,32,2304]{2,1,0:T(8,128)(2,1)S(1)}, u32[]{:S(2)}, u32[]{:S(2)}) collective-permute-start(bf16[2,32,2304]{2,1,0:T(8,128)(2,1)S(1)} %bitcast.199), channel_id=1, source_target_pairs={{0,2},{1,3},{2,0},{3,1},{4,6},{5,7},{6,4},{7,5},{8,10},{9,11},{10,... | collective-permute-start | bytes 884744 | tf_op jit(solution)/shard_map/send_results/ppermute | solution.py:1006
  216.4 14.0 %collective-permute-start.26 = (bf16[2,32,2304]{2,1,0:T(8,128)(2,1)S(1)}, bf16[2,32,2304]{2,1,0:T(8,128)(2,1)S(1)}, u32[]{:S(2)}, u32[]{:S(2)}) collective-permute-start(bf16[2,32,2304]{2,1,0:T(8,128)(2,1)S(1)} %bitcast.198), channel_id=1, source_target_pairs={{0,3},{1,2},{2,1},{3,0},{4,7},{5,6},{6,5},{7,4},{8,11},{9,10},{10,... | collective-permute-start | bytes 884744 | tf_op jit(solution)/shard_map/send_results/ppermute | solution.py:1006
  216.9 26.6 %collective-permute-start.27 = (bf16[2,32,2304]{2,1,0:T(8,128)(2,1)S(1)}, bf16[2,32,2304]{2,1,0:T(8,128)(2,1)S(1)}, u32[]{:S(2)}, u32[]{:S(2)}) collective-permute-start(bf16[2,32,2304]{2,1,0:T(8,128)(2,1)S(1)} %bitcast.197), channel_id=1, source_target_pairs={{0,4},{1,5},{2,6},{3,7},{4,0},{5,1},{6,2},{7,3},{8,12},{9,13},{10,... | collective-permute-start | bytes 884744 | tf_op jit(solution)/shard_map/send_results/ppermute | solution.py:1006
  218.4 25.1 %collective-permute-start.28 = (bf16[2,32,2304]{2,1,0:T(8,128)(2,1)S(1)}, bf16[2,32,2304]{2,1,0:T(8,128)(2,1)S(1)}, u32[]{:S(2)}, u32[]{:S(2)}) collective-permute-start(bf16[2,32,2304]{2,1,0:T(8,128)(2,1)S(1)} %bitcast.196), channel_id=1, source_target_pairs={{0,5},{1,4},{2,7},{3,6},{4,1},{5,0},{6,3},{7,2},{8,13},{9,12},{10,... | collective-permute-start | bytes 884744 | tf_op jit(solution)/shard_map/send_results/ppermute | solution.py:1006
  218.6 24.9 %collective-permute-start.29 = (bf16[2,32,2304]{2,1,0:T(8,128)(2,1)S(1)}, bf16[2,32,2304]{2,1,0:T(8,128)(2,1)S(1)}, u32[]{:S(2)}, u32[]{:S(2)}) collective-permute-start(bf16[2,32,2304]{2,1,0:T(8,128)(2,1)S(1)} %bitcast.195), channel_id=1, source_target_pairs={{0,6},{1,7},{2,4},{3,5},{4,2},{5,3},{6,0},{7,1},{8,14},{9,15},{10,... | collective-permute-start | bytes 884744 | tf_op jit(solution)/shard_map/send_results/ppermute | solution.py:1006
  224.9 20.3 %collective-permute-start.30 = (bf16[2,32,2304]{2,1,0:T(8,128)(2,1)S(1)}, bf16[2,32,2304]{2,1,0:T(8,128)(2,1)S(1)}, u32[]{:S(2)}, u32[]{:S(2)}) collective-permute-start(bf16[2,32,2304]{2,1,0:T(8,128)(2,1)S(1)} %bitcast.194), channel_id=1, source_target_pairs={{0,7},{1,6},{2,5},{3,4},{4,3},{5,2},{6,1},{7,0},{8,15},{9,14},{10,... | collective-permute-start | bytes 884744 | tf_op jit(solution)/shard_map/send_results/ppermute | solution.py:1006
  261.5 153.3 %reduce-scatter.5.cloned.1.call-start = ((), (), s32[]{:S(2)}) async-start(), calls=%async_computation.5 | async-start | bytes 7299072 | tf_op jit(solution)/shard_map/reduce_inner/reduce_scatter | solution.py:683
  261.5 43.1 %collective-permute-start.31 = (bf16[768,1152]{1,0:T(8,128)(2,1)}, bf16[768,1152]{1,0:T(8,128)(2,1)}, u32[]{:S(2)}, u32[]{:S(2)}) collective-permute-start(bf16[768,1152]{1,0:T(8,128)(2,1)} %pad_maximum_fusion.2), channel_id=1, source_target_pairs={{0,8},{4,12},{8,16},{12,20},{16,24},{20,28},{24,0},{28,4},{1,9},{5... | collective-permute-start | bytes 5308424 | tf_op jit(solution)/shard_map/ppermute | solution.py:648
  307.9 42.2 %collective-permute-start.32 = (bf16[768,1152]{1,0:T(8,128)(2,1)}, bf16[768,1152]{1,0:T(8,128)(2,1)}, u32[]{:S(2)}, u32[]{:S(2)}) collective-permute-start(bf16[768,1152]{1,0:T(8,128)(2,1)} %add_convert_fusion.1), channel_id=1, source_target_pairs={{0,8},{4,12},{8,16},{12,20},{16,24},{20,28},{24,0},{28,4},{1,9},{5... | collective-permute-start | bytes 5308424 | tf_op jit(solution)/shard_map/ppermute | solution.py:648
  351.6 8.4 %collective-permute-start.33 = (bf16[2,1,72,1152]{3,2,1,0:T(8,128)(2,1)S(1)}, bf16[2,1,72,1152]{3,2,1,0:T(8,128)(2,1)S(1)}, u32[]{:S(2)}, u32[]{:S(2)}) collective-permute-start(bf16[2,1,72,1152]{3,2,1,0:T(8,128)(2,1)S(1)} %get-tuple-element.392), channel_id=1, source_target_pairs={{0,4},{4,0},{8,12},{12,8},{16,20},{20,16},{24,28},{28,24},{1,5},{5... | collective-permute-start | bytes 995336 | tf_op jit(solution)/shard_map/ppermute | solution.py:648
  360.3 7.2 %collective-permute-start.36 = (bf16[72,1152]{1,0:T(8,128)(2,1)S(1)}, bf16[72,1152]{1,0:T(8,128)(2,1)S(1)}, u32[]{:S(2)}, u32[]{:S(2)}) collective-permute-start(bf16[72,1152]{1,0:T(8,128)(2,1)S(1)} %get-tuple-element.388), channel_id=1, source_target_pairs={{0,24},{4,28},{8,0},{12,4},{16,8},{20,12},{24,16},{28,20},{1,25},{... | collective-permute-start | bytes 497672 | tf_op jit(solution)/shard_map/ppermute | solution.py:648
  360.4 13.8 %collective-permute-start.35 = (bf16[72,1152]{1,0:T(8,128)(2,1)S(1)}, bf16[72,1152]{1,0:T(8,128)(2,1)S(1)}, u32[]{:S(2)}, u32[]{:S(2)}) collective-permute-start(bf16[72,1152]{1,0:T(8,128)(2,1)S(1)} %get-tuple-element.389), channel_id=1, source_target_pairs={{0,16},{4,20},{8,24},{12,28},{16,0},{20,4},{24,8},{28,12},{1,17},{... | collective-permute-start | bytes 497672 | tf_op jit(solution)/shard_map/ppermute | solution.py:648
  360.7 13.5 %collective-permute-start.34 = (bf16[72,1152]{1,0:T(8,128)(2,1)S(1)}, bf16[72,1152]{1,0:T(8,128)(2,1)S(1)}, u32[]{:S(2)}, u32[]{:S(2)}) collective-permute-start(bf16[72,1152]{1,0:T(8,128)(2,1)S(1)} %get-tuple-element.390), channel_id=1, source_target_pairs={{0,8},{4,12},{8,16},{12,20},{16,24},{20,28},{24,0},{28,4},{1,9},{5... | collective-permute-start | bytes 497672 | tf_op jit(solution)/shard_map/ppermute | solution.py:648
  374.2 40.5 %collective-permute-start.37 = (bf16[768,1152]{1,0:T(8,128)(2,1)}, bf16[768,1152]{1,0:T(8,128)(2,1)}, u32[]{:S(2)}, u32[]{:S(2)}) collective-permute-start(bf16[768,1152]{1,0:T(8,128)(2,1)} %add_convert_fusion), channel_id=1, source_target_pairs={{0,8},{4,12},{8,16},{12,20},{16,24},{20,28},{24,0},{28,4},{1,9},{5... | collective-permute-start | bytes 5308424 | tf_op jit(solution)/shard_map/ppermute | solution.py:648
  381.9 40.3 %collective-permute-start.43 = (f32[6,1152]{1,0:T(8,128)S(1)}, f32[6,1152]{1,0:T(8,128)S(1)}, u32[]{:S(2)}, u32[]{:S(2)}) collective-permute-start(f32[6,1152]{1,0:T(8,128)S(1)} %add.394), channel_id=1, source_target_pairs={{0,4},{4,0},{8,12},{12,8},{16,20},{20,16},{24,28},{28,24},{1,5},{5... | collective-permute-start | bytes 82952 | tf_op jit(solution)/shard_map/ppermute | solution.py:633
  416.1 10.7 %collective-permute-start.40 = (bf16[2,72,1152]{2,1,0:T(8,128)(2,1)S(1)}, bf16[2,72,1152]{2,1,0:T(8,128)(2,1)S(1)}, u32[]{:S(2)}, u32[]{:S(2)}) collective-permute-start(bf16[2,72,1152]{2,1,0:T(8,128)(2,1)S(1)} %get-tuple-element.382), channel_id=1, source_target_pairs={{0,24},{4,28},{8,0},{12,4},{16,8},{20,12},{24,16},{28,20},{1,25},{... | collective-permute-start | bytes 995336 | tf_op jit(solution)/shard_map/ppermute | solution.py:648
  418.4 28.7 %collective-permute-start.39 = (bf16[2,72,1152]{2,1,0:T(8,128)(2,1)S(1)}, bf16[2,72,1152]{2,1,0:T(8,128)(2,1)S(1)}, u32[]{:S(2)}, u32[]{:S(2)}) collective-permute-start(bf16[2,72,1152]{2,1,0:T(8,128)(2,1)S(1)} %get-tuple-element.383), channel_id=1, source_target_pairs={{0,16},{4,20},{8,24},{12,28},{16,0},{20,4},{24,8},{28,12},{1,17},{... | collective-permute-start | bytes 995336 | tf_op jit(solution)/shard_map/ppermute | solution.py:648
  418.8 28.4 %collective-permute-start.38 = (bf16[2,72,1152]{2,1,0:T(8,128)(2,1)S(1)}, bf16[2,72,1152]{2,1,0:T(8,128)(2,1)S(1)}, u32[]{:S(2)}, u32[]{:S(2)}) collective-permute-start(bf16[2,72,1152]{2,1,0:T(8,128)(2,1)S(1)} %get-tuple-element.384), channel_id=1, source_target_pairs={{0,8},{4,12},{8,16},{12,20},{16,24},{20,28},{24,0},{28,4},{1,9},{5... | collective-permute-start | bytes 995336 | tf_op jit(solution)/shard_map/ppermute | solution.py:648
  422.2 34.3 %collective-permute-start.45 = (bf16[1,1,72,1152]{3,2,1,0:T(8,128)(2,1)S(1)}, bf16[1,1,72,1152]{3,2,1,0:T(8,128)(2,1)S(1)}, u32[]{:S(2)}, u32[]{:S(2)}) collective-permute-start(bf16[1,1,72,1152]{3,2,1,0:T(8,128)(2,1)S(1)} %bitcast.239), channel_id=1, source_target_pairs={{0,2},{1,3},{2,0},{3,1},{4,6},{5,7},{6,4},{7,5},{8,10},{9,11},{10,... | collective-permute-start | bytes 497672 | tf_op jit(solution)/shard_map/ppermute | solution.py:648
  423.1 28.8 %collective-permute-start.50 = (bf16[2,1,72,208]{3,2,1,0:T(8,128)(2,1)S(1)}, bf16[2,1,72,208]{3,2,1,0:T(8,128)(2,1)S(1)}, u32[]{:S(2)}, u32[]{:S(2)}) collective-permute-start(bf16[2,1,72,208]{3,2,1,0:T(8,128)(2,1)S(1)} %get-tuple-element.403), channel_id=1, source_target_pairs={{0,4},{4,0},{8,12},{12,8},{16,20},{20,16},{24,28},{28,24},{1,5},{5... | collective-permute-start | bytes 179720 | tf_op jit(solution)/shard_map/ppermute | solution.py:648
  447.4 9.7 %collective-permute-start.44 = (bf16[1,2,72,1152]{3,2,1,0:T(8,128)(2,1)S(1)}, bf16[1,2,72,1152]{3,2,1,0:T(8,128)(2,1)S(1)}, u32[]{:S(2)}, u32[]{:S(2)}) collective-permute-start(bf16[1,2,72,1152]{3,2,1,0:T(8,128)(2,1)S(1)} %fusion.66), channel_id=1, source_target_pairs={{0,2},{1,3},{2,0},{3,1},{4,6},{5,7},{6,4},{7,5},{8,10},{9,11},{10,... | collective-permute-start | bytes 995336 | tf_op jit(solution)/shard_map/ppermute | solution.py:648
  453.0 7.5 %collective-permute-start.53 = (bf16[72,208]{0,1:T(8,128)(2,1)S(1)}, bf16[72,208]{0,1:T(8,128)(2,1)S(1)}, u32[]{:S(2)}, u32[]{:S(2)}) collective-permute-start(bf16[72,208]{0,1:T(8,128)(2,1)S(1)} %get-tuple-element.399), channel_id=1, source_target_pairs={{0,24},{4,28},{8,0},{12,4},{16,8},{20,12},{24,16},{28,20},{1,25},{... | collective-permute-start | bytes 89864 | tf_op jit(solution)/shard_map/ppermute | solution.py:648
  456.5 8.6 %collective-permute-start.52 = (bf16[72,208]{0,1:T(8,128)(2,1)S(1)}, bf16[72,208]{0,1:T(8,128)(2,1)S(1)}, u32[]{:S(2)}, u32[]{:S(2)}) collective-permute-start(bf16[72,208]{0,1:T(8,128)(2,1)S(1)} %get-tuple-element.400), channel_id=1, source_target_pairs={{0,16},{4,20},{8,24},{12,28},{16,0},{20,4},{24,8},{28,12},{1,17},{... | collective-permute-start | bytes 89864 | tf_op jit(solution)/shard_map/ppermute | solution.py:648
  456.5 8.6 %collective-permute-start.51 = (bf16[72,208]{0,1:T(8,128)(2,1)S(1)}, bf16[72,208]{0,1:T(8,128)(2,1)S(1)}, u32[]{:S(2)}, u32[]{:S(2)}) collective-permute-start(bf16[72,208]{0,1:T(8,128)(2,1)S(1)} %get-tuple-element.401), channel_id=1, source_target_pairs={{0,8},{4,12},{8,16},{12,20},{16,24},{20,28},{24,0},{28,4},{1,9},{5... | collective-permute-start | bytes 89864 | tf_op jit(solution)/shard_map/ppermute | solution.py:648
  457.1 8.0 %collective-permute-start.49 = (f32[6,1152]{1,0:T(8,128)S(1)}, f32[6,1152]{1,0:T(8,128)S(1)}, u32[]{:S(2)}, u32[]{:S(2)}) collective-permute-start(f32[6,1152]{1,0:T(8,128)S(1)} %add.401), channel_id=1, source_target_pairs={{0,16},{4,20},{8,24},{12,28},{16,0},{20,4},{24,8},{28,12},{1,17},{... | collective-permute-start | bytes 82952 | tf_op jit(solution)/shard_map/ppermute | solution.py:633
  (83 other events, 1075.2 us)
Sparse Core Ops, SparseCore 0:
  46.0 70.2 all-gather.2
  124.3 40.8 all-gather.4
  261.6 80.6 reduce-scatter.2
  350.2 60.8 reduce-scatter.4

commit v5 on v4

--- a/solution.py
+++ b/solution.py
@@ -8,7 +8,7 @@
 from jax.sharding import PartitionSpec as P
 
 LANES = 128
-VMEM_GRANT = 40 << 20
+VMEM_GRANT = 32 << 20
 ROWS = 8
 
 def wide(tile, width):

time: 488 us -> 487 us (level)
    unnamed x167 -> x169, local copies, waits for them, and re-layouts: 23 us -> 27.5 us
  transfers between devices with their start and end apart: 58 -> 58, of which waited for: 32 -> 32; matrix products, arithmetic and copies ran while one was open for 15% -> 15% of each run, Pallas kernels for 16% -> 15%
where the time goes in v5:
time: 487 us; the launch traced here: 480 us
  waiting for transfers between devices  221 us (45%)
  Pallas kernels  83.1 us (17%)
  local copies, waits for them, and re-layouts  55.9 us (11%)
  starting transfers between devices  50.5 us (10%)
  other arithmetic  36.2 us (7%)
  matrix products  17.3 us (4%)
  between operations  15.9 us (3%)
    ppermute x35, waiting for transfers between devices, hop(): return lax.ppermute(values, self.axis_name, pairs)  186 us
    pallas_call x1, Pallas kernels, run_backward(): pl.pallas_call(scan_backward, grid=(count, channels // width), in_specs=[...  33.4 us
    ppermute x35, starting transfers between devices, hop(): return lax.ppermute(values, self.axis_name, pairs)  32.4 us
    ppermute x14, waiting for transfers between devices, exchange(): return lax.ppermute(piece, BOTH, partners(cross, k))  29.9 us
    unnamed x169, local copies, waits for them, and re-layouts  27.5 us
    ppermute x14, starting transfers between devices, exchange(): return lax.ppermute(piece, BOTH, partners(cross, k))  12.4 us
    dot_general x18, matrix products, dot(): lax.dot_general(left, right, (contract, ((), ())), preferred_element_type...  12.1 us
    pallas_call x1, Pallas kernels, run_conv_backward(): pl.pallas_call(conv_backward, grid=(channels // width,), in_specs=[tokens...  12 us
  transfers between devices with their start and end apart: 58, of which 32 were waited for; matrix products, arithmetic and copies ran while one was open for 15% of the time, Pallas kernels for 15%

profile of v5, /device:TPU:0, one launch (start us, length us, event | category | flops | bytes accessed | tf_op | source)
XLA Modules:
  0.0 480.3 jit_solution(2130940503542710024)
XLA Ops:
  8.5 3.1 collective-permute-start
  18.8 4.2 collective-permute-done.1
  24.3 9.8 %collective-permute-done.3 = bf16[1,72,199]{2,1,0:T(8,128)(2,1)S(1)} collective-permute-done((bf16[1,72,199]{2,1,0:T(8,128)(2,1)S(1)}, bf16[1,72,199]{2,1,0:T(8,128)(2,1)S(1)}, u32[]{:S(2)}, u32[]{:S(2)}) %collective-permute-start.3) | collective-permute-done | bytes 28688 | tf_op jit(solution)/shard_map/ppermute | solution.py:648
  34.1 10.2 %collective-permute-done.5 = bf16[1,72,199]{2,1,0:T(8,128)(2,1)S(1)} collective-permute-done((bf16[1,72,199]{2,1,0:T(8,128)(2,1)S(1)}, bf16[1,72,199]{2,1,0:T(8,128)(2,1)S(1)}, u32[]{:S(2)}, u32[]{:S(2)}) %collective-permute-start.5) | collective-permute-done | bytes 28688 | tf_op jit(solution)/shard_map/ppermute | solution.py:648
  51.8 2.6 collective-permute-done.6
  57.8 14.2 %collective-permute-done.8 = bf16[1,576,199]{2,1,0:T(8,128)(2,1)S(1)} collective-permute-done((bf16[1,576,199]{2,1,0:T(8,128)(2,1)S(1)}, bf16[1,576,199]{2,1,0:T(8,128)(2,1)S(1)}, u32[]{:S(2)}, u32[]{:S(2)}) %collective-permute-start.8) | collective-permute-done | bytes 229280 | tf_op jit(solution)/shard_map/ppermute | solution.py:648
  72.6 2.5 collective-permute-start.9
  77.6 10.3 %collective-permute-done.10.refs_5_ = bf16[768,1152]{1,0:T(8,128)(2,1)} collective-permute-done((bf16[768,1152]{1,0:T(8,128)(2,1)S(1)}, bf16[768,1152]{1,0:T(8,128)(2,1)}, u32[]{:S(2)}, u32[]{:S(2)}) %collective-permute-start.10) | collective-permute-done | bytes 1769504 | tf_op jit(solution)/shard_map/ppermute | solution.py:648
  96.4 8.6 %collective-permute-done.13 = bf16[1,72,1152]{2,1,0:T(8,128)(2,1)S(1)} collective-permute-done((bf16[1,72,1152]{2,1,0:T(8,128)(2,1)}, bf16[1,72,1152]{2,1,0:T(8,128)(2,1)S(1)}, u32[]{:S(2)}, u32[]{:S(2)}) %collective-permute-start.13) | collective-permute-done | bytes 165920 | tf_op jit(solution)/shard_map/ppermute | solution.py:648
  105.1 7.1 %collective-permute-done.14 = bf16[1,72,1152]{2,1,0:T(8,128)(2,1)S(1)} collective-permute-done((bf16[1,72,1152]{2,1,0:T(8,128)(2,1)S(1)}, bf16[1,72,1152]{2,1,0:T(8,128)(2,1)S(1)}, u32[]{:S(2)}, u32[]{:S(2)}) %collective-permute-start.14) | collective-permute-done | bytes 165920 | tf_op jit(solution)/shard_map/ppermute | solution.py:648
  115.3 2.7 collective-permute-start.15
  118.0 5.1 %collective-permute-done.15 = bf16[2,1,72,1152]{3,2,1,0:T(8,128)(2,1)S(1)} collective-permute-done((bf16[2,1,72,1152]{3,2,1,0:T(8,128)(2,1)S(1)}, bf16[2,1,72,1152]{3,2,1,0:T(8,128)(2,1)S(1)}, u32[]{:S(2)}, u32[]{:S(2)}) %collective-permute-start.15) | collective-permute-done | bytes 331808 | tf_op jit(solution)/shard_map/ppermute | solution.py:648
  127.6 4.5 copy-done.2
  132.1 5.3 %conv_forward.1 = (f32[192,2304]{1,0:T(8,128)S(1)}, f32[192,2304]{1,0:T(8,128)S(1)}, f32[192,2304]{1,0:T(8,128)S(1)}, f32[192,104]{1,0:T(8,128)S(1)}) custom-call(bf16[192,1152]{1,0:T(8,128)(2,1)S(1)} %multiply_convert_fusion.1.normed_ref, bf16[2304,2304]{1,0:T(8,128)(2,1)S(1)} %copy-done.2, f32[192,4]{1,0:T(8,128)S(1)} %copy.143.masks_ref, ...), custom_call_target="tpu_custom_call" | custom-call | flops 192 | bytes 192 | tf_op jit(solution)/shard_map/conv_forward/pallas_call | solution.py:277
  138.0 2.4 compare_select_fusion
  142.6 11.3 %scan_forward.1 = f32[2,96,2304]{2,1,0:T(8,128)S(1)} custom-call(f32[2,96,2304]{2,1,0:T(8,128)S(1)} %get-tuple-element.381.decay_ref, f32[2,96,2304]{2,1,0:T(8,128)S(1)} %get-tuple-element.380.drive_ref, f32[2,96,16,128]{3,2,1,0:T(8,128)S(1)} %broadcast_in_dim.107.b_ref, f32[2,96,16,128]{3,2,1,0:T(8,128)S(1)} %broadcast_in_dim.109.c_ref, ...), custom_call_target="tpu_custom_call" | custom-call | flops 442368 | bytes 8454144 | tf_op jit(solution)/shard_map/scan_forward/pallas_call | solution.py:170
  154.0 10.4 %collective-permute-done.11.refs_6_ = bf16[768,1152]{1,0:T(8,128)(2,1)} collective-permute-done((bf16[768,1152]{1,0:T(8,128)(2,1)}, bf16[768,1152]{1,0:T(8,128)(2,1)}, u32[]{:S(2)}, u32[]{:S(2)}) %collective-permute-start.11) | collective-permute-done | bytes 1769504 | tf_op jit(solution)/shard_map/ppermute | solution.py:648
  165.4 4.0 multiply_reduce_fusion.4
  177.4 5.4 %collective-permute-done.17 = bf16[2,32,2304]{2,1,0:T(8,128)(2,1)S(1)} collective-permute-done((bf16[2,32,2304]{2,1,0:T(8,128)(2,1)S(1)}, bf16[2,32,2304]{2,1,0:T(8,128)(2,1)S(1)}, u32[]{:S(2)}, u32[]{:S(2)}) %collective-permute-start.17) | collective-permute-done | bytes 294944 | tf_op jit(solution)/shard_map/send_rows/ppermute | solution.py:1006
  184.2 4.1 collective-permute-done.18
  189.9 5.0 %expert_first.2 = (bf16[256,2304]{1,0:T(8,128)(2,1)S(1)}, bf16[256,1152]{1,0:T(8,128)(2,1)S(1)}, bf16[256,1152]{1,0:T(8,128)(2,1)S(1)}, f32[256,2304]{1,0:T(8,128)S(1)}) custom-call(bf16[64,2304]{1,0:T(8,128)(2,1)S(1)} %bitcast.184, bf16[64,2304]{1,0:T(8,128)(2,1)S(1)} %bitcast.188, bf16[64,2304]{1,0:T(8,128)(2,1)S(1)} %bitcast.190, ...), custom_call_target="tpu_custom_call" | custom-call | flops 256 | bytes 256 | tf_op jit(solution)/shard_map/expert_first/pallas_call | solution.py:521
  194.9 3.2 collective-permute-done.21
  198.2 5.5 %collective-permute-done.22 = bf16[2,32,2304]{2,1,0:T(8,128)(2,1)S(1)} collective-permute-done((bf16[2,32,2304]{2,1,0:T(8,128)(2,1)S(1)}, bf16[2,32,2304]{2,1,0:T(8,128)(2,1)S(1)}, u32[]{:S(2)}, u32[]{:S(2)}) %collective-permute-start.22) | collective-permute-done | bytes 294944 | tf_op jit(solution)/shard_map/send_rows/ppermute | solution.py:1006
  203.7 5.2 %expert_first.3 = (bf16[256,2304]{1,0:T(8,128)(2,1)S(1)}, bf16[256,1152]{1,0:T(8,128)(2,1)S(1)}, bf16[256,1152]{1,0:T(8,128)(2,1)S(1)}, f32[256,2304]{1,0:T(8,128)S(1)}) custom-call(bf16[64,2304]{1,0:T(8,128)(2,1)S(1)} %bitcast.187, bf16[64,2304]{1,0:T(8,128)(2,1)S(1)} %bitcast.186, bf16[64,2304]{1,0:T(8,128)(2,1)S(1)} %bitcast.189, ...), custom_call_target="tpu_custom_call" | custom-call | flops 256 | bytes 256 | tf_op jit(solution)/shard_map/expert_first/pallas_call | solution.py:521
  208.9 3.1 collective-permute-done.23.refs_4_
  212.1 2.8 expert_last.1
  220.1 4.9 %collective-permute-done.25 = bf16[2,32,2304]{2,1,0:T(8,128)(2,1)S(1)} collective-permute-done((bf16[2,32,2304]{2,1,0:T(8,128)(2,1)S(1)}, bf16[2,32,2304]{2,1,0:T(8,128)(2,1)S(1)}, u32[]{:S(2)}, u32[]{:S(2)}) %collective-permute-start.25) | collective-permute-done | bytes 294944 | tf_op jit(solution)/shard_map/send_results/ppermute | solution.py:1006
  225.2 5.1 %collective-permute-done.26 = bf16[2,32,2304]{2,1,0:T(8,128)(2,1)S(1)} collective-permute-done((bf16[2,32,2304]{2,1,0:T(8,128)(2,1)S(1)}, bf16[2,32,2304]{2,1,0:T(8,128)(2,1)S(1)}, u32[]{:S(2)}, u32[]{:S(2)}) %collective-permute-start.26) | collective-permute-done | bytes 294944 | tf_op jit(solution)/shard_map/send_results/ppermute | solution.py:1006
  251.3 8.0 %gate_backward.1 = (bf16[2304,2304]{1,0:T(8,128)(2,1)}, bf16[192,2304]{1,0:T(8,128)(2,1)S(1)}, f32[192,2304]{1,0:T(8,128)S(1)}) custom-call(bf16[192,1152]{1,0:T(8,128)(2,1)S(1)} %fusion.113.d_branch_ref, bf16[192,1152]{1,0:T(8,128)(2,1)S(1)} %copy-done.11, bf16[2304,1152]{1,0:T(8,128)(2,1)S(1)} %bitcast.179, bf16[192,2304]{1,0:T(8,128)(2,1)S(1)} %bitcast.181, ...), custom_call_target="tpu_custom_call" | custom-call | flops 192 | bytes 192 | tf_op jit(solution)/shard_map/gate_backward/pallas_call | solution.py:324
  263.4 33.4 %scan_backward.1 = (f32[2,96,2304]{2,1,0:T(8,128)}, bf16[2,96,2304]{2,1,0:T(8,128)(2,1)}, f32[2,96,72]{2,1,0:T(8,128)}, f32[2,24,2304]{2,1,0:T(8,128)}, f32[2,8,1536]{2,1,0:T(8,128)}, /*index=5*/f32[2,8,1536]{2,1,0:T(8,128)}) custom-call(f32[2,96,2304]{2,1,0:T(8,128)} %copy-done.5, f32[2,96,2304]{2,1,0:T(8,128)} %copy-done.4, f32[2,96,16,128]{3,2,1,0:T(8,128)} %copy-done.8, ...), custom_call_target="tpu_custom_call" | custom-call | flops 442368 | bytes 442368 | tf_op jit(solution)/shard_map/scan_backward/pallas_call | solution.py:194
  296.8 7.7 %collective-permute-done.31 = bf16[768,1152]{1,0:T(8,128)(2,1)} collective-permute-done((bf16[768,1152]{1,0:T(8,128)(2,1)}, bf16[768,1152]{1,0:T(8,128)(2,1)}, u32[]{:S(2)}, u32[]{:S(2)}) %collective-permute-start.31) | collective-permute-done | bytes 1769504 | tf_op jit(solution)/shard_map/ppermute | solution.py:648
  304.5 3.3 add_convert_fusion.1
  315.4 12.0 %conv_backward.1 = (bf16[2304,1360]{1,0:T(8,128)(2,1)S(1)}, f32[192,1152]{1,0:T(8,128)S(1)}) custom-call(f32[192,2304]{1,0:T(8,128)S(1)} %bitcast.182, f32[192,2304]{1,0:T(8,128)S(1)} %copy-done.20, bf16[192,2304]{1,0:T(8,128)(2,1)S(1)} %copy-done.25, bf16[192,104]{1,0:T(8,128)(2,1)S(1)} %pad_maximum_fusion.7.d_proj_ref, bf16[192,1152]{1,0:T(8,128)(2,1)S(1)} %copy-done.11, ...), custom_call_target="tpu_custom_call" | custom-call | flops 192 | bytes 192 | tf_op jit(solution)/shard_map/conv_backward/pallas_call | solution.py:423
  327.5 2.6 copy-done.14
  330.1 19.9 %collective-permute-done.32 = bf16[768,1152]{1,0:T(8,128)(2,1)} collective-permute-done((bf16[768,1152]{1,0:T(8,128)(2,1)}, bf16[768,1152]{1,0:T(8,128)(2,1)}, u32[]{:S(2)}, u32[]{:S(2)}) %collective-permute-start.32) | collective-permute-done | bytes 1769504 | tf_op jit(solution)/shard_map/ppermute | solution.py:648
  352.5 7.5 %collective-permute-done.33 = bf16[2,1,72,1152]{3,2,1,0:T(8,128)(2,1)S(1)} collective-permute-done((bf16[2,1,72,1152]{3,2,1,0:T(8,128)(2,1)S(1)}, bf16[2,1,72,1152]{3,2,1,0:T(8,128)(2,1)S(1)}, u32[]{:S(2)}, u32[]{:S(2)}) %collective-permute-start.33) | collective-permute-done | bytes 331808 | tf_op jit(solution)/shard_map/ppermute | solution.py:648
  362.4 3.8 add_convert_fusion
  367.4 6.7 %collective-permute-done.35 = bf16[72,1152]{1,0:T(8,128)(2,1)S(1)} collective-permute-done((bf16[72,1152]{1,0:T(8,128)(2,1)S(1)}, bf16[72,1152]{1,0:T(8,128)(2,1)S(1)}, u32[]{:S(2)}, u32[]{:S(2)}) %collective-permute-start.35) | collective-permute-done | bytes 165920 | tf_op jit(solution)/shard_map/ppermute | solution.py:648
  377.8 3.9 collective-permute-done.42
  382.7 32.1 %collective-permute-done.37 = bf16[768,1152]{1,0:T(8,128)(2,1)} collective-permute-done((bf16[768,1152]{1,0:T(8,128)(2,1)}, bf16[768,1152]{1,0:T(8,128)(2,1)}, u32[]{:S(2)}, u32[]{:S(2)}) %collective-permute-start.37) | collective-permute-done | bytes 1769504 | tf_op jit(solution)/shard_map/ppermute | solution.py:648
  416.0 2.3 collective-permute-start.40
  418.7 1.9 collective-permute-start.38
  424.4 2.3 collective-permute-done.40
  426.7 20.4 %collective-permute-done.39 = bf16[2,72,1152]{2,1,0:T(8,128)(2,1)S(1)} collective-permute-done((bf16[2,72,1152]{2,1,0:T(8,128)(2,1)S(1)}, bf16[2,72,1152]{2,1,0:T(8,128)(2,1)S(1)}, u32[]{:S(2)}, u32[]{:S(2)}) %collective-permute-start.39) | collective-permute-done | bytes 331808 | tf_op jit(solution)/shard_map/ppermute | solution.py:648
  448.3 3.6 convert_add_fusion
  453.0 3.4 collective-permute-start.53
  457.1 2.8 collective-permute-start.49
  461.0 4.0 slice_bitcast_fusion
  (411 shorter events, 120.1 us)
Async XLA Ops:
  7.2 120.4 %all-gather.3.cloned.1.call-start = ((), (), s32[]{:S(2)}) async-start(), calls=%async_computation.2 | async-start | bytes 11943936 | tf_op jit(solution)/shard_map/fetch_in/all_gather | solution.py:679
  8.5 14.4 %collective-permute-start = (bf16[1,144,1152]{2,1,0:T(8,128)(2,1)S(1)}, bf16[1,144,1152]{2,1,0:T(8,128)(2,1)S(1)}, u32[]{:S(2)}, u32[]{:S(2)}) collective-permute-start(bf16[1,144,1152]{2,1,0:T(8,128)(2,1)S(1)} %bitcast.228), channel_id=1, source_target_pairs={{0,8},{4,12},{8,16},{12,20},{16,24},{20,28},{24,0},{28,4},{1,9},{5... | collective-permute-start | bytes 995336 | tf_op jit(solution)/shard_map/ppermute | solution.py:648
  23.0 11.1 %collective-permute-start.2 = (bf16[1,144,1152]{2,1,0:T(8,128)(2,1)S(1)}, bf16[1,144,1152]{2,1,0:T(8,128)(2,1)S(1)}, u32[]{:S(2)}, u32[]{:S(2)}) collective-permute-start(bf16[1,144,1152]{2,1,0:T(8,128)(2,1)S(1)} %collective-permute-done), channel_id=1, source_target_pairs={{0,8},{4,12},{8,16},{12,20},{16,24},{20,28},{24,0},{28,4},{1,9},{5... | collective-permute-start | bytes 995336 | tf_op jit(solution)/shard_map/ppermute | solution.py:648
  23.0 11.1 %collective-permute-start.3 = (bf16[1,72,199]{2,1,0:T(8,128)(2,1)S(1)}, bf16[1,72,199]{2,1,0:T(8,128)(2,1)S(1)}, u32[]{:S(2)}, u32[]{:S(2)}) collective-permute-start(bf16[1,72,199]{2,1,0:T(8,128)(2,1)S(1)} %collective-permute-done.1), channel_id=1, source_target_pairs={{0,8},{4,12},{8,16},{12,20},{16,24},{20,28},{24,0},{28,4},{1,9},{5... | collective-permute-start | bytes 85976 | tf_op jit(solution)/shard_map/ppermute | solution.py:648
  34.1 10.2 %collective-permute-start.4 = (bf16[1,144,1152]{2,1,0:T(8,128)(2,1)S(1)}, bf16[1,144,1152]{2,1,0:T(8,128)(2,1)S(1)}, u32[]{:S(2)}, u32[]{:S(2)}) collective-permute-start(bf16[1,144,1152]{2,1,0:T(8,128)(2,1)S(1)} %collective-permute-done.2), channel_id=1, source_target_pairs={{0,8},{4,12},{8,16},{12,20},{16,24},{20,28},{24,0},{28,4},{1,9},{5... | collective-permute-start | bytes 995336 | tf_op jit(solution)/shard_map/ppermute | solution.py:648
  34.1 10.2 %collective-permute-start.5 = (bf16[1,72,199]{2,1,0:T(8,128)(2,1)S(1)}, bf16[1,72,199]{2,1,0:T(8,128)(2,1)S(1)}, u32[]{:S(2)}, u32[]{:S(2)}) collective-permute-start(bf16[1,72,199]{2,1,0:T(8,128)(2,1)S(1)} %collective-permute-done.3), channel_id=1, source_target_pairs={{0,8},{4,12},{8,16},{12,20},{16,24},{20,28},{24,0},{28,4},{1,9},{5... | collective-permute-start | bytes 85976 | tf_op jit(solution)/shard_map/ppermute | solution.py:648
  45.9 119.3 %all-gather.5.cloned.1.call-start = ((), (), s32[]{:S(2)}) async-start(), calls=%async_computation.3 | async-start | bytes 5971968 | tf_op jit(solution)/shard_map/fetch_out/all_gather | solution.py:679
  48.4 39.5 %collective-permute-start.10 = (bf16[768,1152]{1,0:T(8,128)(2,1)S(1)}, bf16[768,1152]{1,0:T(8,128)(2,1)}, u32[]{:S(2)}, u32[]{:S(2)}) collective-permute-start(bf16[768,1152]{1,0:T(8,128)(2,1)S(1)} %pad_maximum_fusion.refs_4_), channel_id=1, source_target_pairs={{0,8},{4,12},{8,16},{12,20},{16,24},{20,28},{24,0},{28,4},{1,9},{5... | collective-permute-start | bytes 5308424 | tf_op jit(solution)/shard_map/ppermute | solution.py:648
  56.1 16.0 %collective-permute-start.8 = (bf16[1,576,199]{2,1,0:T(8,128)(2,1)S(1)}, bf16[1,576,199]{2,1,0:T(8,128)(2,1)S(1)}, u32[]{:S(2)}, u32[]{:S(2)}) collective-permute-start(bf16[1,576,199]{2,1,0:T(8,128)(2,1)S(1)} %bitcast.231), channel_id=1, source_target_pairs={{0,2},{1,3},{2,0},{3,1},{4,6},{5,7},{6,4},{7,5},{8,10},{9,11},{10,... | collective-permute-start | bytes 687752 | tf_op jit(solution)/shard_map/ppermute | solution.py:648
  72.6 16.3 %collective-permute-start.9 = (bf16[1,1152,199]{1,2,0:T(8,128)(2,1)S(1)}, bf16[1,1152,199]{1,2,0:T(8,128)(2,1)S(1)}, u32[]{:S(2)}, u32[]{:S(2)}) collective-permute-start(bf16[1,1152,199]{1,2,0:T(8,128)(2,1)S(1)} %copy.154), channel_id=1, source_target_pairs={{0,4},{4,0},{8,12},{12,8},{16,20},{20,16},{24,28},{28,24},{1,5},{5... | collective-permute-start | bytes 1375496 | tf_op jit(solution)/shard_map/ppermute | solution.py:648
  89.0 7.5 %collective-permute-start.12 = (bf16[1,72,1152]{2,1,0:T(8,128)(2,1)}, bf16[1,72,1152]{2,1,0:T(8,128)(2,1)}, u32[]{:S(2)}, u32[]{:S(2)}) collective-permute-start(bf16[1,72,1152]{2,1,0:T(8,128)(2,1)} %bitcast.19), channel_id=1, source_target_pairs={{0,8},{4,12},{8,16},{12,20},{16,24},{20,28},{24,0},{28,4},{1,9},{5... | collective-permute-start | bytes 497672 | tf_op jit(solution)/shard_map/ppermute | solution.py:648
  96.4 8.6 %collective-permute-start.13 = (bf16[1,72,1152]{2,1,0:T(8,128)(2,1)}, bf16[1,72,1152]{2,1,0:T(8,128)(2,1)S(1)}, u32[]{:S(2)}, u32[]{:S(2)}) collective-permute-start(bf16[1,72,1152]{2,1,0:T(8,128)(2,1)} %collective-permute-done.12), channel_id=1, source_target_pairs={{0,8},{4,12},{8,16},{12,20},{16,24},{20,28},{24,0},{28,4},{1,9},{5... | collective-permute-start | bytes 497672 | tf_op jit(solution)/shard_map/ppermute | solution.py:648
  105.1 7.1 %collective-permute-start.14 = (bf16[1,72,1152]{2,1,0:T(8,128)(2,1)S(1)}, bf16[1,72,1152]{2,1,0:T(8,128)(2,1)S(1)}, u32[]{:S(2)}, u32[]{:S(2)}) collective-permute-start(bf16[1,72,1152]{2,1,0:T(8,128)(2,1)S(1)} %collective-permute-done.13), channel_id=1, source_target_pairs={{0,8},{4,12},{8,16},{12,20},{16,24},{20,28},{24,0},{28,4},{1,9},{5... | collective-permute-start | bytes 497672 | tf_op jit(solution)/shard_map/ppermute | solution.py:648
  115.3 7.8 %collective-permute-start.15 = (bf16[2,1,72,1152]{3,2,1,0:T(8,128)(2,1)S(1)}, bf16[2,1,72,1152]{3,2,1,0:T(8,128)(2,1)S(1)}, u32[]{:S(2)}, u32[]{:S(2)}) collective-permute-start(bf16[2,1,72,1152]{3,2,1,0:T(8,128)(2,1)S(1)} %get-tuple-element.394), channel_id=1, source_target_pairs={{0,4},{4,0},{8,12},{12,8},{16,20},{20,16},{24,28},{28,24},{1,5},{5... | collective-permute-start | bytes 995336 | tf_op jit(solution)/shard_map/ppermute | solution.py:648
  124.2 225.9 %reduce-scatter.3.cloned.1.call-start = ((), (), s32[]{:S(2)}) async-start(), calls=%async_computation.4 | async-start | bytes 11943936 | tf_op jit(solution)/shard_map/reduce_out_gate/reduce_scatter | solution.py:683
  125.3 39.0 %collective-permute-start.11 = (bf16[768,1152]{1,0:T(8,128)(2,1)}, bf16[768,1152]{1,0:T(8,128)(2,1)}, u32[]{:S(2)}, u32[]{:S(2)}) collective-permute-start(bf16[768,1152]{1,0:T(8,128)(2,1)} %collective-permute-done.10.refs_5_), channel_id=1, source_target_pairs={{0,8},{4,12},{8,16},{12,20},{16,24},{20,28},{24,0},{28,4},{1,9},{5... | collective-permute-start | bytes 5308424 | tf_op jit(solution)/shard_map/ppermute | solution.py:648
  169.4 42.7 %collective-permute-start.23 = (bf16[768,1152]{1,0:T(8,128)(2,1)}, bf16[768,1152]{1,0:T(8,128)(2,1)S(1)}, u32[]{:S(2)}, u32[]{:S(2)}) collective-permute-start(bf16[768,1152]{1,0:T(8,128)(2,1)} %collective-permute-done.11.refs_6_), channel_id=1, source_target_pairs={{0,8},{4,12},{8,16},{12,20},{16,24},{20,28},{24,0},{28,4},{1,9},{5... | collective-permute-start | bytes 5308424 | tf_op jit(solution)/shard_map/ppermute | solution.py:648
  172.9 9.9 %collective-permute-start.17 = (bf16[2,32,2304]{2,1,0:T(8,128)(2,1)S(1)}, bf16[2,32,2304]{2,1,0:T(8,128)(2,1)S(1)}, u32[]{:S(2)}, u32[]{:S(2)}) collective-permute-start(bf16[2,32,2304]{2,1,0:T(8,128)(2,1)S(1)} %convolution_convert_fusion.1), channel_id=1, source_target_pairs={{0,2},{1,3},{2,0},{3,1},{4,6},{5,7},{6,4},{7,5},{8,10},{9,11},{10,... | collective-permute-start | bytes 884744 | tf_op jit(solution)/shard_map/send_rows/ppermute | solution.py:1006
  174.5 13.8 %collective-permute-start.18 = (bf16[2,32,2304]{2,1,0:T(8,128)(2,1)S(1)}, bf16[2,32,2304]{2,1,0:T(8,128)(2,1)S(1)}, u32[]{:S(2)}, u32[]{:S(2)}) collective-permute-start(bf16[2,32,2304]{2,1,0:T(8,128)(2,1)S(1)} %convolution_convert_fusion), channel_id=1, source_target_pairs={{0,3},{1,2},{2,1},{3,0},{4,7},{5,6},{6,5},{7,4},{8,11},{9,10},{10,... | collective-permute-start | bytes 884744 | tf_op jit(solution)/shard_map/send_rows/ppermute | solution.py:1006
  175.1 19.8 %collective-permute-start.20 = (bf16[2,32,2304]{2,1,0:T(8,128)(2,1)S(1)}, bf16[2,32,2304]{2,1,0:T(8,128)(2,1)S(1)}, u32[]{:S(2)}, u32[]{:S(2)}) collective-permute-start(bf16[2,32,2304]{2,1,0:T(8,128)(2,1)S(1)} %convolution_convert_fusion.2), channel_id=1, source_target_pairs={{0,5},{1,4},{2,7},{3,6},{4,1},{5,0},{6,3},{7,2},{8,13},{9,12},{10,... | collective-permute-start | bytes 884744 | tf_op jit(solution)/shard_map/send_rows/ppermute | solution.py:1006
  176.8 18.2 %collective-permute-start.19 = (bf16[2,32,2304]{2,1,0:T(8,128)(2,1)S(1)}, bf16[2,32,2304]{2,1,0:T(8,128)(2,1)S(1)}, u32[]{:S(2)}, u32[]{:S(2)}) collective-permute-start(bf16[2,32,2304]{2,1,0:T(8,128)(2,1)S(1)} %convolution_convert_fusion.3), channel_id=1, source_target_pairs={{0,4},{1,5},{2,6},{3,7},{4,0},{5,1},{6,2},{7,3},{8,12},{9,13},{10,... | collective-permute-start | bytes 884744 | tf_op jit(solution)/shard_map/send_rows/ppermute | solution.py:1006
  182.8 15.4 %collective-permute-start.21 = (bf16[2,32,2304]{2,1,0:T(8,128)(2,1)S(1)}, bf16[2,32,2304]{2,1,0:T(8,128)(2,1)S(1)}, u32[]{:S(2)}, u32[]{:S(2)}) collective-permute-start(bf16[2,32,2304]{2,1,0:T(8,128)(2,1)S(1)} %convolution_convert_fusion.1), channel_id=1, source_target_pairs={{0,6},{1,7},{2,4},{3,5},{4,2},{5,3},{6,0},{7,1},{8,14},{9,15},{10,... | collective-permute-start | bytes 884744 | tf_op jit(solution)/shard_map/send_rows/ppermute | solution.py:1006
  188.3 15.4 %collective-permute-start.22 = (bf16[2,32,2304]{2,1,0:T(8,128)(2,1)S(1)}, bf16[2,32,2304]{2,1,0:T(8,128)(2,1)S(1)}, u32[]{:S(2)}, u32[]{:S(2)}) collective-permute-start(bf16[2,32,2304]{2,1,0:T(8,128)(2,1)S(1)} %convolution_convert_fusion), channel_id=1, source_target_pairs={{0,7},{1,6},{2,5},{3,4},{4,3},{5,2},{6,1},{7,0},{8,15},{9,14},{10,... | collective-permute-start | bytes 884744 | tf_op jit(solution)/shard_map/send_rows/ppermute | solution.py:1006
  215.1 9.9 %collective-permute-start.25 = (bf16[2,32,2304]{2,1,0:T(8,128)(2,1)S(1)}, bf16[2,32,2304]{2,1,0:T(8,128)(2,1)S(1)}, u32[]{:S(2)}, u32[]{:S(2)}) collective-permute-start(bf16[2,32,2304]{2,1,0:T(8,128)(2,1)S(1)} %bitcast.199), channel_id=1, source_target_pairs={{0,2},{1,3},{2,0},{3,1},{4,6},{5,7},{6,4},{7,5},{8,10},{9,11},{10,... | collective-permute-start | bytes 884744 | tf_op jit(solution)/shard_map/send_results/ppermute | solution.py:1006
  216.4 14.0 %collective-permute-start.26 = (bf16[2,32,2304]{2,1,0:T(8,128)(2,1)S(1)}, bf16[2,32,2304]{2,1,0:T(8,128)(2,1)S(1)}, u32[]{:S(2)}, u32[]{:S(2)}) collective-permute-start(bf16[2,32,2304]{2,1,0:T(8,128)(2,1)S(1)} %bitcast.198), channel_id=1, source_target_pairs={{0,3},{1,2},{2,1},{3,0},{4,7},{5,6},{6,5},{7,4},{8,11},{9,10},{10,... | collective-permute-start | bytes 884744 | tf_op jit(solution)/shard_map/send_results/ppermute | solution.py:1006
  216.9 26.6 %collective-permute-start.27 = (bf16[2,32,2304]{2,1,0:T(8,128)(2,1)S(1)}, bf16[2,32,2304]{2,1,0:T(8,128)(2,1)S(1)}, u32[]{:S(2)}, u32[]{:S(2)}) collective-permute-start(bf16[2,32,2304]{2,1,0:T(8,128)(2,1)S(1)} %bitcast.197), channel_id=1, source_target_pairs={{0,4},{1,5},{2,6},{3,7},{4,0},{5,1},{6,2},{7,3},{8,12},{9,13},{10,... | collective-permute-start | bytes 884744 | tf_op jit(solution)/shard_map/send_results/ppermute | solution.py:1006
  218.4 25.2 %collective-permute-start.28 = (bf16[2,32,2304]{2,1,0:T(8,128)(2,1)S(1)}, bf16[2,32,2304]{2,1,0:T(8,128)(2,1)S(1)}, u32[]{:S(2)}, u32[]{:S(2)}) collective-permute-start(bf16[2,32,2304]{2,1,0:T(8,128)(2,1)S(1)} %bitcast.196), channel_id=1, source_target_pairs={{0,5},{1,4},{2,7},{3,6},{4,1},{5,0},{6,3},{7,2},{8,13},{9,12},{10,... | collective-permute-start | bytes 884744 | tf_op jit(solution)/shard_map/send_results/ppermute | solution.py:1006
  218.6 24.9 %collective-permute-start.29 = (bf16[2,32,2304]{2,1,0:T(8,128)(2,1)S(1)}, bf16[2,32,2304]{2,1,0:T(8,128)(2,1)S(1)}, u32[]{:S(2)}, u32[]{:S(2)}) collective-permute-start(bf16[2,32,2304]{2,1,0:T(8,128)(2,1)S(1)} %bitcast.195), channel_id=1, source_target_pairs={{0,6},{1,7},{2,4},{3,5},{4,2},{5,3},{6,0},{7,1},{8,14},{9,15},{10,... | collective-permute-start | bytes 884744 | tf_op jit(solution)/shard_map/send_results/ppermute | solution.py:1006
  224.9 20.3 %collective-permute-start.30 = (bf16[2,32,2304]{2,1,0:T(8,128)(2,1)S(1)}, bf16[2,32,2304]{2,1,0:T(8,128)(2,1)S(1)}, u32[]{:S(2)}, u32[]{:S(2)}) collective-permute-start(bf16[2,32,2304]{2,1,0:T(8,128)(2,1)S(1)} %bitcast.194), channel_id=1, source_target_pairs={{0,7},{1,6},{2,5},{3,4},{4,3},{5,2},{6,1},{7,0},{8,15},{9,14},{10,... | collective-permute-start | bytes 884744 | tf_op jit(solution)/shard_map/send_results/ppermute | solution.py:1006
  261.4 153.3 %reduce-scatter.5.cloned.1.call-start = ((), (), s32[]{:S(2)}) async-start(), calls=%async_computation.5 | async-start | bytes 7299072 | tf_op jit(solution)/shard_map/reduce_inner/reduce_scatter | solution.py:683
  261.4 43.1 %collective-permute-start.31 = (bf16[768,1152]{1,0:T(8,128)(2,1)}, bf16[768,1152]{1,0:T(8,128)(2,1)}, u32[]{:S(2)}, u32[]{:S(2)}) collective-permute-start(bf16[768,1152]{1,0:T(8,128)(2,1)} %pad_maximum_fusion.2), channel_id=1, source_target_pairs={{0,8},{4,12},{8,16},{12,20},{16,24},{20,28},{24,0},{28,4},{1,9},{5... | collective-permute-start | bytes 5308424 | tf_op jit(solution)/shard_map/ppermute | solution.py:648
  307.8 42.2 %collective-permute-start.32 = (bf16[768,1152]{1,0:T(8,128)(2,1)}, bf16[768,1152]{1,0:T(8,128)(2,1)}, u32[]{:S(2)}, u32[]{:S(2)}) collective-permute-start(bf16[768,1152]{1,0:T(8,128)(2,1)} %add_convert_fusion.1), channel_id=1, source_target_pairs={{0,8},{4,12},{8,16},{12,20},{16,24},{20,28},{24,0},{28,4},{1,9},{5... | collective-permute-start | bytes 5308424 | tf_op jit(solution)/shard_map/ppermute | solution.py:648
  351.5 8.4 %collective-permute-start.33 = (bf16[2,1,72,1152]{3,2,1,0:T(8,128)(2,1)S(1)}, bf16[2,1,72,1152]{3,2,1,0:T(8,128)(2,1)S(1)}, u32[]{:S(2)}, u32[]{:S(2)}) collective-permute-start(bf16[2,1,72,1152]{3,2,1,0:T(8,128)(2,1)S(1)} %get-tuple-element.392), channel_id=1, source_target_pairs={{0,4},{4,0},{8,12},{12,8},{16,20},{20,16},{24,28},{28,24},{1,5},{5... | collective-permute-start | bytes 995336 | tf_op jit(solution)/shard_map/ppermute | solution.py:648
  360.2 7.2 %collective-permute-start.36 = (bf16[72,1152]{1,0:T(8,128)(2,1)S(1)}, bf16[72,1152]{1,0:T(8,128)(2,1)S(1)}, u32[]{:S(2)}, u32[]{:S(2)}) collective-permute-start(bf16[72,1152]{1,0:T(8,128)(2,1)S(1)} %get-tuple-element.388), channel_id=1, source_target_pairs={{0,24},{4,28},{8,0},{12,4},{16,8},{20,12},{24,16},{28,20},{1,25},{... | collective-permute-start | bytes 497672 | tf_op jit(solution)/shard_map/ppermute | solution.py:648
  360.3 13.8 %collective-permute-start.35 = (bf16[72,1152]{1,0:T(8,128)(2,1)S(1)}, bf16[72,1152]{1,0:T(8,128)(2,1)S(1)}, u32[]{:S(2)}, u32[]{:S(2)}) collective-permute-start(bf16[72,1152]{1,0:T(8,128)(2,1)S(1)} %get-tuple-element.389), channel_id=1, source_target_pairs={{0,16},{4,20},{8,24},{12,28},{16,0},{20,4},{24,8},{28,12},{1,17},{... | collective-permute-start | bytes 497672 | tf_op jit(solution)/shard_map/ppermute | solution.py:648
  360.6 13.5 %collective-permute-start.34 = (bf16[72,1152]{1,0:T(8,128)(2,1)S(1)}, bf16[72,1152]{1,0:T(8,128)(2,1)S(1)}, u32[]{:S(2)}, u32[]{:S(2)}) collective-permute-start(bf16[72,1152]{1,0:T(8,128)(2,1)S(1)} %get-tuple-element.390), channel_id=1, source_target_pairs={{0,8},{4,12},{8,16},{12,20},{16,24},{20,28},{24,0},{28,4},{1,9},{5... | collective-permute-start | bytes 497672 | tf_op jit(solution)/shard_map/ppermute | solution.py:648
  374.2 40.5 %collective-permute-start.37 = (bf16[768,1152]{1,0:T(8,128)(2,1)}, bf16[768,1152]{1,0:T(8,128)(2,1)}, u32[]{:S(2)}, u32[]{:S(2)}) collective-permute-start(bf16[768,1152]{1,0:T(8,128)(2,1)} %add_convert_fusion), channel_id=1, source_target_pairs={{0,8},{4,12},{8,16},{12,20},{16,24},{20,28},{24,0},{28,4},{1,9},{5... | collective-permute-start | bytes 5308424 | tf_op jit(solution)/shard_map/ppermute | solution.py:648
  381.8 40.3 %collective-permute-start.43 = (f32[6,1152]{1,0:T(8,128)S(1)}, f32[6,1152]{1,0:T(8,128)S(1)}, u32[]{:S(2)}, u32[]{:S(2)}) collective-permute-start(f32[6,1152]{1,0:T(8,128)S(1)} %add.394), channel_id=1, source_target_pairs={{0,4},{4,0},{8,12},{12,8},{16,20},{20,16},{24,28},{28,24},{1,5},{5... | collective-permute-start | bytes 82952 | tf_op jit(solution)/shard_map/ppermute | solution.py:633
  416.0 10.7 %collective-permute-start.40 = (bf16[2,72,1152]{2,1,0:T(8,128)(2,1)S(1)}, bf16[2,72,1152]{2,1,0:T(8,128)(2,1)S(1)}, u32[]{:S(2)}, u32[]{:S(2)}) collective-permute-start(bf16[2,72,1152]{2,1,0:T(8,128)(2,1)S(1)} %get-tuple-element.382), channel_id=1, source_target_pairs={{0,24},{4,28},{8,0},{12,4},{16,8},{20,12},{24,16},{28,20},{1,25},{... | collective-permute-start | bytes 995336 | tf_op jit(solution)/shard_map/ppermute | solution.py:648
  418.4 28.7 %collective-permute-start.39 = (bf16[2,72,1152]{2,1,0:T(8,128)(2,1)S(1)}, bf16[2,72,1152]{2,1,0:T(8,128)(2,1)S(1)}, u32[]{:S(2)}, u32[]{:S(2)}) collective-permute-start(bf16[2,72,1152]{2,1,0:T(8,128)(2,1)S(1)} %get-tuple-element.383), channel_id=1, source_target_pairs={{0,16},{4,20},{8,24},{12,28},{16,0},{20,4},{24,8},{28,12},{1,17},{... | collective-permute-start | bytes 995336 | tf_op jit(solution)/shard_map/ppermute | solution.py:648
  418.7 28.4 %collective-permute-start.38 = (bf16[2,72,1152]{2,1,0:T(8,128)(2,1)S(1)}, bf16[2,72,1152]{2,1,0:T(8,128)(2,1)S(1)}, u32[]{:S(2)}, u32[]{:S(2)}) collective-permute-start(bf16[2,72,1152]{2,1,0:T(8,128)(2,1)S(1)} %get-tuple-element.384), channel_id=1, source_target_pairs={{0,8},{4,12},{8,16},{12,20},{16,24},{20,28},{24,0},{28,4},{1,9},{5... | collective-permute-start | bytes 995336 | tf_op jit(solution)/shard_map/ppermute | solution.py:648
  422.1 34.3 %collective-permute-start.45 = (bf16[1,1,72,1152]{3,2,1,0:T(8,128)(2,1)S(1)}, bf16[1,1,72,1152]{3,2,1,0:T(8,128)(2,1)S(1)}, u32[]{:S(2)}, u32[]{:S(2)}) collective-permute-start(bf16[1,1,72,1152]{3,2,1,0:T(8,128)(2,1)S(1)} %bitcast.239), channel_id=1, source_target_pairs={{0,2},{1,3},{2,0},{3,1},{4,6},{5,7},{6,4},{7,5},{8,10},{9,11},{10,... | collective-permute-start | bytes 497672 | tf_op jit(solution)/shard_map/ppermute | solution.py:648
  423.1 28.8 %collective-permute-start.50 = (bf16[2,1,72,208]{3,2,1,0:T(8,128)(2,1)S(1)}, bf16[2,1,72,208]{3,2,1,0:T(8,128)(2,1)S(1)}, u32[]{:S(2)}, u32[]{:S(2)}) collective-permute-start(bf16[2,1,72,208]{3,2,1,0:T(8,128)(2,1)S(1)} %get-tuple-element.403), channel_id=1, source_target_pairs={{0,4},{4,0},{8,12},{12,8},{16,20},{20,16},{24,28},{28,24},{1,5},{5... | collective-permute-start | bytes 179720 | tf_op jit(solution)/shard_map/ppermute | solution.py:648
  447.3 9.7 %collective-permute-start.44 = (bf16[1,2,72,1152]{3,2,1,0:T(8,128)(2,1)S(1)}, bf16[1,2,72,1152]{3,2,1,0:T(8,128)(2,1)S(1)}, u32[]{:S(2)}, u32[]{:S(2)}) collective-permute-start(bf16[1,2,72,1152]{3,2,1,0:T(8,128)(2,1)S(1)} %fusion.66), channel_id=1, source_target_pairs={{0,2},{1,3},{2,0},{3,1},{4,6},{5,7},{6,4},{7,5},{8,10},{9,11},{10,... | collective-permute-start | bytes 995336 | tf_op jit(solution)/shard_map/ppermute | solution.py:648
  453.0 7.5 %collective-permute-start.53 = (bf16[72,208]{0,1:T(8,128)(2,1)S(1)}, bf16[72,208]{0,1:T(8,128)(2,1)S(1)}, u32[]{:S(2)}, u32[]{:S(2)}) collective-permute-start(bf16[72,208]{0,1:T(8,128)(2,1)S(1)} %get-tuple-element.399), channel_id=1, source_target_pairs={{0,24},{4,28},{8,0},{12,4},{16,8},{20,12},{24,16},{28,20},{1,25},{... | collective-permute-start | bytes 89864 | tf_op jit(solution)/shard_map/ppermute | solution.py:648
  456.4 8.6 %collective-permute-start.52 = (bf16[72,208]{0,1:T(8,128)(2,1)S(1)}, bf16[72,208]{0,1:T(8,128)(2,1)S(1)}, u32[]{:S(2)}, u32[]{:S(2)}) collective-permute-start(bf16[72,208]{0,1:T(8,128)(2,1)S(1)} %get-tuple-element.400), channel_id=1, source_target_pairs={{0,16},{4,20},{8,24},{12,28},{16,0},{20,4},{24,8},{28,12},{1,17},{... | collective-permute-start | bytes 89864 | tf_op jit(solution)/shard_map/ppermute | solution.py:648
  456.4 8.6 %collective-permute-start.51 = (bf16[72,208]{0,1:T(8,128)(2,1)S(1)}, bf16[72,208]{0,1:T(8,128)(2,1)S(1)}, u32[]{:S(2)}, u32[]{:S(2)}) collective-permute-start(bf16[72,208]{0,1:T(8,128)(2,1)S(1)} %get-tuple-element.401), channel_id=1, source_target_pairs={{0,8},{4,12},{8,16},{12,20},{16,24},{20,28},{24,0},{28,4},{1,9},{5... | collective-permute-start | bytes 89864 | tf_op jit(solution)/shard_map/ppermute | solution.py:648
  457.1 8.0 %collective-permute-start.49 = (f32[6,1152]{1,0:T(8,128)S(1)}, f32[6,1152]{1,0:T(8,128)S(1)}, u32[]{:S(2)}, u32[]{:S(2)}) collective-permute-start(f32[6,1152]{1,0:T(8,128)S(1)} %add.401), channel_id=1, source_target_pairs={{0,16},{4,20},{8,24},{12,28},{16,0},{20,4},{24,8},{28,12},{1,17},{... | collective-permute-start | bytes 82952 | tf_op jit(solution)/shard_map/ppermute | solution.py:633
  (84 other events, 1082.4 us)
Sparse Core Ops, SparseCore 0:
  46.0 70.2 all-gather.2
  124.3 40.8 all-gather.4
  261.5 80.6 reduce-scatter.2
  350.2 60.8 reduce-scatter.4
